TPU v7x, 512 devices: a whole 4x8x8 slice. The times are simulated.
512 devices in a mesh: freq: 8 (over z), sx: 16 (over y, core), sy: 4 (over x).
Axes of the slice: x: 4, y: 8, z: 8, core: 2. Of those that a mesh axis runs over, the one named last changes fastest.
Arguments:
- stiffness: bfloat16 [16, 4, 3072, 3072], P('sx', 'sy', None, 'freq')
- mass_matrix: bfloat16 [16, 4, 3072, 3072], P('sx', 'sy', None, 'freq')
- omega_table: float32 [32], replicated, may hold values from 0.5 to 6
- assignment: int32 [32], P('freq'), may hold values from 0 to 31, each once
- adjoint_load: float32 [16, 4, 32, 2, 4, 768], P('sx', 'sy', 'freq'), as said below
- forward_state: bfloat16 [16, 4, 32, 2, 4, 768], P('sx', 'sy', 'freq'), may hold values from -6 to 6
- owner_index: int32 [16, 4, 4, 768], P('sx', 'sy'), may hold values from 0 to 1727
Outputs:
- adjoint: float32 [16, 4, 32, 2, 4, 768], P('sx', 'sy', 'freq')
- gradient: float32 [16, 4, 1728], P('sx', 'sy', 'freq')
- residual_level: float32 [32], P('freq')
Inputs may be any that keep to these rules, and one draw needn't show every extreme that they name: `adjoint_load`: the two copies of a face shared by neighbouring substructures are equal.
All inputs are finite; a program needn't handle non-finite values.
Results may differ from a plain program's by a relative error of at most 0.012.
Values may be sent and summed in bfloat16 or wider, within the bound.
No kernel may reach another device: no remote copies, remote signals or barrier semaphores. Data moves between devices by JAX's collectives and lax.ppermute only.
A program may use at most 64 MiB of HBM per device.

v0:
```python
import jax
import jax.numpy as jnp
from jax import lax
from jax.sharding import PartitionSpec as P

ITERS = 4
DE_SUB = 1728


LOSS_FACTOR = 0.3


def padded(cells, sides, width):
    for axis, dim in sides:
        count = lax.axis_size(axis)
        ends = count - 1
        head = lax.slice_in_dim(cells, 0, width, axis=dim)
        tail = lax.slice_in_dim(cells, cells.shape[dim] - width, cells.shape[dim], axis=dim)
        cells = jnp.concatenate(
            [
                lax.ppermute(tail, axis, [(i, (i + 1) % count) for i in range(ends)]),
                cells,
                lax.ppermute(head, axis, [((i + 1) % count, i) for i in range(ends)]),
            ],
            axis=dim,
        )
    return cells


def face_weights():
    index_x = lax.axis_index("sx")
    size_x = lax.axis_size("sx")
    index_y = lax.axis_index("sy")
    size_y = lax.axis_size("sy")
    west_weight = jnp.where(index_x > 0, 0.5, 1.0)
    east_weight = jnp.where(index_x < size_x - 1, 0.5, 1.0)
    south_weight = jnp.where(index_y > 0, 0.5, 1.0)
    north_weight = jnp.where(index_y < size_y - 1, 0.5, 1.0)
    return jnp.stack([west_weight, east_weight, south_weight, north_weight]).astype(jnp.float32)


def assemble(local_vals):
    padded_x = padded(local_vals[:, :, 0:2].astype(jnp.bfloat16), (("sx", 2),), 1).astype(
        jnp.float32
    )
    padded_y = padded(local_vals[:, :, 2:4].astype(jnp.bfloat16), (("sy", 2),), 1).astype(
        jnp.float32
    )
    west_face = padded_x[:, :, 1] + padded_x[:, :, 0]
    east_face = padded_x[:, :, 2] + padded_x[:, :, 3]
    south_face = padded_y[:, :, 1] + padded_y[:, :, 0]
    north_face = padded_y[:, :, 2] + padded_y[:, :, 3]
    return jnp.stack([west_face, east_face, south_face, north_face], axis=2)


def mix_parts(stiff_part, mass_part, omega_sq, sign_factor):
    factor = omega_sq[:, None, None]
    real_part = (
        stiff_part[:, 0] - sign_factor * LOSS_FACTOR * stiff_part[:, 1] - factor * mass_part[:, 0]
    )
    imag_part = (
        stiff_part[:, 1] + sign_factor * LOSS_FACTOR * stiff_part[:, 0] - factor * mass_part[:, 1]
    )
    return jnp.stack([real_part, imag_part], axis=1)


def apply_rows(vector, stiff_cols, mass_cols, omega_every, sign_factor):
    face_count = vector.shape[2]
    matrix_order = face_count * vector.shape[3]
    rounded = vector.astype(jnp.bfloat16)
    pieces = lax.all_gather(rounded, "freq", axis=0, tiled=True)
    count = pieces.shape[0]
    flattened = pieces.reshape(-1, matrix_order)
    stiff_part = jnp.dot(flattened, stiff_cols, preferred_element_type=jnp.float32)
    mass_part = jnp.dot(flattened, mass_cols, preferred_element_type=jnp.float32)
    local_vals = mix_parts(
        stiff_part.reshape(count, 2, face_count, -1),
        mass_part.reshape(count, 2, face_count, -1),
        omega_every,
        sign_factor,
    )
    returned = lax.all_to_all(
        local_vals.astype(jnp.bfloat16), "freq", split_axis=0, concat_axis=3, tiled=True
    ).astype(local_vals.dtype)
    return assemble(returned)


def reduce_dots(factor_pairs, weights):
    partial_value = tuple(
        (
            jnp.sum(first_vec * second_vec * weights[None, None, :, None], axis=(1, 2, 3))
            for first_vec, second_vec in factor_pairs
        )
    )
    summed = lax.psum(partial_value, ("sx", "sy"))
    return summed


def per_freq(values):
    return values[:, None, None, None]


def face_columns(matrix, matrix_order, face_count):
    grouped = matrix.reshape(matrix_order, -1, face_count)
    return jnp.swapaxes(grouped, 1, 2).reshape(matrix_order, -1)


def body(stiffness, mass_matrix, omega_table, assignment, adjoint_load, forward_state, owner_index):
    n_freq = lax.axis_size("freq")
    slot_count = adjoint_load.shape[2]
    face_count = adjoint_load.shape[4]
    face_len = adjoint_load.shape[5]
    matrix_order = face_count * face_len
    stiff_cols = face_columns(stiffness[0, 0], matrix_order, face_count)
    mass_cols = face_columns(mass_matrix[0, 0], matrix_order, face_count)
    matches = assignment[:, None] == jnp.arange(omega_table.shape[0], dtype=jnp.int32)[None, :]
    slot_omega = jnp.sum(jnp.where(matches, omega_table[None, :], 0.0), axis=1)
    weights = face_weights()
    load_rows = adjoint_load[0, 0]
    omega_every = lax.all_gather(slot_omega, "freq", axis=0, tiled=True)

    def operate(vector, sign_factor):
        return apply_rows(vector, stiff_cols, mass_cols, omega_every, sign_factor)

    residual = load_rows
    solution = jnp.zeros_like(load_rows)
    normal_res = operate(residual, -1.0)
    direction = normal_res
    gamma_now = reduce_dots(((normal_res, normal_res),), weights)[0]
    for iteration in range(ITERS):
        image_vec = operate(direction, 1.0)
        delta_now = reduce_dots(((image_vec, image_vec),), weights)[0]
        step_size = gamma_now / delta_now
        solution = solution + per_freq(step_size) * direction
        if iteration + 1 < ITERS:
            residual = residual - per_freq(step_size) * image_vec
            normal_res = operate(residual, -1.0)
            gamma_next = reduce_dots(((normal_res, normal_res),), weights)[0]
            direction = normal_res + per_freq(gamma_next / gamma_now) * direction
            gamma_now = gamma_next
    cell_count = float(lax.axis_size("sx") * lax.axis_size("sy") * 2 * matrix_order)
    residual_level = jnp.log(gamma_now / cell_count)
    state_vec = forward_state[0, 0].astype(jnp.float32)
    lambda_real = solution[:, 0]
    lambda_imag = solution[:, 1]
    state_real = state_vec[:, 0]
    state_imag = state_vec[:, 1]
    product_term = (
        lambda_real * state_real
        - lambda_imag * state_imag
        - LOSS_FACTOR * (lambda_real * state_imag + lambda_imag * state_real)
    )
    dof_total = jnp.sum(product_term, axis=0)
    partial_grad = jax.ops.segment_sum(
        dof_total.reshape(-1), owner_index[0, 0].reshape(-1), num_segments=DE_SUB
    )
    grad_factor = (DE_SUB / (slot_count * n_freq * matrix_order)) ** 0.5
    gradient = lax.psum_scatter(
        -grad_factor * partial_grad, "freq", scatter_dimension=0, tiled=True
    )
    return (solution[None, None], gradient[None, None], residual_level)


def solution(mesh):
    return jax.shard_map(
        body,
        mesh=mesh,
        in_specs=(
            P("sx", "sy", None, "freq"),
            P("sx", "sy", None, "freq"),
            P(),
            P("freq"),
            P("sx", "sy", "freq", None, None, None),
            P("sx", "sy", "freq", None, None, None),
            P("sx", "sy", None, None),
        ),
        out_specs=(P("sx", "sy", "freq", None, None, None), P("sx", "sy", "freq"), P("freq")),
        check_vma=False,
    )
```

profile of v0, /device:TPU:32, one launch (start us, length us, event | category | flops | bytes accessed | tf_op | source)
XLA Modules:
  0.0 1387.7 jit_solution(9510212069884050593)
XLA Ops:
  5.9 31.4 %all_gather.27 = bf16[32,2,4,768]{3,2,1,0:T(4,128)(2,1)S(1)} all-gather(bf16[4,2,4,768]{3,2,1,0:T(4,128)(2,1)S(1)} %bitcast_convert_fusion), channel_id=1, replica_groups=mesh['freq'=8,'sx'=16,'sy'=4] {'freq'}, dimensions={0}, use_global_device_ids=true | all-gather | bytes 442368 | tf_op jit(solution)/shard_map/all_gather | solution.py:71
  48.3 17.0 %all-reduce = f32[32]{0:T(128)S(1)} all-reduce(f32[32]{0:T(128)S(1)} %dynamic-update-slice), channel_id=1, replica_groups=mesh['freq'=8,'sx'=16,'sy'=4] {'freq'}, use_global_device_ids=true, to_apply=%add | all-reduce | flops 32 | bytes 256
  69.5 8.3 all-to-all-done
  83.7 4.5 collective-permute-start.2
  90.1 25.1 %all_gather.29 = bf16[32,2,4,768]{3,2,1,0:T(4,128)(2,1)S(1)} all-gather(bf16[4,2,4,768]{3,2,1,0:T(4,128)(2,1)S(1)} %fusion.103), channel_id=1, replica_groups=mesh['freq'=8,'sx'=16,'sy'=4] {'freq'}, dimensions={0}, use_global_device_ids=true | all-gather | bytes 442368 | tf_op jit(solution)/shard_map/all_gather | solution.py:71
  122.3 8.2 all-to-all-done.1
  132.1 5.0 collective-permute-start.6
  145.9 126.0 %all-reduce.2 = (f32[4]{0:T(128)S(1)}, f32[4]{0:T(128)S(1)}) all-reduce(f32[4]{0:T(128)S(1)} %get-tuple-element.4, f32[4]{0:T(128)S(1)} %get-tuple-element.3), channel_id=1, replica_groups=mesh['freq'=8,'sx'=16,'sy'=4] {'sx','sy'}, use_global_device_ids=true, to_apply=%region_2.3 | all-reduce | flops 8 | bytes 64 | tf_op jit(solution)/shard_map/psum | solution.py:95
  272.1 25.5 %all_gather.30 = bf16[32,2,4,768]{3,2,1,0:T(4,128)(2,1)S(1)} all-gather(bf16[4,2,4,768]{3,2,1,0:T(4,128)(2,1)S(1)} %get-tuple-element.13), channel_id=1, replica_groups=mesh['freq'=8,'sx'=16,'sy'=4] {'freq'}, dimensions={0}, use_global_device_ids=true | all-gather | bytes 442368 | tf_op jit(solution)/shard_map/all_gather | solution.py:71
  300.6 10.8 all_to_all.32
  312.9 4.5 collective-permute-start.10
  326.2 124.5 %psum.58 = f32[4]{0:T(128)S(1)} all-reduce(f32[4]{0:T(128)S(1)} %multiply_reduce_fusion.4), channel_id=1, replica_groups=mesh['freq'=8,'sx'=16,'sy'=4] {'sx','sy'}, use_global_device_ids=true, to_apply=%region_6.7 | all-reduce | flops 4 | bytes 32 | tf_op jit(solution)/shard_map/psum | solution.py:95
  450.9 25.0 %all_gather.31 = bf16[32,2,4,768]{3,2,1,0:T(4,128)(2,1)S(1)} all-gather(bf16[4,2,4,768]{3,2,1,0:T(4,128)(2,1)S(1)} %get-tuple-element.11), channel_id=1, replica_groups=mesh['freq'=8,'sx'=16,'sy'=4] {'freq'}, dimensions={0}, use_global_device_ids=true | all-gather | bytes 442368 | tf_op jit(solution)/shard_map/all_gather | solution.py:71
  479.0 11.0 all_to_all.33
  491.6 5.1 collective-permute-start.14
  505.4 126.1 %psum.59 = f32[4]{0:T(128)S(1)} all-reduce(f32[4]{0:T(128)S(1)} %multiply_reduce_fusion.3), channel_id=1, replica_groups=mesh['freq'=8,'sx'=16,'sy'=4] {'sx','sy'}, use_global_device_ids=true, to_apply=%region_8.9 | all-reduce | flops 4 | bytes 32 | tf_op jit(solution)/shard_map/psum | solution.py:95
  632.2 25.5 %all_gather.32 = bf16[32,2,4,768]{3,2,1,0:T(4,128)(2,1)S(1)} all-gather(bf16[4,2,4,768]{3,2,1,0:T(4,128)(2,1)S(1)} %get-tuple-element.9), channel_id=1, replica_groups=mesh['freq'=8,'sx'=16,'sy'=4] {'freq'}, dimensions={0}, use_global_device_ids=true | all-gather | bytes 442368 | tf_op jit(solution)/shard_map/all_gather | solution.py:71
  660.7 10.8 all_to_all.34
  686.3 124.3 %psum.60 = f32[4]{0:T(128)S(1)} all-reduce(f32[4]{0:T(128)S(1)} %multiply_reduce_fusion.2), channel_id=1, replica_groups=mesh['freq'=8,'sx'=16,'sy'=4] {'sx','sy'}, use_global_device_ids=true, to_apply=%region_10.11 | all-reduce | flops 4 | bytes 32 | tf_op jit(solution)/shard_map/psum | solution.py:95
  811.1 25.0 %all_gather.33 = bf16[32,2,4,768]{3,2,1,0:T(4,128)(2,1)S(1)} all-gather(bf16[4,2,4,768]{3,2,1,0:T(4,128)(2,1)S(1)} %get-tuple-element.7), channel_id=1, replica_groups=mesh['freq'=8,'sx'=16,'sy'=4] {'freq'}, dimensions={0}, use_global_device_ids=true | all-gather | bytes 442368 | tf_op jit(solution)/shard_map/all_gather | solution.py:71
  839.2 11.0 all_to_all.35
  851.8 4.8 collective-permute-start.22
  865.3 126.1 %psum.61 = f32[4]{0:T(128)S(1)} all-reduce(f32[4]{0:T(128)S(1)} %multiply_reduce_fusion.1), channel_id=1, replica_groups=mesh['freq'=8,'sx'=16,'sy'=4] {'sx','sy'}, use_global_device_ids=true, to_apply=%region_12.13 | all-reduce | flops 4 | bytes 32 | tf_op jit(solution)/shard_map/psum | solution.py:95
  992.0 25.7 %all_gather.34 = bf16[32,2,4,768]{3,2,1,0:T(4,128)(2,1)S(1)} all-gather(bf16[4,2,4,768]{3,2,1,0:T(4,128)(2,1)S(1)} %subtract_convert_fusion), channel_id=1, replica_groups=mesh['freq'=8,'sx'=16,'sy'=4] {'freq'}, dimensions={0}, use_global_device_ids=true | all-gather | bytes 442368 | tf_op jit(solution)/shard_map/all_gather | solution.py:71
  1020.7 10.8 all_to_all.36
  1046.3 124.3 %psum.62 = f32[4]{0:T(128)S(1)} all-reduce(f32[4]{0:T(128)S(1)} %multiply_reduce_fusion), channel_id=1, replica_groups=mesh['freq'=8,'sx'=16,'sy'=4] {'sx','sy'}, use_global_device_ids=true, to_apply=%region_14.15 | all-reduce | flops 4 | bytes 32 | tf_op jit(solution)/shard_map/psum | solution.py:95
  1171.2 25.0 %all_gather.35 = bf16[32,2,4,768]{3,2,1,0:T(4,128)(2,1)S(1)} all-gather(bf16[4,2,4,768]{3,2,1,0:T(4,128)(2,1)S(1)} %fusion.68), channel_id=1, replica_groups=mesh['freq'=8,'sx'=16,'sy'=4] {'freq'}, dimensions={0}, use_global_device_ids=true | all-gather | bytes 442368 | tf_op jit(solution)/shard_map/all_gather | solution.py:71
  1203.5 8.2 all-to-all-done.7
  1213.2 4.7 collective-permute-start.30
  1227.3 126.1 %psum.63 = f32[4]{0:T(128)S(1)} all-reduce(f32[4]{0:T(128)S(1)} %fusion.65), channel_id=1, replica_groups=mesh['freq'=8,'sx'=16,'sy'=4] {'sx','sy'}, use_global_device_ids=true, to_apply=%region_16.17 | all-reduce | flops 4 | bytes 32 | tf_op jit(solution)/shard_map/psum | solution.py:95
  1354.2 16.8 %scatter_custom_fusion = f32[1728]{0:T(1024)S(1)} fusion(s32[3072]{0:T(1024)S(1)} %reshape.442, f32[3072]{0:T(1024)S(1)} %reshape.444, f32[]{:T(128)} %constant.14.clone.1), kind=kCustom, calls=%fused_computation.212 | custom fusion | flops 3072 | bytes 6916 | tf_op jit(solution)/shard_map/scatter-add | solution.py:154
  1371.0 15.0 %all-reduce.1 = f32[1728]{0:T(1024)S(1)} all-reduce(f32[1728]{0:T(1024)S(1)} %broadcast_multiply_fusion), channel_id=2, replica_groups=mesh['freq'=8,'sx'=16,'sy'=4] {'freq'}, use_global_device_ids=true, to_apply=%region_19.20.clone | all-reduce | flops 1728 | bytes 13824
  (303 shorter events, 142.2 us)
Async XLA Ops:
  66.1 11.7 all-to-all-start
  78.0 10.2 collective-permute-start.1
  80.0 8.3 collective-permute-start
  82.4 5.9 collective-permute-start.3
  83.7 6.1 collective-permute-start.2
  118.9 11.7 all-to-all-start.1
  130.8 10.7 collective-permute-start.7
  132.1 9.4 collective-permute-start.6
  139.0 6.4 collective-permute-start.4
  311.6 10.2 collective-permute-start.11
  312.9 9.0 collective-permute-start.10
  317.5 4.5 collective-permute-start.9
  319.4 6.4 collective-permute-start.8
  490.3 10.8 collective-permute-start.15
  491.6 9.5 collective-permute-start.14
  496.7 4.5 collective-permute-start.13
  498.6 6.4 collective-permute-start.12
  671.7 10.2 collective-permute-start.19
  673.0 9.0 collective-permute-start.18
  677.6 4.5 collective-permute-start.17
  679.6 6.4 collective-permute-start.16
  850.5 10.5 collective-permute-start.23
  851.8 9.2 collective-permute-start.22
  856.6 4.5 collective-permute-start.21
  858.6 6.4 collective-permute-start.20
  1031.7 10.2 collective-permute-start.27
  1033.0 9.0 collective-permute-start.26
  1039.6 6.4 collective-permute-start.24
  1200.0 11.7 all-to-all-start.7
  1211.9 10.4 collective-permute-start.31
  1213.2 9.1 collective-permute-start.30
  1219.9 6.4 collective-permute-start.28
  (49 other events, 3992.8 us)
where the time goes:
time: 1390 us
  blocking collectives  1170 us (84%)
  starting transfers between devices  92.8 us (7%)
  waiting for transfers between devices  52.5 us (4%)
  other arithmetic  25.2 us (2%)
  local copies, waits for them, and re-layouts  23 us (2%)
  matrix products  18.9 us (1%)
    psum x7, blocking collectives, reduce_dots(): summed = lax.psum(partial_value, ('sx', 'sy'))  877 us
    all_gather x8, blocking collectives, apply_rows(): pieces = lax.all_gather(rounded, 'freq', axis=0, tiled=True)  208 us
    ppermute x16, starting transfers between devices, padded(): lax.ppermute(tail, axis, [(i, (i + 1) % count) for i in range(ends)])  57 us
    all_to_all x5, blocking collectives, apply_rows(): lax.all_to_all(local_vals.astype(jnp.bfloat16), 'freq', split_axis=0, con...  54.3 us
    unnamed x2, blocking collectives  32 us
  transfers between devices with their start and end apart: 35, of which 11 were waited for; matrix products, arithmetic and copies ran while one was open for 0% of the time, Pallas kernels for 0%

commit v1 on v0

v1 whole, which is shorter than its diff:
```python
import functools

import jax
import jax.numpy as jnp
from jax import lax
from jax.experimental import pallas as pl
from jax.experimental.pallas import tpu as pltpu
from jax.sharding import PartitionSpec as P

DE_SUB = 1728
LOSS_FACTOR = 0.3
LOW = 64
BF = jnp.bfloat16
F32 = jnp.float32


def params():
    return pltpu.CompilerParams(vmem_limit_bytes=24 * 1024 * 1024)


def arrange_kernel(stiff_ref, mass_ref, out_ref, order_ref):
    faces, _, run, width = stiff_ref.shape

    @pl.when(pl.program_id(0) == 0)
    def _():
        source = lax.broadcasted_iota(jnp.int32, (width, width), 0)
        target = lax.broadcasted_iota(jnp.int32, (width, width), 1)
        wanted = faces * lax.rem(target, run) + lax.div(target, run)
        order_ref[...] = jnp.where(source == wanted, 1.0, 0.0).astype(BF)

    for at, ref in enumerate((stiff_ref, mass_ref)):
        rows = ref[...].reshape(faces * run, width)
        moved = jnp.dot(rows, order_ref[...], preferred_element_type=F32)
        out_ref[0, :, at * width : (at + 1) * width] = moved.astype(BF)


def arrange(stiffness, mass_matrix, faces, n_freq):
    order, width = stiffness.shape
    run = order // (faces * n_freq)
    block = pl.BlockSpec((faces, 1, run, width), lambda d: (0, d, 0, 0))
    return pl.pallas_call(
        arrange_kernel,
        grid=(n_freq,),
        in_specs=[block, block],
        out_specs=pl.BlockSpec((1, width, 2 * width), lambda d: (d, 0, 0)),
        out_shape=jax.ShapeDtypeStruct((n_freq, width, 2 * width), BF),
        scratch_shapes=[pltpu.VMEM((width, width), BF)],
        compiler_params=params(),
        name="arrange",
    )(
        stiffness.reshape(faces, n_freq, run, width),
        mass_matrix.reshape(faces, n_freq, run, width),
    )


def apply_kernel(sign, faces, field_ref, pair_ref, omega_ref, local_ref, *rest):
    face_refs, sum_ref = rest[:faces], rest[faces]
    step = pl.program_id(0)
    width = local_ref.shape[1]
    rows = field_ref[...].reshape(-1, field_ref.shape[-1])
    count = rows.shape[0]
    if rows.dtype == F32:
        head = rows.astype(BF)
        rows = jnp.concatenate([head, (rows - head.astype(F32)).astype(BF)], axis=0)
    product = jnp.dot(rows, pair_ref[0], preferred_element_type=F32)
    if rows.shape[0] != count:
        product = product[:count] + product[count:]

    @pl.when(step == 0)
    def _():
        sum_ref[...] = product

    @pl.when(step > 0)
    def _():
        sum_ref[...] += product

    @pl.when(step == pl.num_programs(0) - 1)
    def _():
        stiff_part = sum_ref[:, :width]
        mass_part = sum_ref[:, width:]
        row = lax.broadcasted_iota(jnp.int32, (count, width), 0)
        real = lax.rem(row, 8) < 4
        other = jnp.where(
            real, -pltpu.roll(stiff_part, count - 4, 0), pltpu.roll(stiff_part, 4, 0)
        )
        local = stiff_part + (sign * LOSS_FACTOR) * other - omega_ref[...] * mass_part
        local_ref[...] = local
        run = width // faces
        for face, ref in enumerate(face_refs):
            ref[...] = local[:, face * run : (face + 1) * run]


def apply_local(field, pair, omega_rows, sign, faces, by_slot=False):
    n_freq, width, double = pair.shape
    count = omega_rows.shape[0]
    run = width // faces
    if by_slot:
        field_spec = pl.BlockSpec((n_freq, count // n_freq, width), lambda d: (0, 0, d))
    else:
        field_spec = pl.BlockSpec((1, count, width), lambda d: (d, 0, 0))
    whole = lambda d: (0, 0)
    return pl.pallas_call(
        functools.partial(apply_kernel, sign, faces),
        grid=(n_freq,),
        in_specs=[
            field_spec,
            pl.BlockSpec((1, width, double), lambda d: (d, 0, 0)),
            pl.BlockSpec((count, 1), whole),
        ],
        out_specs=[pl.BlockSpec((count, width), whole)]
        + [pl.BlockSpec((count, run), whole)] * faces,
        out_shape=[jax.ShapeDtypeStruct((count, width), F32)]
        + [jax.ShapeDtypeStruct((count, run), F32)] * faces,
        scratch_shapes=[pltpu.VMEM((count, double), F32)],
        compiler_params=params(),
        name="apply_local",
    )(field, pair, omega_rows)


def swap_faces(face_vals, once=False):
    west, east, south, north = face_vals

    def shift(values, axis, by):
        count = lax.axis_size(axis)
        pairs = [(i, i + by) for i in range(count) if 0 <= i + by < count]
        return lax.ppermute(values, axis, pairs)

    return (
        shift(east, "sx", 1),
        None if once else shift(west, "sx", -1),
        shift(north, "sy", 1),
        None if once else shift(south, "sy", -1),
    )


def finish_kernel(plan, faces, n_in, copies, *refs):
    combine, products, keep, send, places = plan
    given = sum(i is not None for i in places)
    local_ref, face_refs = refs[0], refs[1 : 1 + given]
    earlier = refs[1 + given : 1 + given + n_in]
    at = 1 + given + n_in
    coefs_ref = weight_ref = None
    if combine:
        coefs_ref, at = refs[at], at + 1
    if products:
        weight_ref, at = refs[at], at + 1
    outs = list(refs[at:])
    vector = local_ref[...]
    run = vector.shape[1] // faces
    halo = [jnp.zeros((vector.shape[0], run), F32) if i is None else face_refs[i][...] for i in places]
    vector = vector + jnp.concatenate(halo, axis=1)
    known = [ref[...] for ref in earlier]
    if combine:
        vector = vector * coefs_ref[:, len(combine) : len(combine) + 1]
        for slot, which in enumerate(combine):
            vector = vector + known[which] * coefs_ref[:, slot : slot + 1]
    known.append(vector)
    if keep:
        outs.pop(0)[...] = vector
    sums = None
    if products:
        weight = weight_ref[...]
        count = vector.shape[0]
        lane = lax.broadcasted_iota(jnp.int32, (count, 128), 1)
        sums = jnp.zeros((count, 128), F32)
        for slot, (left, right) in enumerate(products):
            value = jnp.sum(known[left] * known[right] * weight, axis=1, keepdims=True)
            sums = jnp.where(lane == slot, value, sums)
    if send is not None:
        sent = vector.astype(send)
        width = sent.shape[1]
        out = outs.pop(0)
        for copy in range(copies):
            out[copy, :, :width] = sent
            if products:
                out[copy, :, width:] = sums
    elif products:
        outs.pop(0)[...] = sums


def finish(
    local, halos, n_freq, earlier=(), combine=(), coefs=None, products=(), weight=None,
    keep=True, send=BF,
):
    count, width = local.shape
    given = [i for i, halo in enumerate(halos) if halo is not None]
    places = tuple(given.index(i) if i in given else None for i in range(len(halos)))
    args = [local, *(halos[i] for i in given), *earlier]
    if combine:
        args.append(coefs)
    if products:
        args.append(weight)
    shapes = []
    if keep:
        shapes.append(jax.ShapeDtypeStruct((count, width), F32))
    if send is not None:
        extra = 128 if products else 0
        shapes.append(jax.ShapeDtypeStruct((n_freq, count, width + extra), send))
    elif products:
        shapes.append(jax.ShapeDtypeStruct((count, 128), F32))
    plan = (tuple(combine), tuple(products), keep, send, places)
    return pl.pallas_call(
        functools.partial(finish_kernel, plan, len(halos), len(earlier), n_freq),
        out_shape=shapes,
        compiler_params=params(),
        name="finish",
    )(*args)


def exchange(blocks, axis):
    return lax.all_to_all(blocks, axis, 0, 0, tiled=False)


def total(values, axis):
    count = lax.axis_size(axis)
    return jnp.sum(exchange(jnp.broadcast_to(values[None], (count, *values.shape)), axis), axis=0)


def quad(entries, coefs):
    result = 0.0
    for i, left in enumerate(coefs):
        for j in range(i, len(coefs)):
            if left is None or coefs[j] is None:
                continue
            term = left * coefs[j] * entries[(i, j)]
            result = result + (term if i == j else 2.0 * term)
    return result


def combo(first, scale, second):
    out = []
    for a, b in zip(first, second):
        b = None if b is None else scale * b
        out.append(b if a is None else a if b is None else a + b)
    return out


def first_scalars(g, w):
    one = jnp.ones_like(g[(0, 0)])
    alpha0 = g[(0, 0)] / w[(0, 0)]
    res1 = [one, -alpha0]
    gamma1 = quad(g, res1)
    beta0 = gamma1 / g[(0, 0)]
    dir1 = [one + beta0, -alpha0]
    alpha1 = gamma1 / quad(w, dir1)
    return alpha0, res1, gamma1, beta0, dir1, alpha1


def last_scalars(g, w):
    alpha0, res1, gamma1, beta0, dir1, alpha1 = first_scalars(g, w)
    one = jnp.ones_like(alpha0)
    res1 = res1 + [None, None]
    dir1 = dir1 + [None, None]
    res2 = [None, None, one, None]
    gamma2 = g[(2, 2)]
    beta1 = gamma2 / gamma1
    dir2 = combo(res2, beta1, dir1)
    alpha2 = gamma2 / quad(w, dir2)
    change = combo(res1, -1.0, res2)
    image = combo([None, None, None, one], beta1 / alpha1, change)
    res3 = combo(res2, -alpha2, image)
    gamma3 = quad(g, res3)
    dir3 = combo(res3, gamma3 / gamma2, dir2)
    alpha3 = gamma3 / quad(w, dir3)
    answer = combo([alpha0, None, None, None], alpha1, dir1)
    answer = combo(answer, alpha2, dir2)
    answer = combo(answer, alpha3, dir3)
    return answer, gamma3


def body(stiffness, mass_matrix, omega_table, assignment, adjoint_load, forward_state, owner_index):
    n_freq = lax.axis_size("freq")
    n_sub = lax.axis_size("sx") * lax.axis_size("sy")
    slots, faces, face_len = adjoint_load.shape[2], adjoint_load.shape[4], adjoint_load.shape[5]
    order = faces * face_len
    run = face_len // n_freq
    width = faces * run
    count = n_freq * slots * 2
    own = 2 * slots
    me = lax.axis_index("freq")

    load = jnp.swapaxes(adjoint_load[0, 0].astype(BF), 0, 1).reshape(own, faces, n_freq, run)
    load = jnp.swapaxes(load, 1, 2).reshape(own, order)
    tags = jnp.broadcast_to(assignment.astype(BF)[None, :], (2, slots)).reshape(own, 1)
    packet = jnp.concatenate([load, jnp.broadcast_to(tags, (own, 128))], axis=1)
    field = exchange(jnp.broadcast_to(packet[None], (n_freq, *packet.shape)), "freq")
    pair = arrange(stiffness[0, 0], mass_matrix[0, 0], faces, n_freq)
    slot_tags = field[:, :, order].reshape(count).astype(jnp.int32)
    matches = slot_tags[:, None] == jnp.arange(omega_table.shape[0], dtype=jnp.int32)[None, :]
    omega_rows = jnp.sum(jnp.where(matches, omega_table[None, :], 0.0), axis=1, keepdims=True)

    def inside(axis, at):
        return jnp.where(lax.axis_index(axis) == at, 1.0, 0.5).astype(F32)

    face_weight = jnp.stack(
        [
            inside("sx", 0),
            inside("sx", lax.axis_size("sx") - 1),
            inside("sy", 0),
            inside("sy", lax.axis_size("sy") - 1),
        ]
    )
    weight = jnp.repeat(face_weight, run)[None, :]
    once = jnp.where(face_weight < 1.0, jnp.array([1.0, 0.0, 1.0, 0.0], F32), 1.0)
    weight_once = jnp.repeat(once, run)[None, :]

    def local_of(field, sign, by_slot=False, once=False):
        local, *face_vals = apply_local(field, pair, omega_rows, sign, faces, by_slot)
        return local, swap_faces(face_vals, once)

    def part_sum(rows):
        return jnp.sum(rows.reshape(-1, 2, slots, rows.shape[-1]), axis=1)

    def to_rows(values):
        wide = jnp.broadcast_to(values[:, None], (n_freq, 2, slots, values.shape[-1]))
        return wide.reshape(count, values.shape[-1])

    local, halo = local_of(field, -1.0, by_slot=True)
    u0, send = finish(local, halo, n_freq, send=F32)
    sent0 = exchange(send, "freq")
    local, halo = local_of(sent0, 1.0)
    w0, send = finish(local, halo, n_freq, send=F32)
    local, halo = local_of(exchange(send, "freq"), -1.0)
    u1, send = finish(local, halo, n_freq, send=F32)
    sent1 = exchange(send, "freq")
    local, halo = local_of(sent1, 1.0)
    products = ((0, 0), (0, 1), (1, 1), (2, 2), (2, 3), (3, 3))
    w1, send = finish(
        local, halo, n_freq, earlier=(u0, u1, w0), products=products, weight=weight, send=F32
    )
    sent = exchange(send, "freq")
    sums = jnp.sum(sent[:, :, width : width + len(products)], axis=0)
    sums = part_sum(sums)
    sums = total(total(sums.reshape(-1), "sy"), "sx").reshape(n_freq, slots, len(products))
    g = {(0, 0): sums[..., 0], (0, 1): sums[..., 1], (1, 1): sums[..., 2]}
    w = {(0, 0): sums[..., 3], (0, 1): sums[..., 4], (1, 1): sums[..., 5]}
    alpha0, _, _, beta0, _, alpha1 = first_scalars(g, w)
    coefs = to_rows(
        jnp.stack(
            [jnp.ones_like(alpha0), -(alpha0 + alpha1 * (1.0 + beta0)), alpha0 * alpha1], axis=-1
        )
    )
    local, halo = local_of(sent, -1.0)
    u2, send = finish(local, halo, n_freq, earlier=(u0, u1), combine=(0, 1), coefs=coefs)
    sent2 = exchange(send, "freq")
    local, halo = local_of(sent2, 1.0)
    w2, send = finish(local, halo, n_freq)
    local, halo = local_of(exchange(send, "freq"), -1.0)
    u3, send = finish(local, halo, n_freq)
    sent3 = exchange(send, "freq")
    local, halo = local_of(sent3, 1.0, once=True)
    later = ((0, 2), (1, 2), (2, 2), (0, 3), (1, 3), (2, 3), (3, 3))
    products = later + tuple((4 + i, 4 + j) for i, j in later)
    (rows,) = finish(
        local, halo, n_freq, earlier=(u0, u1, u2, u3, w0, w1, w2), products=products,
        weight=weight_once, keep=False, send=None,
    )
    rows = part_sum(rows[:, : len(products)]).reshape(n_freq, slots * len(products))
    ours = jnp.sum(exchange(rows, "freq"), axis=0)
    ours = total(total(ours, "sy"), "sx").reshape(slots, len(products))
    mine = lax.dynamic_index_in_dim(sums, me, 0, keepdims=False)
    g = {(0, 0): mine[:, 0], (0, 1): mine[:, 1], (1, 1): mine[:, 2]}
    w = {(0, 0): mine[:, 3], (0, 1): mine[:, 4], (1, 1): mine[:, 5]}
    for at, key in enumerate(later):
        g[key] = ours[:, at]
        w[key] = ours[:, len(later) + at]
    answer, gamma = last_scalars(g, w)
    residual_level = jnp.log(gamma / float(n_sub * 2 * order))

    adjoint = 0.0
    for values, sent in zip(answer, (sent0, sent1, sent2, sent3)):
        block = lax.dynamic_slice_in_dim(sent, me * own, own, axis=1)[:, :, :width].astype(F32)
        adjoint = adjoint + block * jnp.tile(values, 2)[None, :, None]
    adjoint = adjoint.reshape(n_freq, 2, slots, faces, run)
    adjoint = jnp.transpose(adjoint, (2, 1, 3, 0, 4)).reshape(slots, 2, faces, face_len)

    state = forward_state[0, 0].astype(F32)
    adj_real, adj_imag = adjoint[:, 0], adjoint[:, 1]
    state_real, state_imag = state[:, 0], state[:, 1]
    term = (
        adj_real * state_real
        - adj_imag * state_imag
        - LOSS_FACTOR * (adj_real * state_imag + adj_imag * state_real)
    )
    dof_total = jnp.sum(term, axis=0).reshape(1, order)
    owner = owner_index[0, 0].reshape(1, order)
    high = jnp.arange(DE_SUB // LOW, dtype=jnp.int32)[:, None]
    low = jnp.arange(LOW, dtype=jnp.int32)[:, None]
    spread = jnp.where(lax.div(owner, LOW) == high, dof_total, 0.0)
    places = jnp.where(lax.rem(owner, LOW) == low, 1.0, 0.0)
    partial_grad = lax.dot_general(
        spread, places, (((1,), (1,)), ((), ())), precision=lax.Precision.HIGHEST
    )
    grad_factor = (DE_SUB / (slots * n_freq * order)) ** 0.5
    partial_grad = (-grad_factor * partial_grad).reshape(n_freq, DE_SUB // n_freq)
    gradient = jnp.sum(exchange(partial_grad, "freq"), axis=0)
    return (adjoint[None, None], gradient[None, None], residual_level)


def solution(mesh):
    return jax.shard_map(
        body,
        mesh=mesh,
        in_specs=(
            P("sx", "sy", None, "freq"),
            P("sx", "sy", None, "freq"),
            P(),
            P("freq"),
            P("sx", "sy", "freq", None, None, None),
            P("sx", "sy", "freq", None, None, None),
            P("sx", "sy", None, None),
        ),
        out_specs=(P("sx", "sy", "freq", None, None, None), P("sx", "sy", "freq"), P("freq")),
        check_vma=False,
    )
```

time: 1390 us -> 386 us (0.28)
  the two profiles are of different devices: /device:TPU:32 before, /device:TPU:1 now
where the time goes in v1:
time: 386 us; the launch traced here: 384 us
  blocking collectives  140 us (36%)
  starting transfers between devices  117 us (30%)
  waiting for transfers between devices  71.9 us (19%)
  Pallas kernels  26.6 us (7%)
  local copies, waits for them, and re-layouts  23 us (6%)
    all_to_all x7, blocking collectives, exchange(): return lax.all_to_all(blocks, axis, 0, 0, tiled=False)  140 us
    ppermute x30, starting transfers between devices, shift(): return lax.ppermute(values, axis, pairs)  79.1 us
    all_to_all x7, waiting for transfers between devices, exchange(): return lax.all_to_all(blocks, axis, 0, 0, tiled=False)  49.1 us
    all_to_all x7, starting transfers between devices, exchange(): return lax.all_to_all(blocks, axis, 0, 0, tiled=False)  37.8 us
    ppermute x30, waiting for transfers between devices, shift(): return lax.ppermute(values, axis, pairs)  22.8 us
    pallas_call x8, Pallas kernels, apply_local(): pl.pallas_call(functools.partial(apply_kernel, sign, faces), grid=(n_freq...  19.5 us
    unnamed x32, local copies, waits for them, and re-layouts  15.4 us
  transfers between devices with their start and end apart: 37, of which 14 were waited for; matrix products, arithmetic and copies ran while one was open for 1% of the time, Pallas kernels for 2%

profile of v1, /device:TPU:1, one launch (start us, length us, event | category | flops | bytes accessed | tf_op | source)
XLA Modules:
  0.0 383.9 jit_solution(4457874336355080133)
XLA Ops:
  3.5 10.9 %all-to-all-start = ((bf16[8,8,3200]{2,1,0:T(8,128)(2,1)}), bf16[8,8,3200]{2,1,0:T(8,128)(2,1)S(1)}, u32[]{:S(2)}, u32[]{:S(2)}) async-start(bf16[8,8,3200]{2,1,0:T(8,128)(2,1)} %broadcast_in_dim.106), calls=%async_computation | async-start | bytes 819200 | tf_op jit(solution)/shard_map/all_to_all | solution.py:211
  17.7 4.9 %arrange.1.pair_ref = bf16[8,384,768]{2,1,0:T(8,128)(2,1)S(1)} custom-call(bf16[4,8,96,384]{3,2,1,0:T(8,128)(2,1)S(1)} %bitcast.29, bf16[4,8,96,384]{3,2,1,0:T(8,128)(2,1)S(1)} %bitcast.30), custom_call_target="tpu_custom_call" | custom-call | tf_op jit(solution)/shard_map/arrange/pallas_call | solution.py:41
  24.7 4.3 %all-to-all-done.field_ref = bf16[8,8,3200]{2,1,0:T(8,128)(2,1)S(1)} async-done(((bf16[8,8,3200]{2,1,0:T(8,128)(2,1)}), bf16[8,8,3200]{2,1,0:T(8,128)(2,1)S(1)}, u32[]{:S(2)}, u32[]{:S(2)}) %all-to-all-start) | async-done | bytes 409632 | tf_op jit(solution)/shard_map/all_to_all | solution.py:211
  34.3 4.4 %collective-permute-start = (f32[64,96]{1,0:T(8,128)S(1)}, f32[64,96]{1,0:T(8,128)S(1)}, u32[]{:S(2)}, u32[]{:S(2)}) collective-permute-start(f32[64,96]{1,0:T(8,128)S(1)} %get-tuple-element.56), channel_id=1, source_target_pairs={{0,4},{4,8},{8,12},{12,16},{16,20},{20,24},{24,28},{28,32},{32,36}... | collective-permute-start | bytes 73736 | tf_op jit(solution)/shard_map/ppermute | solution.py:126
  45.1 3.3 collective-permute-done.3.refs_4_
  48.6 25.3 %all_to_all.83.field_ref = f32[8,64,384]{2,1,0:T(8,128)S(1)} all-to-all(f32[8,64,384]{2,1,0:T(8,128)S(1)} %get-tuple-element.60), channel_id=1, replica_groups=mesh['freq'=8,'sx'=16,'sy'=4] {'freq'}, dimensions={0} | all-to-all | bytes 1572864 | tf_op jit(solution)/shard_map/all_to_all | solution.py:211
  76.4 4.2 %collective-permute-start.4 = (f32[64,96]{1,0:T(8,128)S(1)}, f32[64,96]{1,0:T(8,128)S(1)}, u32[]{:S(2)}, u32[]{:S(2)}) collective-permute-start(f32[64,96]{1,0:T(8,128)S(1)} %get-tuple-element.62), channel_id=1, source_target_pairs={{0,4},{4,8},{8,12},{12,16},{16,20},{20,24},{24,28},{28,32},{32,36}... | collective-permute-start | bytes 73736 | tf_op jit(solution)/shard_map/ppermute | solution.py:126
  87.0 3.3 collective-permute-done.7.refs_4_
  90.5 25.4 %all_to_all.84.field_ref = f32[8,64,384]{2,1,0:T(8,128)S(1)} all-to-all(f32[8,64,384]{2,1,0:T(8,128)S(1)} %get-tuple-element.66), channel_id=1, replica_groups=mesh['freq'=8,'sx'=16,'sy'=4] {'freq'}, dimensions={0} | all-to-all | bytes 1572864 | tf_op jit(solution)/shard_map/all_to_all | solution.py:211
  122.5 4.5 %collective-permute-start.8 = (f32[64,96]{1,0:T(8,128)S(1)}, f32[64,96]{1,0:T(8,128)S(1)}, u32[]{:S(2)}, u32[]{:S(2)}) collective-permute-start(f32[64,96]{1,0:T(8,128)S(1)} %get-tuple-element.68), channel_id=1, source_target_pairs={{0,4},{4,8},{8,12},{12,16},{16,20},{20,24},{24,28},{28,32},{32,36}... | collective-permute-start | bytes 73736 | tf_op jit(solution)/shard_map/ppermute | solution.py:126
  133.3 3.5 all-to-all-start.3
  136.8 21.8 %all-to-all-done.3.field_ref = f32[8,64,384]{2,1,0:T(8,128)S(1)} async-done(((f32[8,64,384]{2,1,0:T(8,128)}), f32[8,64,384]{2,1,0:T(8,128)S(1)}, u32[]{:S(2)}, u32[]{:S(2)}) %all-to-all-start.3) | async-done | bytes 786464 | tf_op jit(solution)/shard_map/all_to_all | solution.py:211
  163.5 5.2 %collective-permute-start.12 = (f32[64,96]{1,0:T(8,128)S(1)}, f32[64,96]{1,0:T(8,128)S(1)}, u32[]{:S(2)}, u32[]{:S(2)}) collective-permute-start(f32[64,96]{1,0:T(8,128)S(1)} %get-tuple-element.74), channel_id=1, source_target_pairs={{0,4},{4,8},{8,12},{12,16},{16,20},{20,24},{24,28},{28,32},{32,36}... | collective-permute-start | bytes 73736 | tf_op jit(solution)/shard_map/ppermute | solution.py:126
  170.7 4.3 %collective-permute-start.14 = (f32[64,96]{1,0:T(8,128)S(1)}, f32[64,96]{1,0:T(8,128)S(1)}, u32[]{:S(2)}, u32[]{:S(2)}) collective-permute-start(f32[64,96]{1,0:T(8,128)S(1)} %get-tuple-element.76), channel_id=1, source_target_pairs={{0,1},{1,2},{2,3},{4,5},{5,6},{6,7},{8,9},{9,10},{10,11},{12,13},{... | collective-permute-start | bytes 73736 | tf_op jit(solution)/shard_map/ppermute | solution.py:126
  179.9 29.8 %all_to_all.85.field_ref = f32[8,64,512]{2,1,0:T(8,128)S(1)} all-to-all(f32[8,64,512]{2,1,0:T(8,128)S(1)} %get-tuple-element.81), channel_id=1, replica_groups=mesh['freq'=8,'sx'=16,'sy'=4] {'freq'}, dimensions={0} | all-to-all | bytes 2097152 | tf_op jit(solution)/shard_map/all_to_all | solution.py:211
  209.9 6.5 %all_to_all.86 = f32[4,1,192]{2,1,0:T(1,128)S(1)} all-to-all(f32[4,1,192]{2,1,0:T(1,128)S(1)} %broadcast_in_dim.112), channel_id=1, replica_groups=mesh['freq'=8,'sx'=16,'sy'=4] {'sy'}, dimensions={0} | all-to-all | bytes 6144 | tf_op jit(solution)/shard_map/all_to_all | solution.py:211
  217.0 7.2 %all-to-all-start.6 = ((f32[16,1,192]{2,1,0:T(1,128)}), f32[16,1,192]{2,1,0:T(1,128)S(1)}, u32[]{:S(2)}, u32[]{:S(2)}) async-start(f32[16,1,192]{2,1,0:T(1,128)} %broadcast_in_dim.113), calls=%async_computation.6 | async-start | bytes 32768 | tf_op jit(solution)/shard_map/all_to_all | solution.py:211
  229.2 3.6 collective-permute-start.16
  241.8 17.6 %all_to_all.87.field_ref = bf16[8,64,384]{2,1,0:T(8,128)(2,1)S(1)} all-to-all(bf16[8,64,384]{2,1,0:T(8,128)(2,1)S(1)} %get-tuple-element.87), channel_id=1, replica_groups=mesh['freq'=8,'sx'=16,'sy'=4] {'freq'}, dimensions={0} | all-to-all | bytes 786432 | tf_op jit(solution)/shard_map/all_to_all | solution.py:211
  272.6 3.3 collective-permute-done.23.refs_4_
  276.1 17.6 %all_to_all.88.field_ref = bf16[8,64,384]{2,1,0:T(8,128)(2,1)S(1)} all-to-all(bf16[8,64,384]{2,1,0:T(8,128)(2,1)S(1)} %get-tuple-element.93), channel_id=1, replica_groups=mesh['freq'=8,'sx'=16,'sy'=4] {'freq'}, dimensions={0} | all-to-all | bytes 786432 | tf_op jit(solution)/shard_map/all_to_all | solution.py:211
  295.8 3.4 collective-permute-start.24
  305.6 3.3 collective-permute-done.27.refs_4_
  309.0 17.6 %all_to_all.89.field_ref = bf16[8,64,384]{2,1,0:T(8,128)(2,1)S(1)} all-to-all(bf16[8,64,384]{2,1,0:T(8,128)(2,1)S(1)} %get-tuple-element.99), channel_id=1, replica_groups=mesh['freq'=8,'sx'=16,'sy'=4] {'freq'}, dimensions={0} | all-to-all | bytes 786432 | tf_op jit(solution)/shard_map/all_to_all | solution.py:211
  329.4 5.2 %collective-permute-start.28 = (f32[64,96]{1,0:T(8,128)S(1)}, f32[64,96]{1,0:T(8,128)S(1)}, u32[]{:S(2)}, u32[]{:S(2)}) collective-permute-start(f32[64,96]{1,0:T(8,128)S(1)} %get-tuple-element.101), channel_id=1, source_target_pairs={{0,4},{4,8},{8,12},{12,16},{16,20},{20,24},{24,28},{28,32},{32,36}... | collective-permute-start | bytes 73736 | tf_op jit(solution)/shard_map/ppermute | solution.py:126
  341.8 6.4 %all-to-all-done.10 = f32[8,1,56]{2,1,0:T(1,128)S(1)} async-done(((f32[8,1,56]{2,1,0:T(1,128)}), f32[8,1,56]{2,1,0:T(1,128)S(1)}, u32[]{:S(2)}, u32[]{:S(2)}) %all-to-all-start.10) | async-done | bytes 1824 | tf_op jit(solution)/shard_map/all_to_all | solution.py:211
  348.8 3.3 all-to-all-start.11
  352.1 4.1 %all-to-all-done.11 = f32[4,1,56]{2,1,0:T(1,128)S(1)} async-done(((f32[4,1,56]{2,1,0:T(1,128)}), f32[4,1,56]{2,1,0:T(1,128)S(1)}, u32[]{:S(2)}, u32[]{:S(2)}) %all-to-all-start.11) | async-done | bytes 928 | tf_op jit(solution)/shard_map/all_to_all | solution.py:211
  356.8 6.2 %all-to-all-start.12 = ((f32[16,1,56]{2,1,0:T(1,128)}), f32[16,1,56]{2,1,0:T(1,128)S(1)}, u32[]{:S(2)}, u32[]{:S(2)}) async-start(f32[16,1,56]{2,1,0:T(1,128)} %broadcast_in_dim.117), calls=%async_computation.12 | async-start | bytes 16384 | tf_op jit(solution)/shard_map/all_to_all | solution.py:211
  363.3 6.7 %all-to-all-done.12 = f32[16,1,56]{2,1,0:T(1,128)S(1)} async-done(((f32[16,1,56]{2,1,0:T(1,128)}), f32[16,1,56]{2,1,0:T(1,128)S(1)}, u32[]{:S(2)}, u32[]{:S(2)}) %all-to-all-start.12) | async-done | bytes 3616 | tf_op jit(solution)/shard_map/all_to_all | solution.py:211
  373.5 3.3 all-to-all-start.13
  377.6 5.8 %all-to-all-done.13 = f32[8,1,216]{2,1,0:T(1,128)S(1)} async-done(((f32[8,1,216]{2,1,0:T(1,128)}), f32[8,1,216]{2,1,0:T(1,128)S(1)}, u32[]{:S(2)}, u32[]{:S(2)}) %all-to-all-start.13) | async-done | bytes 6944 | tf_op jit(solution)/shard_map/all_to_all | solution.py:211
  (168 shorter events, 106.0 us)
Async XLA Ops:
  3.5 25.5 %all-to-all-start = ((bf16[8,8,3200]{2,1,0:T(8,128)(2,1)}), bf16[8,8,3200]{2,1,0:T(8,128)(2,1)S(1)}, u32[]{:S(2)}, u32[]{:S(2)}) async-start(bf16[8,8,3200]{2,1,0:T(8,128)(2,1)} %broadcast_in_dim.106), calls=%async_computation | async-start | bytes 819200 | tf_op jit(solution)/shard_map/all_to_all | solution.py:211
  34.3 10.8 %collective-permute-start = (f32[64,96]{1,0:T(8,128)S(1)}, f32[64,96]{1,0:T(8,128)S(1)}, u32[]{:S(2)}, u32[]{:S(2)}) collective-permute-start(f32[64,96]{1,0:T(8,128)S(1)} %get-tuple-element.56), channel_id=1, source_target_pairs={{0,4},{4,8},{8,12},{12,16},{16,20},{20,24},{24,28},{28,32},{32,36}... | collective-permute-start | bytes 73736 | tf_op jit(solution)/shard_map/ppermute | solution.py:126
  38.7 6.4 %collective-permute-start.1 = (f32[64,96]{1,0:T(8,128)S(1)}, f32[64,96]{1,0:T(8,128)S(1)}, u32[]{:S(2)}, u32[]{:S(2)}) collective-permute-start(f32[64,96]{1,0:T(8,128)S(1)} %get-tuple-element.57), channel_id=1, source_target_pairs={{4,0},{8,4},{12,8},{16,12},{20,16},{24,20},{28,24},{32,28},{36,32}... | collective-permute-start | bytes 73736 | tf_op jit(solution)/shard_map/ppermute | solution.py:126
  43.8 4.7 %collective-permute-start.3 = (f32[64,96]{1,0:T(8,128)S(1)}, f32[64,96]{1,0:T(8,128)S(1)}, u32[]{:S(2)}, u32[]{:S(2)}) collective-permute-start(f32[64,96]{1,0:T(8,128)S(1)} %get-tuple-element.59), channel_id=1, source_target_pairs={{1,0},{2,1},{3,2},{5,4},{6,5},{7,6},{9,8},{10,9},{11,10},{13,12},{... | collective-permute-start | bytes 73736 | tf_op jit(solution)/shard_map/ppermute | solution.py:126
  76.4 10.6 %collective-permute-start.4 = (f32[64,96]{1,0:T(8,128)S(1)}, f32[64,96]{1,0:T(8,128)S(1)}, u32[]{:S(2)}, u32[]{:S(2)}) collective-permute-start(f32[64,96]{1,0:T(8,128)S(1)} %get-tuple-element.62), channel_id=1, source_target_pairs={{0,4},{4,8},{8,12},{12,16},{16,20},{20,24},{24,28},{28,32},{32,36}... | collective-permute-start | bytes 73736 | tf_op jit(solution)/shard_map/ppermute | solution.py:126
  80.7 6.4 %collective-permute-start.5 = (f32[64,96]{1,0:T(8,128)S(1)}, f32[64,96]{1,0:T(8,128)S(1)}, u32[]{:S(2)}, u32[]{:S(2)}) collective-permute-start(f32[64,96]{1,0:T(8,128)S(1)} %get-tuple-element.63), channel_id=1, source_target_pairs={{4,0},{8,4},{12,8},{16,12},{20,16},{24,20},{28,24},{32,28},{36,32}... | collective-permute-start | bytes 73736 | tf_op jit(solution)/shard_map/ppermute | solution.py:126
  85.7 4.7 %collective-permute-start.7 = (f32[64,96]{1,0:T(8,128)S(1)}, f32[64,96]{1,0:T(8,128)S(1)}, u32[]{:S(2)}, u32[]{:S(2)}) collective-permute-start(f32[64,96]{1,0:T(8,128)S(1)} %get-tuple-element.65), channel_id=1, source_target_pairs={{1,0},{2,1},{3,2},{5,4},{6,5},{7,6},{9,8},{10,9},{11,10},{13,12},{... | collective-permute-start | bytes 73736 | tf_op jit(solution)/shard_map/ppermute | solution.py:126
  118.4 10.6 %collective-permute-start.10 = (f32[64,96]{1,0:T(8,128)S(1)}, f32[64,96]{1,0:T(8,128)S(1)}, u32[]{:S(2)}, u32[]{:S(2)}) collective-permute-start(f32[64,96]{1,0:T(8,128)S(1)} %get-tuple-element.70), channel_id=1, source_target_pairs={{0,1},{1,2},{2,3},{4,5},{5,6},{6,7},{8,9},{9,10},{10,11},{12,13},{... | collective-permute-start | bytes 73736 | tf_op jit(solution)/shard_map/ppermute | solution.py:126
  121.2 7.7 %collective-permute-start.11 = (f32[64,96]{1,0:T(8,128)S(1)}, f32[64,96]{1,0:T(8,128)S(1)}, u32[]{:S(2)}, u32[]{:S(2)}) collective-permute-start(f32[64,96]{1,0:T(8,128)S(1)} %get-tuple-element.71), channel_id=1, source_target_pairs={{1,0},{2,1},{3,2},{5,4},{6,5},{7,6},{9,8},{10,9},{11,10},{13,12},{... | collective-permute-start | bytes 73736 | tf_op jit(solution)/shard_map/ppermute | solution.py:126
  122.5 6.4 %collective-permute-start.8 = (f32[64,96]{1,0:T(8,128)S(1)}, f32[64,96]{1,0:T(8,128)S(1)}, u32[]{:S(2)}, u32[]{:S(2)}) collective-permute-start(f32[64,96]{1,0:T(8,128)S(1)} %get-tuple-element.68), channel_id=1, source_target_pairs={{0,4},{4,8},{8,12},{12,16},{16,20},{20,24},{24,28},{28,32},{32,36}... | collective-permute-start | bytes 73736 | tf_op jit(solution)/shard_map/ppermute | solution.py:126
  127.0 5.2 %collective-permute-start.9 = (f32[64,96]{1,0:T(8,128)S(1)}, f32[64,96]{1,0:T(8,128)S(1)}, u32[]{:S(2)}, u32[]{:S(2)}) collective-permute-start(f32[64,96]{1,0:T(8,128)S(1)} %get-tuple-element.69), channel_id=1, source_target_pairs={{4,0},{8,4},{12,8},{16,12},{20,16},{24,20},{28,24},{32,28},{36,32}... | collective-permute-start | bytes 73736 | tf_op jit(solution)/shard_map/ppermute | solution.py:126
  133.3 25.4 %all-to-all-start.3 = ((f32[8,64,384]{2,1,0:T(8,128)}), f32[8,64,384]{2,1,0:T(8,128)S(1)}, u32[]{:S(2)}, u32[]{:S(2)}) async-start(f32[8,64,384]{2,1,0:T(8,128)} %get-tuple-element.72), calls=%async_computation.3 | async-start | bytes 1572864 | tf_op jit(solution)/shard_map/all_to_all | solution.py:211
  163.5 13.0 %collective-permute-start.12 = (f32[64,96]{1,0:T(8,128)S(1)}, f32[64,96]{1,0:T(8,128)S(1)}, u32[]{:S(2)}, u32[]{:S(2)}) collective-permute-start(f32[64,96]{1,0:T(8,128)S(1)} %get-tuple-element.74), channel_id=1, source_target_pairs={{0,4},{4,8},{8,12},{12,16},{16,20},{20,24},{24,28},{28,32},{32,36}... | collective-permute-start | bytes 73736 | tf_op jit(solution)/shard_map/ppermute | solution.py:126
  168.7 7.8 %collective-permute-start.13 = (f32[64,96]{1,0:T(8,128)S(1)}, f32[64,96]{1,0:T(8,128)S(1)}, u32[]{:S(2)}, u32[]{:S(2)}) collective-permute-start(f32[64,96]{1,0:T(8,128)S(1)} %get-tuple-element.75), channel_id=1, source_target_pairs={{4,0},{8,4},{12,8},{16,12},{20,16},{24,20},{28,24},{32,28},{36,32}... | collective-permute-start | bytes 73736 | tf_op jit(solution)/shard_map/ppermute | solution.py:126
  170.7 5.8 %collective-permute-start.14 = (f32[64,96]{1,0:T(8,128)S(1)}, f32[64,96]{1,0:T(8,128)S(1)}, u32[]{:S(2)}, u32[]{:S(2)}) collective-permute-start(f32[64,96]{1,0:T(8,128)S(1)} %get-tuple-element.76), channel_id=1, source_target_pairs={{0,1},{1,2},{2,3},{4,5},{5,6},{6,7},{8,9},{9,10},{10,11},{12,13},{... | collective-permute-start | bytes 73736 | tf_op jit(solution)/shard_map/ppermute | solution.py:126
  174.9 4.7 %collective-permute-start.15 = (f32[64,96]{1,0:T(8,128)S(1)}, f32[64,96]{1,0:T(8,128)S(1)}, u32[]{:S(2)}, u32[]{:S(2)}) collective-permute-start(f32[64,96]{1,0:T(8,128)S(1)} %get-tuple-element.77), channel_id=1, source_target_pairs={{1,0},{2,1},{3,2},{5,4},{6,5},{7,6},{9,8},{10,9},{11,10},{13,12},{... | collective-permute-start | bytes 73736 | tf_op jit(solution)/shard_map/ppermute | solution.py:126
  217.0 21.2 %all-to-all-start.6 = ((f32[16,1,192]{2,1,0:T(1,128)}), f32[16,1,192]{2,1,0:T(1,128)S(1)}, u32[]{:S(2)}, u32[]{:S(2)}) async-start(f32[16,1,192]{2,1,0:T(1,128)} %broadcast_in_dim.113), calls=%async_computation.6 | async-start | bytes 32768 | tf_op jit(solution)/shard_map/all_to_all | solution.py:211
  229.2 10.1 %collective-permute-start.16 = (f32[64,96]{1,0:T(8,128)S(1)}, f32[64,96]{1,0:T(8,128)S(1)}, u32[]{:S(2)}, u32[]{:S(2)}) collective-permute-start(f32[64,96]{1,0:T(8,128)S(1)} %get-tuple-element.83), channel_id=1, source_target_pairs={{0,4},{4,8},{8,12},{12,16},{16,20},{20,24},{24,28},{28,32},{32,36}... | collective-permute-start | bytes 73736 | tf_op jit(solution)/shard_map/ppermute | solution.py:126
  232.8 6.5 %collective-permute-start.17 = (f32[64,96]{1,0:T(8,128)S(1)}, f32[64,96]{1,0:T(8,128)S(1)}, u32[]{:S(2)}, u32[]{:S(2)}) collective-permute-start(f32[64,96]{1,0:T(8,128)S(1)} %get-tuple-element.84), channel_id=1, source_target_pairs={{4,0},{8,4},{12,8},{16,12},{20,16},{24,20},{28,24},{32,28},{36,32}... | collective-permute-start | bytes 73736 | tf_op jit(solution)/shard_map/ppermute | solution.py:126
  234.8 4.6 %collective-permute-start.18 = (f32[64,96]{1,0:T(8,128)S(1)}, f32[64,96]{1,0:T(8,128)S(1)}, u32[]{:S(2)}, u32[]{:S(2)}) collective-permute-start(f32[64,96]{1,0:T(8,128)S(1)} %get-tuple-element.85), channel_id=1, source_target_pairs={{0,1},{1,2},{2,3},{4,5},{5,6},{6,7},{8,9},{9,10},{10,11},{12,13},{... | collective-permute-start | bytes 73736 | tf_op jit(solution)/shard_map/ppermute | solution.py:126
  236.9 4.7 %collective-permute-start.19 = (f32[64,96]{1,0:T(8,128)S(1)}, f32[64,96]{1,0:T(8,128)S(1)}, u32[]{:S(2)}, u32[]{:S(2)}) collective-permute-start(f32[64,96]{1,0:T(8,128)S(1)} %get-tuple-element.86), channel_id=1, source_target_pairs={{1,0},{2,1},{3,2},{5,4},{6,5},{7,6},{9,8},{10,9},{11,10},{13,12},{... | collective-permute-start | bytes 73736 | tf_op jit(solution)/shard_map/ppermute | solution.py:126
  263.9 8.7 %collective-permute-start.20 = (f32[64,96]{1,0:T(8,128)S(1)}, f32[64,96]{1,0:T(8,128)S(1)}, u32[]{:S(2)}, u32[]{:S(2)}) collective-permute-start(f32[64,96]{1,0:T(8,128)S(1)} %get-tuple-element.89), channel_id=1, source_target_pairs={{0,4},{4,8},{8,12},{12,16},{16,20},{20,24},{24,28},{28,32},{32,36}... | collective-permute-start | bytes 73736 | tf_op jit(solution)/shard_map/ppermute | solution.py:126
  267.2 5.4 %collective-permute-start.21 = (f32[64,96]{1,0:T(8,128)S(1)}, f32[64,96]{1,0:T(8,128)S(1)}, u32[]{:S(2)}, u32[]{:S(2)}) collective-permute-start(f32[64,96]{1,0:T(8,128)S(1)} %get-tuple-element.90), channel_id=1, source_target_pairs={{4,0},{8,4},{12,8},{16,12},{20,16},{24,20},{28,24},{32,28},{36,32}... | collective-permute-start | bytes 73736 | tf_op jit(solution)/shard_map/ppermute | solution.py:126
  271.3 4.7 %collective-permute-start.23 = (f32[64,96]{1,0:T(8,128)S(1)}, f32[64,96]{1,0:T(8,128)S(1)}, u32[]{:S(2)}, u32[]{:S(2)}) collective-permute-start(f32[64,96]{1,0:T(8,128)S(1)} %get-tuple-element.92), channel_id=1, source_target_pairs={{1,0},{2,1},{3,2},{5,4},{6,5},{7,6},{9,8},{10,9},{11,10},{13,12},{... | collective-permute-start | bytes 73736 | tf_op jit(solution)/shard_map/ppermute | solution.py:126
  295.8 9.8 %collective-permute-start.24 = (f32[64,96]{1,0:T(8,128)S(1)}, f32[64,96]{1,0:T(8,128)S(1)}, u32[]{:S(2)}, u32[]{:S(2)}) collective-permute-start(f32[64,96]{1,0:T(8,128)S(1)} %get-tuple-element.95), channel_id=1, source_target_pairs={{0,4},{4,8},{8,12},{12,16},{16,20},{20,24},{24,28},{28,32},{32,36}... | collective-permute-start | bytes 73736 | tf_op jit(solution)/shard_map/ppermute | solution.py:126
  299.2 6.3 %collective-permute-start.25 = (f32[64,96]{1,0:T(8,128)S(1)}, f32[64,96]{1,0:T(8,128)S(1)}, u32[]{:S(2)}, u32[]{:S(2)}) collective-permute-start(f32[64,96]{1,0:T(8,128)S(1)} %get-tuple-element.96), channel_id=1, source_target_pairs={{4,0},{8,4},{12,8},{16,12},{20,16},{24,20},{28,24},{32,28},{36,32}... | collective-permute-start | bytes 73736 | tf_op jit(solution)/shard_map/ppermute | solution.py:126
  304.3 4.7 %collective-permute-start.27 = (f32[64,96]{1,0:T(8,128)S(1)}, f32[64,96]{1,0:T(8,128)S(1)}, u32[]{:S(2)}, u32[]{:S(2)}) collective-permute-start(f32[64,96]{1,0:T(8,128)S(1)} %get-tuple-element.98), channel_id=1, source_target_pairs={{1,0},{2,1},{3,2},{5,4},{6,5},{7,6},{9,8},{10,9},{11,10},{13,12},{... | collective-permute-start | bytes 73736 | tf_op jit(solution)/shard_map/ppermute | solution.py:126
  329.4 7.3 %collective-permute-start.28 = (f32[64,96]{1,0:T(8,128)S(1)}, f32[64,96]{1,0:T(8,128)S(1)}, u32[]{:S(2)}, u32[]{:S(2)}) collective-permute-start(f32[64,96]{1,0:T(8,128)S(1)} %get-tuple-element.101), channel_id=1, source_target_pairs={{0,4},{4,8},{8,12},{12,16},{16,20},{20,24},{24,28},{28,32},{32,36}... | collective-permute-start | bytes 73736 | tf_op jit(solution)/shard_map/ppermute | solution.py:126
  338.5 9.7 %all-to-all-start.10 = ((f32[8,1,56]{2,1,0:T(1,128)}), f32[8,1,56]{2,1,0:T(1,128)S(1)}, u32[]{:S(2)}, u32[]{:S(2)}) async-start(f32[8,1,56]{2,1,0:T(1,128)} %all_to_all.62), calls=%async_computation.10 | async-start | bytes 8192 | tf_op jit(solution)/shard_map/all_to_all | solution.py:211
  348.8 7.4 %all-to-all-start.11 = ((f32[4,1,56]{2,1,0:T(1,128)}), f32[4,1,56]{2,1,0:T(1,128)S(1)}, u32[]{:S(2)}, u32[]{:S(2)}) async-start(f32[4,1,56]{2,1,0:T(1,128)} %broadcast_in_dim.116), calls=%async_computation.11 | async-start | bytes 4096 | tf_op jit(solution)/shard_map/all_to_all | solution.py:211
  356.8 13.2 %all-to-all-start.12 = ((f32[16,1,56]{2,1,0:T(1,128)}), f32[16,1,56]{2,1,0:T(1,128)S(1)}, u32[]{:S(2)}, u32[]{:S(2)}) async-start(f32[16,1,56]{2,1,0:T(1,128)} %broadcast_in_dim.117), calls=%async_computation.12 | async-start | bytes 16384 | tf_op jit(solution)/shard_map/all_to_all | solution.py:211
  373.5 9.9 %all-to-all-start.13 = ((f32[8,1,216]{2,1,0:T(1,128)}), f32[8,1,216]{2,1,0:T(1,128)S(1)}, u32[]{:S(2)}, u32[]{:S(2)}) async-start(f32[8,1,216]{2,1,0:T(1,128)} %all_to_all.68), calls=%async_computation.13 | async-start | bytes 16384 | tf_op jit(solution)/shard_map/all_to_all | solution.py:211
  (18 other events, 155.4 us)

commit v2 on v1

v2 whole, which is shorter than its diff:
```python
import functools

import jax
import jax.numpy as jnp
from jax import lax
from jax.experimental import pallas as pl
from jax.experimental.pallas import tpu as pltpu
from jax.sharding import PartitionSpec as P

DE_SUB = 1728
LOSS_FACTOR = 0.3
LOW = 64
BF = jnp.bfloat16
F32 = jnp.float32


def params():
    return pltpu.CompilerParams(vmem_limit_bytes=24 * 1024 * 1024)


def arrange_kernel(stiff_ref, mass_ref, out_ref, order_ref):
    faces, _, run, width = stiff_ref.shape

    @pl.when(pl.program_id(0) == 0)
    def _():
        source = lax.broadcasted_iota(jnp.int32, (width, width), 0)
        target = lax.broadcasted_iota(jnp.int32, (width, width), 1)
        wanted = faces * lax.rem(target, run) + lax.div(target, run)
        order_ref[...] = jnp.where(source == wanted, 1.0, 0.0).astype(BF)

    for at, ref in enumerate((stiff_ref, mass_ref)):
        rows = ref[...].reshape(faces * run, width)
        moved = jnp.dot(rows, order_ref[...], preferred_element_type=F32)
        out_ref[0, :, at * width : (at + 1) * width] = moved.astype(BF)


def arrange(stiffness, mass_matrix, faces, n_freq):
    order, width = stiffness.shape
    run = order // (faces * n_freq)
    block = pl.BlockSpec((faces, 1, run, width), lambda d: (0, d, 0, 0))
    return pl.pallas_call(
        arrange_kernel,
        grid=(n_freq,),
        in_specs=[block, block],
        out_specs=pl.BlockSpec((1, width, 2 * width), lambda d: (d, 0, 0)),
        out_shape=jax.ShapeDtypeStruct((n_freq, width, 2 * width), BF),
        scratch_shapes=[pltpu.VMEM((width, width), BF)],
        compiler_params=params(),
        name="arrange",
    )(
        stiffness.reshape(faces, n_freq, run, width),
        mass_matrix.reshape(faces, n_freq, run, width),
    )


def apply_kernel(sign, faces, by_slot, sides, *refs):
    field_ref, pair_ref, omega_ref, odd_ref, local_ref = refs[:5]
    face_refs = refs[5:-2]
    held_ref, sems = refs[-2:]
    n_freq = pair_ref.shape[0]
    count, width = local_ref.shape
    copies = [
        pltpu.make_async_copy(pair_ref.at[d], held_ref.at[d], sems.at[d]) for d in range(n_freq)
    ]
    for copy in copies:
        copy.start()
    total_sum = None
    for d in range(n_freq):
        if by_slot:
            rows = field_ref[:, :, d * width : (d + 1) * width].reshape(count, width)
        else:
            rows = field_ref[d, :count, :]
        copies[d].wait()
        product = jnp.dot(rows, held_ref[d], preferred_element_type=F32)
        total_sum = product if total_sum is None else total_sum + product
    stiff_part = total_sum[:, :width]
    mass_part = total_sum[:, width:]
    row = lax.broadcasted_iota(jnp.int32, (count, width), 0)
    real = lax.rem(row, 8) < 4
    other = jnp.where(
        real, -pltpu.roll(stiff_part, count - 4, 0), pltpu.roll(stiff_part, 4, 0)
    )
    local = stiff_part + (sign * LOSS_FACTOR) * other - omega_ref[...] * mass_part
    local_ref[...] = local
    run = width // faces
    west, east, south, north = (local[:, f * run : (f + 1) * run] for f in range(faces))
    if sides:
        face_refs[0][...] = east
        face_refs[1][...] = north
        return
    odd_x, odd_y = odd_ref[0] == 1, odd_ref[1] == 1
    face_refs[0][...] = jnp.where(odd_x, west, east)
    face_refs[1][...] = jnp.where(odd_x, east, west)
    face_refs[2][...] = jnp.where(odd_y, south, north)
    face_refs[3][...] = jnp.where(odd_y, north, south)


def apply_local(field, pair, omega_rows, odd, sign, faces, by_slot=False, sides=False):
    n_freq, width, double = pair.shape
    count = omega_rows.shape[0]
    run = width // faces
    n_out = 2 if sides else faces
    vmem = pl.BlockSpec(memory_space=pltpu.VMEM)
    return pl.pallas_call(
        functools.partial(apply_kernel, sign, faces, by_slot, sides),
        in_specs=[
            vmem,
            pl.BlockSpec(memory_space=pltpu.HBM),
            vmem,
            pl.BlockSpec(memory_space=pltpu.SMEM),
        ],
        out_specs=[vmem] * (1 + n_out),
        out_shape=[jax.ShapeDtypeStruct((count, width), F32)]
        + [jax.ShapeDtypeStruct((count, run), F32)] * n_out,
        scratch_shapes=[
            pltpu.VMEM((n_freq, width, double), BF),
            pltpu.SemaphoreType.DMA((n_freq,)),
        ],
        compiler_params=params(),
        name="apply_local",
    )(field, pair, omega_rows, odd)


def permute(values, axis, pairs):
    return lax.ppermute(values, axis, pairs) if pairs else jnp.zeros_like(values)


def swap_faces(face_vals):
    out = []
    for axis, (near, far) in (("sx", face_vals[:2]), ("sy", face_vals[2:])):
        count = lax.axis_size(axis)
        low = [(i, i ^ 1) for i in range(count)]
        high = [(i, ((i + 1) ^ 1) - 1) for i in range(1, count - 1)]
        out += [permute(near, axis, low), permute(far, axis, high)]
    return out


def pass_faces(face_vals):
    out = []
    for axis, values in zip(("sx", "sy"), face_vals):
        pairs = [(i, i + 1) for i in range(lax.axis_size(axis) - 1)]
        out.append(permute(values, axis, pairs))
    return out


def finish_kernel(plan, faces, n_in, copies, *refs):
    combine, products, keep, send, n_halo = plan
    odd_ref, local_ref = refs[:2]
    halo = [ref[...] for ref in refs[2 : 2 + n_halo]]
    at = 2 + n_halo
    earlier = refs[at : at + n_in]
    at += n_in
    coefs_ref = weight_ref = None
    if combine:
        coefs_ref, at = refs[at], at + 1
    if products:
        weight_ref, at = refs[at], at + 1
    outs = list(refs[at:])
    if n_halo == faces:
        odd_x, odd_y = odd_ref[0] == 1, odd_ref[1] == 1
        near_x, far_x, near_y, far_y = halo
        halo = [
            jnp.where(odd_x, near_x, far_x),
            jnp.where(odd_x, far_x, near_x),
            jnp.where(odd_y, near_y, far_y),
            jnp.where(odd_y, far_y, near_y),
        ]
    else:
        none = jnp.zeros_like(halo[0])
        halo = [halo[0], none, halo[1], none]
    vector = local_ref[...] + jnp.concatenate(halo, axis=1)
    count, width = vector.shape
    known = [ref[...] for ref in earlier]
    if combine:
        vector = vector * coefs_ref[:, len(combine) : len(combine) + 1]
        for slot, which in enumerate(combine):
            vector = vector + known[which] * coefs_ref[:, slot : slot + 1]
    known.append(vector)
    if keep:
        outs.pop(0)[...] = vector
    sums = None
    if products:
        weight = jnp.broadcast_to(weight_ref[...], (8, width))
        high = -(-len(products) // 8) * 8
        place = lax.broadcasted_iota(jnp.int32, (high, count), 0)
        sums = jnp.zeros((high, count), F32)
        for slot, (left, right) in enumerate(products):
            value = lax.dot_general(
                weight,
                known[left] * known[right],
                (((1,), (1,)), ((), ())),
                precision=lax.Precision.HIGHEST,
                preferred_element_type=F32,
            )
            sums = jnp.where(place == slot, value[:1], sums)
    if send:
        sent = vector.astype(BF)
        out = outs.pop(0)
        extra = None
        if products:
            parts = []
            for _ in range(3):
                part = sums.astype(BF)
                parts.append(part.astype(F32))
                sums = sums - parts[-1]
            parts.append(jnp.zeros((sums.shape[0], width - 3 * count), F32))
            extra = jnp.concatenate(parts, axis=1).astype(BF)
        for copy in range(copies):
            out[copy, :count, :] = sent
            if extra is not None:
                out[copy, count:, :] = extra
    elif products:
        outs.pop(0)[...] = sums


def finish(
    local, halos, odd, n_freq, faces, earlier=(), combine=(), coefs=None, products=(),
    weight=None, keep=True, send=True,
):
    count, width = local.shape
    args = [odd, local, *halos, *earlier]
    if combine:
        args.append(coefs)
    if products:
        args.append(weight)
    shapes = []
    high = -(-len(products) // 8) * 8
    if keep:
        shapes.append(jax.ShapeDtypeStruct((count, width), F32))
    if send:
        shapes.append(jax.ShapeDtypeStruct((n_freq, count + high, width), BF))
    elif products:
        shapes.append(jax.ShapeDtypeStruct((high, count), F32))
    plan = (tuple(combine), tuple(products), keep, send, len(halos))
    vmem = pl.BlockSpec(memory_space=pltpu.VMEM)
    return pl.pallas_call(
        functools.partial(finish_kernel, plan, faces, len(earlier), n_freq),
        in_specs=[pl.BlockSpec(memory_space=pltpu.SMEM)] + [vmem] * (len(args) - 1),
        out_specs=[vmem] * len(shapes),
        out_shape=shapes,
        compiler_params=params(),
        name="finish",
    )(*args)


def exchange(blocks, axis):
    return lax.all_to_all(blocks, axis, 0, 0, tiled=False)


def total(values, axis):
    count = lax.axis_size(axis)
    return jnp.sum(exchange(jnp.broadcast_to(values[None], (count, *values.shape)), axis), axis=0)


def quad(entries, coefs):
    result = 0.0
    for i, left in enumerate(coefs):
        for j in range(i, len(coefs)):
            if left is None or coefs[j] is None:
                continue
            term = left * coefs[j] * entries[(i, j)]
            result = result + (term if i == j else 2.0 * term)
    return result


def combo(first, scale, second):
    out = []
    for a, b in zip(first, second):
        b = None if b is None else scale * b
        out.append(b if a is None else a if b is None else a + b)
    return out


def unit(at, one):
    return [one if i == at else None for i in range(4)]


def last_scalars(alpha0, beta0, alpha1, g, w):
    one = jnp.ones_like(alpha0)
    res0, res1, res2, lead = (unit(i, one) for i in range(4))
    dir1 = combo(res1, beta0, res0)
    gamma2 = g[(2, 2)]
    beta1 = gamma2 / g[(1, 1)]
    dir2 = combo(res2, beta1, dir1)
    alpha2 = gamma2 / quad(w, dir2)
    image = combo(lead, beta1 / alpha1, combo(res1, -1.0, res2))
    res3 = combo(res2, -alpha2, image)
    gamma3 = quad(g, res3)
    dir3 = combo(res3, gamma3 / gamma2, dir2)
    alpha3 = gamma3 / quad(w, dir3)
    answer = combo([alpha0, None, None, None], alpha1, dir1)
    answer = combo(answer, alpha2, dir2)
    answer = combo(answer, alpha3, dir3)
    return answer, gamma3


def body(stiffness, mass_matrix, omega_table, assignment, adjoint_load, forward_state, owner_index):
    n_freq = lax.axis_size("freq")
    n_sub = lax.axis_size("sx") * lax.axis_size("sy")
    slots, faces, face_len = adjoint_load.shape[2], adjoint_load.shape[4], adjoint_load.shape[5]
    order = faces * face_len
    run = face_len // n_freq
    width = faces * run
    count = n_freq * slots * 2
    own = 2 * slots
    me = lax.axis_index("freq")

    load = jnp.swapaxes(adjoint_load[0, 0].astype(BF), 0, 1).reshape(own, faces, n_freq, run)
    load = jnp.swapaxes(load, 1, 2).reshape(own, order)
    tags = jnp.broadcast_to(assignment.astype(BF)[None, :], (2, slots)).reshape(own, 1)
    packet = jnp.concatenate([load, jnp.broadcast_to(tags, (own, 128))], axis=1)
    field = exchange(jnp.broadcast_to(packet[None], (n_freq, *packet.shape)), "freq")
    pair = arrange(stiffness[0, 0], mass_matrix[0, 0], faces, n_freq)
    slot_tags = field[:, :, order].reshape(count).astype(jnp.int32)
    matches = slot_tags[:, None] == jnp.arange(omega_table.shape[0], dtype=jnp.int32)[None, :]
    omega_rows = jnp.sum(jnp.where(matches, omega_table[None, :], 0.0), axis=1, keepdims=True)

    def inside(axis, at):
        return jnp.where(lax.axis_index(axis) == at, 1.0, 0.5).astype(F32)

    face_weight = jnp.stack(
        [
            inside("sx", 0),
            inside("sx", lax.axis_size("sx") - 1),
            inside("sy", 0),
            inside("sy", lax.axis_size("sy") - 1),
        ]
    )
    weight = jnp.repeat(face_weight, run)[None, :]
    once = jnp.where(face_weight < 1.0, jnp.array([1.0, 0.0, 1.0, 0.0], F32), 1.0)
    weight_once = jnp.repeat(once, run)[None, :]

    odd = jnp.stack([lax.rem(lax.axis_index(axis), 2) for axis in ("sx", "sy")]).astype(jnp.int32)

    def step(field, sign, by_slot=False, **how):
        local, *face_vals = apply_local(field, pair, omega_rows, odd, sign, faces, by_slot)
        return finish(local, swap_faces(face_vals), odd, n_freq, faces, **how)

    def by_slots(sums, n_products):
        return jnp.sum(sums[:n_products].reshape(n_products, n_freq, 2, slots), axis=2)

    def spread(sent, n_products):
        sums = sum(
            jnp.sum(sent[:, count:, k * count : (k + 1) * count].astype(F32), axis=0)
            for k in range(3)
        )
        sums = by_slots(sums, n_products)
        flat = total(total(sums.reshape(-1), "sy"), "sx")
        return flat.reshape(n_products, n_freq, slots)

    def to_rows(values):
        wide = jnp.stack(values, axis=-1)[:, None]
        return jnp.broadcast_to(wide, (n_freq, 2, slots, len(values))).reshape(count, len(values))

    u0, send = step(field, -1.0, by_slot=True)
    sent0 = exchange(send, "freq")
    w0, send = step(sent0, 1.0, earlier=(u0,), products=((0, 0), (1, 1)), weight=weight)
    sent = exchange(send, "freq")
    gamma0, delta0 = spread(sent, 2)
    alpha0 = gamma0 / delta0
    coefs = to_rows([jnp.ones_like(alpha0), -alpha0])
    u1, send = step(sent, -1.0, earlier=(u0,), combine=(0,), coefs=coefs)
    sent1 = exchange(send, "freq")
    w1, send = step(
        sent1, 1.0, earlier=(u1, w0), products=((0, 0), (1, 2), (2, 2)), weight=weight
    )
    sent = exchange(send, "freq")
    gamma1, cross, image1 = spread(sent, 3)
    beta0 = gamma1 / gamma0
    alpha1 = gamma1 / (image1 + beta0 * (2.0 * cross + beta0 * delta0))
    ratio = alpha1 * beta0 / alpha0
    coefs = to_rows([-ratio, 1.0 + ratio, -alpha1])
    u2, send = step(sent, -1.0, earlier=(u0, u1), combine=(0, 1), coefs=coefs)
    sent2 = exchange(send, "freq")
    w2, send = step(sent2, 1.0)
    u3, send = step(exchange(send, "freq"), -1.0)
    sent3 = exchange(send, "freq")
    local, *face_vals = apply_local(sent3, pair, omega_rows, odd, 1.0, faces, sides=True)
    later_g = ((1, 2), (2, 2), (1, 3), (2, 3), (3, 3))
    later_w = ((0, 2), (1, 2), (2, 2), (0, 3), (1, 3), (2, 3), (3, 3))
    products = tuple((i - 1, j - 1) for i, j in later_g) + tuple((3 + i, 3 + j) for i, j in later_w)
    (sums,) = finish(
        local, pass_faces(face_vals), odd, n_freq, faces, earlier=(u1, u2, u3, w0, w1, w2),
        products=products, weight=weight_once, keep=False, send=False,
    )
    sums = by_slots(sums, len(products))
    sums = jnp.swapaxes(sums, 0, 1).reshape(n_freq, len(products) * slots)
    ours = jnp.sum(exchange(sums, "freq"), axis=0)
    ours = total(total(ours, "sy"), "sx").reshape(len(products), slots)
    earlier = jnp.stack([alpha0, beta0, alpha1, gamma1, delta0, cross, image1])
    mine = lax.dynamic_index_in_dim(earlier, me, 1, keepdims=False)
    g = {(1, 1): mine[3]}
    w = {(0, 0): mine[4], (0, 1): mine[5], (1, 1): mine[6]}
    for at, key in enumerate(later_g):
        g[key] = ours[at]
    for at, key in enumerate(later_w):
        w[key] = ours[len(later_g) + at]
    answer, gamma = last_scalars(mine[0], mine[1], mine[2], g, w)
    residual_level = jnp.log(gamma / float(n_sub * 2 * order))

    adjoint = 0.0
    for values, sent in zip(answer, (sent0, sent1, sent2, sent3)):
        block = lax.dynamic_slice_in_dim(sent, me * own, own, axis=1)[:, :, :width].astype(F32)
        adjoint = adjoint + block * jnp.tile(values, 2)[None, :, None]
    adjoint = adjoint.reshape(n_freq, 2, slots, faces, run)
    adjoint = jnp.transpose(adjoint, (2, 1, 3, 0, 4)).reshape(slots, 2, faces, face_len)

    state = forward_state[0, 0].astype(F32)
    adj_real, adj_imag = adjoint[:, 0], adjoint[:, 1]
    state_real, state_imag = state[:, 0], state[:, 1]
    term = (
        adj_real * state_real
        - adj_imag * state_imag
        - LOSS_FACTOR * (adj_real * state_imag + adj_imag * state_real)
    )
    dof_total = jnp.sum(term, axis=0).reshape(1, order)
    owner = owner_index[0, 0].reshape(1, order)
    high = jnp.arange(DE_SUB // LOW, dtype=jnp.int32)[:, None]
    low = jnp.arange(LOW, dtype=jnp.int32)[:, None]
    spread = jnp.where(lax.div(owner, LOW) == high, dof_total, 0.0)
    places = jnp.where(lax.rem(owner, LOW) == low, 1.0, 0.0)
    partial_grad = lax.dot_general(
        spread, places, (((1,), (1,)), ((), ())), precision=lax.Precision.HIGHEST
    )
    grad_factor = (DE_SUB / (slots * n_freq * order)) ** 0.5
    partial_grad = (-grad_factor * partial_grad).reshape(n_freq, DE_SUB // n_freq)
    gradient = jnp.sum(exchange(partial_grad, "freq"), axis=0)
    return (adjoint[None, None], gradient[None, None], residual_level)


def solution(mesh):
    return jax.shard_map(
        body,
        mesh=mesh,
        in_specs=(
            P("sx", "sy", None, "freq"),
            P("sx", "sy", None, "freq"),
            P(),
            P("freq"),
            P("sx", "sy", "freq", None, None, None),
            P("sx", "sy", "freq", None, None, None),
            P("sx", "sy", None, None),
        ),
        out_specs=(P("sx", "sy", "freq", None, None, None), P("sx", "sy", "freq"), P("freq")),
        check_vma=False,
    )
```

time: 386 us -> 384 us (level)
  blocking collectives: 140 us -> 96.8 us
  starting transfers between devices: 117 us -> 150 us
  waiting for transfers between devices: 71.9 us -> 59.3 us
  Pallas kernels: 26.6 us -> 39.1 us
  local copies, waits for them, and re-layouts: 23 us -> 30.6 us
    all_to_all x7, blocking collectives: 140 us -> 96.8 us  [exchange(): return lax.all_to_all(blocks, axis, 0, 0, tiled=False)]
    all_to_all x7 -> x9, starting transfers between devices: 37.8 us -> 55.6 us  [exchange(): return lax.all_to_all(blocks, axis, 0, 0, tiled=False)]
    ppermute x30, waiting for transfers between devices: 22.8 us -> 6.48 us  [permute(): lax.ppermute(values, axis, pairs)]
    ppermute x30, starting transfers between devices: 79.1 us -> 94 us  [permute(): lax.ppermute(values, axis, pairs)]
    pallas_call x16, Pallas kernels: 21.7 us -> 34.2 us  [the longest x8 25.4 us: apply_local(): pl.pallas_call(functools.partial(apply_kernel, sign, faces, by_slot, side...]
    unnamed x32 -> x34, local copies, waits for them, and re-layouts: 15.4 us -> 22 us
    all_to_all x7 -> x9, waiting for transfers between devices: 49.1 us -> 52.8 us  [exchange(): return lax.all_to_all(blocks, axis, 0, 0, tiled=False)]
  transfers between devices with their start and end apart: 37 -> 39, of which waited for: 14 -> 15; matrix products, arithmetic and copies ran while one was open for 1% -> 1% of each run, Pallas kernels for 2% -> 3%
where the time goes in v2:
time: 384 us; the launch traced here: 382 us
  starting transfers between devices  150 us (39%)
  blocking collectives  96.8 us (25%)
  waiting for transfers between devices  59.3 us (15%)
  Pallas kernels  39.1 us (10%)
  local copies, waits for them, and re-layouts  30.6 us (8%)
  other arithmetic  4.18 us (1%)
    all_to_all x7, blocking collectives, exchange(): return lax.all_to_all(blocks, axis, 0, 0, tiled=False)  96.8 us
    ppermute x30, starting transfers between devices, permute(): lax.ppermute(values, axis, pairs)  94 us
    all_to_all x9, starting transfers between devices, exchange(): return lax.all_to_all(blocks, axis, 0, 0, tiled=False)  55.6 us
    all_to_all x9, waiting for transfers between devices, exchange(): return lax.all_to_all(blocks, axis, 0, 0, tiled=False)  52.8 us
    pallas_call x8, Pallas kernels, apply_local(): pl.pallas_call(functools.partial(apply_kernel, sign, faces, by_slot, side...  25.4 us
    unnamed x34, local copies, waits for them, and re-layouts  22 us
    pallas_call x8, Pallas kernels, finish(): pl.pallas_call(functools.partial(finish_kernel, plan, faces, len(earlier)...  8.82 us
  transfers between devices with their start and end apart: 39, of which 15 were waited for; matrix products, arithmetic and copies ran while one was open for 1% of the time, Pallas kernels for 3%

profile of v2, /device:TPU:1, one launch (start us, length us, event | category | flops | bytes accessed | tf_op | source)
XLA Modules:
  0.0 381.8 jit_solution(10849103407138013734)
XLA Ops:
  3.5 10.9 %all-to-all-start = ((bf16[8,8,3200]{2,1,0:T(8,128)(2,1)}), bf16[8,8,3200]{2,1,0:T(8,128)(2,1)S(1)}, u32[]{:S(2)}, u32[]{:S(2)}) async-start(bf16[8,8,3200]{2,1,0:T(8,128)(2,1)} %broadcast_in_dim.125), calls=%async_computation | async-start | bytes 819200 | tf_op jit(solution)/shard_map/all_to_all | solution.py:247
  17.7 4.9 %arrange.1.refs_1_ = bf16[8,384,768]{2,1,0:T(8,128)(2,1)S(1)} custom-call(bf16[4,8,96,384]{3,2,1,0:T(8,128)(2,1)S(1)} %bitcast.76, bf16[4,8,96,384]{3,2,1,0:T(8,128)(2,1)S(1)} %bitcast.77), custom_call_target="tpu_custom_call" | custom-call | tf_op jit(solution)/shard_map/arrange/pallas_call | solution.py:41
  24.8 4.2 %all-to-all-done.refs_0_ = bf16[8,8,3200]{2,1,0:T(8,128)(2,1)S(1)} async-done(((bf16[8,8,3200]{2,1,0:T(8,128)(2,1)}), bf16[8,8,3200]{2,1,0:T(8,128)(2,1)S(1)}, u32[]{:S(2)}, u32[]{:S(2)}) %all-to-all-start) | async-done | bytes 409632 | tf_op jit(solution)/shard_map/all_to_all | solution.py:247
  47.5 3.5 all-to-all-start.1
  50.9 14.2 %all-to-all-done.1.refs_0_ = bf16[8,64,384]{2,1,0:T(8,128)(2,1)S(1)} async-done(((bf16[8,64,384]{2,1,0:T(8,128)(2,1)}), bf16[8,64,384]{2,1,0:T(8,128)(2,1)S(1)}, u32[]{:S(2)}, u32[]{:S(2)}) %all-to-all-start.1) | async-done | bytes 393248 | tf_op jit(solution)/shard_map/all_to_all | solution.py:247
  72.9 4.4 %collective-permute-start.5 = (f32[64,96]{1,0:T(8,128)S(1)}, f32[64,96]{1,0:T(8,128)S(1)}, u32[]{:S(2)}, u32[]{:S(2)}) collective-permute-start(f32[64,96]{1,0:T(8,128)S(1)} %get-tuple-element.63), channel_id=1, source_target_pairs={{4,8},{8,4},{12,16},{16,12},{20,24},{24,20},{28,32},{32,28},{36,40... | collective-permute-start | bytes 73736 | tf_op jit(solution)/shard_map/ppermute | solution.py:125
  77.4 5.7 %collective-permute-start.6 = (f32[64,96]{1,0:T(8,128)S(1)}, f32[64,96]{1,0:T(8,128)S(1)}, u32[]{:S(2)}, u32[]{:S(2)}) collective-permute-start(f32[64,96]{1,0:T(8,128)S(1)} %get-tuple-element.64), channel_id=1, source_target_pairs={{0,1},{1,0},{2,3},{3,2},{4,5},{5,4},{6,7},{7,6},{8,9},{9,8},{10,11... | collective-permute-start | bytes 73736 | tf_op jit(solution)/shard_map/ppermute | solution.py:125
  85.4 16.1 %all_to_all.95.refs_0_ = bf16[8,72,384]{2,1,0:T(8,128)(2,1)S(1)} all-to-all(bf16[8,72,384]{2,1,0:T(8,128)(2,1)S(1)} %get-tuple-element.67), channel_id=1, replica_groups=mesh['freq'=8,'sx'=16,'sy'=4] {'freq'}, dimensions={0} | all-to-all | bytes 884736 | tf_op jit(solution)/shard_map/all_to_all | solution.py:247
  101.8 11.0 %all_to_all.96 = f32[4,1,64]{2,1,0:T(1,128)S(1)} all-to-all(f32[4,1,64]{2,1,0:T(1,128)S(1)} %broadcast_in_dim.131), channel_id=1, replica_groups=mesh['freq'=8,'sx'=16,'sy'=4] {'sy'}, dimensions={0} | all-to-all | bytes 2048 | tf_op jit(solution)/shard_map/all_to_all | solution.py:247
  113.5 8.9 %all-to-all-start.4 = ((f32[16,1,64]{2,1,0:T(1,128)}), f32[16,1,64]{2,1,0:T(1,128)S(1)}, u32[]{:S(2)}, u32[]{:S(2)}) async-start(f32[16,1,64]{2,1,0:T(1,128)} %broadcast_in_dim.132), calls=%async_computation.4 | async-start | bytes 16384 | tf_op jit(solution)/shard_map/all_to_all | solution.py:247
  139.0 13.9 %all_to_all.97.refs_0_ = bf16[8,64,384]{2,1,0:T(8,128)(2,1)S(1)} all-to-all(bf16[8,64,384]{2,1,0:T(8,128)(2,1)S(1)} %get-tuple-element.73), channel_id=1, replica_groups=mesh['freq'=8,'sx'=16,'sy'=4] {'freq'}, dimensions={0} | all-to-all | bytes 786432 | tf_op jit(solution)/shard_map/all_to_all | solution.py:247
  160.4 7.6 %collective-permute-start.13 = (f32[64,96]{1,0:T(8,128)S(1)}, f32[64,96]{1,0:T(8,128)S(1)}, u32[]{:S(2)}, u32[]{:S(2)}) collective-permute-start(f32[64,96]{1,0:T(8,128)S(1)} %get-tuple-element.76), channel_id=1, source_target_pairs={{4,8},{8,4},{12,16},{16,12},{20,24},{24,20},{28,32},{32,28},{36,40... | collective-permute-start | bytes 73736 | tf_op jit(solution)/shard_map/ppermute | solution.py:125
  168.0 4.9 %collective-permute-start.14 = (f32[64,96]{1,0:T(8,128)S(1)}, f32[64,96]{1,0:T(8,128)S(1)}, u32[]{:S(2)}, u32[]{:S(2)}) collective-permute-start(f32[64,96]{1,0:T(8,128)S(1)} %get-tuple-element.77), channel_id=1, source_target_pairs={{0,1},{1,0},{2,3},{3,2},{4,5},{5,4},{6,7},{7,6},{8,9},{9,8},{10,11... | collective-permute-start | bytes 73736 | tf_op jit(solution)/shard_map/ppermute | solution.py:125
  175.3 13.7 %all_to_all.98.refs_0_ = bf16[8,72,384]{2,1,0:T(8,128)(2,1)S(1)} all-to-all(bf16[8,72,384]{2,1,0:T(8,128)(2,1)S(1)} %get-tuple-element.81), channel_id=1, replica_groups=mesh['freq'=8,'sx'=16,'sy'=4] {'freq'}, dimensions={0} | all-to-all | bytes 884736 | tf_op jit(solution)/shard_map/all_to_all | solution.py:247
  189.3 10.1 %all_to_all.99 = f32[4,1,96]{2,1,0:T(1,128)S(1)} all-to-all(f32[4,1,96]{2,1,0:T(1,128)S(1)} %broadcast_in_dim.135), channel_id=1, replica_groups=mesh['freq'=8,'sx'=16,'sy'=4] {'sy'}, dimensions={0} | all-to-all | bytes 3072 | tf_op jit(solution)/shard_map/all_to_all | solution.py:247
  200.0 12.7 %all-to-all-start.8 = ((f32[16,1,96]{2,1,0:T(1,128)}), f32[16,1,96]{2,1,0:T(1,128)S(1)}, u32[]{:S(2)}, u32[]{:S(2)}) async-start(f32[16,1,96]{2,1,0:T(1,128)} %broadcast_in_dim.136), calls=%async_computation.8 | async-start | bytes 16384 | tf_op jit(solution)/shard_map/all_to_all | solution.py:247
  220.2 3.6 collective-permute-start.17
  229.2 16.5 %all_to_all.100.refs_0_ = bf16[8,64,384]{2,1,0:T(8,128)(2,1)S(1)} all-to-all(bf16[8,64,384]{2,1,0:T(8,128)(2,1)S(1)} %get-tuple-element.87), channel_id=1, replica_groups=mesh['freq'=8,'sx'=16,'sy'=4] {'freq'}, dimensions={0} | all-to-all | bytes 786432 | tf_op jit(solution)/shard_map/all_to_all | solution.py:247
  253.1 4.5 %collective-permute-start.21 = (f32[64,96]{1,0:T(8,128)S(1)}, f32[64,96]{1,0:T(8,128)S(1)}, u32[]{:S(2)}, u32[]{:S(2)}) collective-permute-start(f32[64,96]{1,0:T(8,128)S(1)} %get-tuple-element.90), channel_id=1, source_target_pairs={{4,8},{8,4},{12,16},{16,12},{20,24},{24,20},{28,32},{32,28},{36,40... | collective-permute-start | bytes 73736 | tf_op jit(solution)/shard_map/ppermute | solution.py:125
  257.7 5.5 %collective-permute-start.22 = (f32[64,96]{1,0:T(8,128)S(1)}, f32[64,96]{1,0:T(8,128)S(1)}, u32[]{:S(2)}, u32[]{:S(2)}) collective-permute-start(f32[64,96]{1,0:T(8,128)S(1)} %get-tuple-element.91), channel_id=1, source_target_pairs={{0,1},{1,0},{2,3},{3,2},{4,5},{5,4},{6,7},{7,6},{8,9},{9,8},{10,11... | collective-permute-start | bytes 73736 | tf_op jit(solution)/shard_map/ppermute | solution.py:125
  265.1 15.5 %all_to_all.101.refs_0_ = bf16[8,64,384]{2,1,0:T(8,128)(2,1)S(1)} all-to-all(bf16[8,64,384]{2,1,0:T(8,128)(2,1)S(1)} %get-tuple-element.93), channel_id=1, replica_groups=mesh['freq'=8,'sx'=16,'sy'=4] {'freq'}, dimensions={0} | all-to-all | bytes 786432 | tf_op jit(solution)/shard_map/all_to_all | solution.py:247
  285.8 5.8 %collective-permute-start.25 = (f32[64,96]{1,0:T(8,128)S(1)}, f32[64,96]{1,0:T(8,128)S(1)}, u32[]{:S(2)}, u32[]{:S(2)}) collective-permute-start(f32[64,96]{1,0:T(8,128)S(1)} %get-tuple-element.96), channel_id=1, source_target_pairs={{4,8},{8,4},{12,16},{16,12},{20,24},{24,20},{28,32},{32,28},{36,40... | collective-permute-start | bytes 73736 | tf_op jit(solution)/shard_map/ppermute | solution.py:125
  291.6 5.3 %collective-permute-start.26 = (f32[64,96]{1,0:T(8,128)S(1)}, f32[64,96]{1,0:T(8,128)S(1)}, u32[]{:S(2)}, u32[]{:S(2)}) collective-permute-start(f32[64,96]{1,0:T(8,128)S(1)} %get-tuple-element.97), channel_id=1, source_target_pairs={{0,1},{1,0},{2,3},{3,2},{4,5},{5,4},{6,7},{7,6},{8,9},{9,8},{10,11... | collective-permute-start | bytes 73736 | tf_op jit(solution)/shard_map/ppermute | solution.py:125
  303.6 11.2 %all-to-all-done.11.refs_0_ = bf16[8,64,384]{2,1,0:T(8,128)(2,1)S(1)} async-done(((bf16[8,64,384]{2,1,0:T(8,128)(2,1)}), bf16[8,64,384]{2,1,0:T(8,128)(2,1)S(1)}, u32[]{:S(2)}, u32[]{:S(2)}) %all-to-all-start.11) | async-done | bytes 393248 | tf_op jit(solution)/shard_map/all_to_all | solution.py:247
  320.3 6.9 %collective-permute-start.28 = (f32[64,96]{1,0:T(8,128)S(1)}, f32[64,96]{1,0:T(8,128)S(1)}, u32[]{:S(2)}, u32[]{:S(2)}) collective-permute-start(f32[64,96]{1,0:T(8,128)S(1)} %get-tuple-element.101), channel_id=1, source_target_pairs={{0,4},{4,8},{8,12},{12,16},{16,20},{20,24},{24,28},{28,32},{32,36}... | collective-permute-start | bytes 73736 | tf_op jit(solution)/shard_map/ppermute | solution.py:125
  327.2 5.6 %collective-permute-start.29 = (f32[64,96]{1,0:T(8,128)S(1)}, f32[64,96]{1,0:T(8,128)S(1)}, u32[]{:S(2)}, u32[]{:S(2)}) collective-permute-start(f32[64,96]{1,0:T(8,128)S(1)} %get-tuple-element.102), channel_id=1, source_target_pairs={{0,1},{1,2},{2,3},{4,5},{5,6},{6,7},{8,9},{9,10},{10,11},{12,13},{... | collective-permute-start | bytes 73736 | tf_op jit(solution)/shard_map/ppermute | solution.py:125
  339.9 6.4 %all-to-all-done.12 = f32[8,1,48]{2,1,0:T(1,128)S(1)} async-done(((f32[8,1,48]{2,1,0:T(1,128)}), f32[8,1,48]{2,1,0:T(1,128)S(1)}, u32[]{:S(2)}, u32[]{:S(2)}) %all-to-all-start.12) | async-done | bytes 1568 | tf_op jit(solution)/shard_map/all_to_all | solution.py:247
  346.9 3.6 all-to-all-start.13
  350.5 4.1 %all-to-all-done.13 = f32[4,1,48]{2,1,0:T(1,128)S(1)} async-done(((f32[4,1,48]{2,1,0:T(1,128)}), f32[4,1,48]{2,1,0:T(1,128)S(1)}, u32[]{:S(2)}, u32[]{:S(2)}) %all-to-all-start.13) | async-done | bytes 800 | tf_op jit(solution)/shard_map/all_to_all | solution.py:247
  355.2 6.0 %all-to-all-start.14 = ((f32[16,1,48]{2,1,0:T(1,128)}), f32[16,1,48]{2,1,0:T(1,128)S(1)}, u32[]{:S(2)}, u32[]{:S(2)}) async-start(f32[16,1,48]{2,1,0:T(1,128)} %broadcast_in_dim.140), calls=%async_computation.14 | async-start | bytes 16384 | tf_op jit(solution)/shard_map/all_to_all | solution.py:247
  361.2 7.0 %all-to-all-done.14 = f32[16,1,48]{2,1,0:T(1,128)S(1)} async-done(((f32[16,1,48]{2,1,0:T(1,128)}), f32[16,1,48]{2,1,0:T(1,128)S(1)}, u32[]{:S(2)}, u32[]{:S(2)}) %all-to-all-start.14) | async-done | bytes 3104 | tf_op jit(solution)/shard_map/all_to_all | solution.py:247
  375.5 5.8 %all-to-all-done.15 = f32[8,1,216]{2,1,0:T(1,128)S(1)} async-done(((f32[8,1,216]{2,1,0:T(1,128)}), f32[8,1,216]{2,1,0:T(1,128)S(1)}, u32[]{:S(2)}, u32[]{:S(2)}) %all-to-all-start.15) | async-done | bytes 6944 | tf_op jit(solution)/shard_map/all_to_all | solution.py:247
  (202 shorter events, 120.6 us)
Async XLA Ops:
  3.5 25.5 %all-to-all-start = ((bf16[8,8,3200]{2,1,0:T(8,128)(2,1)}), bf16[8,8,3200]{2,1,0:T(8,128)(2,1)S(1)}, u32[]{:S(2)}, u32[]{:S(2)}) async-start(bf16[8,8,3200]{2,1,0:T(8,128)(2,1)} %broadcast_in_dim.125), calls=%async_computation | async-start | bytes 819200 | tf_op jit(solution)/shard_map/all_to_all | solution.py:247
  35.0 10.1 %collective-permute-start = (f32[64,96]{1,0:T(8,128)S(1)}, f32[64,96]{1,0:T(8,128)S(1)}, u32[]{:S(2)}, u32[]{:S(2)}) collective-permute-start(f32[64,96]{1,0:T(8,128)S(1)} %get-tuple-element.56), channel_id=1, source_target_pairs={{0,4},{4,0},{8,12},{12,8},{16,20},{20,16},{24,28},{28,24},{32,36},... | collective-permute-start | bytes 73736 | tf_op jit(solution)/shard_map/ppermute | solution.py:125
  38.3 6.9 %collective-permute-start.1 = (f32[64,96]{1,0:T(8,128)S(1)}, f32[64,96]{1,0:T(8,128)S(1)}, u32[]{:S(2)}, u32[]{:S(2)}) collective-permute-start(f32[64,96]{1,0:T(8,128)S(1)} %get-tuple-element.57), channel_id=1, source_target_pairs={{4,8},{8,4},{12,16},{16,12},{20,24},{24,20},{28,32},{32,28},{36,40... | collective-permute-start | bytes 73736 | tf_op jit(solution)/shard_map/ppermute | solution.py:125
  41.4 4.7 %collective-permute-start.2 = (f32[64,96]{1,0:T(8,128)S(1)}, f32[64,96]{1,0:T(8,128)S(1)}, u32[]{:S(2)}, u32[]{:S(2)}) collective-permute-start(f32[64,96]{1,0:T(8,128)S(1)} %get-tuple-element.58), channel_id=1, source_target_pairs={{0,1},{1,0},{2,3},{3,2},{4,5},{5,4},{6,7},{7,6},{8,9},{9,8},{10,11... | collective-permute-start | bytes 73736 | tf_op jit(solution)/shard_map/ppermute | solution.py:125
  47.5 17.6 %all-to-all-start.1 = ((bf16[8,64,384]{2,1,0:T(8,128)(2,1)}), bf16[8,64,384]{2,1,0:T(8,128)(2,1)S(1)}, u32[]{:S(2)}, u32[]{:S(2)}) async-start(bf16[8,64,384]{2,1,0:T(8,128)(2,1)} %get-tuple-element.60), calls=%async_computation.1 | async-start | bytes 786432 | tf_op jit(solution)/shard_map/all_to_all | solution.py:247
  70.6 13.4 %collective-permute-start.4 = (f32[64,96]{1,0:T(8,128)S(1)}, f32[64,96]{1,0:T(8,128)S(1)}, u32[]{:S(2)}, u32[]{:S(2)}) collective-permute-start(f32[64,96]{1,0:T(8,128)S(1)} %get-tuple-element.62), channel_id=1, source_target_pairs={{0,4},{4,0},{8,12},{12,8},{16,20},{20,16},{24,28},{28,24},{32,36},... | collective-permute-start | bytes 73736 | tf_op jit(solution)/shard_map/ppermute | solution.py:125
  72.9 11.1 %collective-permute-start.5 = (f32[64,96]{1,0:T(8,128)S(1)}, f32[64,96]{1,0:T(8,128)S(1)}, u32[]{:S(2)}, u32[]{:S(2)}) collective-permute-start(f32[64,96]{1,0:T(8,128)S(1)} %get-tuple-element.63), channel_id=1, source_target_pairs={{4,8},{8,4},{12,16},{16,12},{20,24},{24,20},{28,32},{32,28},{36,40... | collective-permute-start | bytes 73736 | tf_op jit(solution)/shard_map/ppermute | solution.py:125
  77.4 7.0 %collective-permute-start.6 = (f32[64,96]{1,0:T(8,128)S(1)}, f32[64,96]{1,0:T(8,128)S(1)}, u32[]{:S(2)}, u32[]{:S(2)}) collective-permute-start(f32[64,96]{1,0:T(8,128)S(1)} %get-tuple-element.64), channel_id=1, source_target_pairs={{0,1},{1,0},{2,3},{3,2},{4,5},{5,4},{6,7},{7,6},{8,9},{9,8},{10,11... | collective-permute-start | bytes 73736 | tf_op jit(solution)/shard_map/ppermute | solution.py:125
  113.5 23.1 %all-to-all-start.4 = ((f32[16,1,64]{2,1,0:T(1,128)}), f32[16,1,64]{2,1,0:T(1,128)S(1)}, u32[]{:S(2)}, u32[]{:S(2)}) async-start(f32[16,1,64]{2,1,0:T(1,128)} %broadcast_in_dim.132), calls=%async_computation.4 | async-start | bytes 16384 | tf_op jit(solution)/shard_map/all_to_all | solution.py:247
  127.9 9.1 %collective-permute-start.10 = (f32[64,96]{1,0:T(8,128)S(1)}, f32[64,96]{1,0:T(8,128)S(1)}, u32[]{:S(2)}, u32[]{:S(2)}) collective-permute-start(f32[64,96]{1,0:T(8,128)S(1)} %get-tuple-element.71), channel_id=1, source_target_pairs={{0,1},{1,0},{2,3},{3,2},{4,5},{5,4},{6,7},{7,6},{8,9},{9,8},{10,11... | collective-permute-start | bytes 73736 | tf_op jit(solution)/shard_map/ppermute | solution.py:125
  130.1 6.9 %collective-permute-start.11 = (f32[64,96]{1,0:T(8,128)S(1)}, f32[64,96]{1,0:T(8,128)S(1)}, u32[]{:S(2)}, u32[]{:S(2)}) collective-permute-start(f32[64,96]{1,0:T(8,128)S(1)} %get-tuple-element.72), channel_id=1, source_target_pairs={{1,2},{2,1},{5,6},{6,5},{9,10},{10,9},{13,14},{14,13},{17,18},{18,... | collective-permute-start | bytes 73736 | tf_op jit(solution)/shard_map/ppermute | solution.py:125
  130.8 6.3 %collective-permute-start.8 = (f32[64,96]{1,0:T(8,128)S(1)}, f32[64,96]{1,0:T(8,128)S(1)}, u32[]{:S(2)}, u32[]{:S(2)}) collective-permute-start(f32[64,96]{1,0:T(8,128)S(1)} %get-tuple-element.69), channel_id=1, source_target_pairs={{0,4},{4,0},{8,12},{12,8},{16,20},{20,16},{24,28},{28,24},{32,36},... | collective-permute-start | bytes 73736 | tf_op jit(solution)/shard_map/ppermute | solution.py:125
  133.1 5.2 %collective-permute-start.9 = (f32[64,96]{1,0:T(8,128)S(1)}, f32[64,96]{1,0:T(8,128)S(1)}, u32[]{:S(2)}, u32[]{:S(2)}) collective-permute-start(f32[64,96]{1,0:T(8,128)S(1)} %get-tuple-element.70), channel_id=1, source_target_pairs={{4,8},{8,4},{12,16},{16,12},{20,24},{24,20},{28,32},{32,28},{36,40... | collective-permute-start | bytes 73736 | tf_op jit(solution)/shard_map/ppermute | solution.py:125
  158.5 15.1 %collective-permute-start.12 = (f32[64,96]{1,0:T(8,128)S(1)}, f32[64,96]{1,0:T(8,128)S(1)}, u32[]{:S(2)}, u32[]{:S(2)}) collective-permute-start(f32[64,96]{1,0:T(8,128)S(1)} %get-tuple-element.75), channel_id=1, source_target_pairs={{0,4},{4,0},{8,12},{12,8},{16,20},{20,16},{24,28},{28,24},{32,36},... | collective-permute-start | bytes 73736 | tf_op jit(solution)/shard_map/ppermute | solution.py:125
  160.4 13.2 %collective-permute-start.13 = (f32[64,96]{1,0:T(8,128)S(1)}, f32[64,96]{1,0:T(8,128)S(1)}, u32[]{:S(2)}, u32[]{:S(2)}) collective-permute-start(f32[64,96]{1,0:T(8,128)S(1)} %get-tuple-element.76), channel_id=1, source_target_pairs={{4,8},{8,4},{12,16},{16,12},{20,24},{24,20},{28,32},{32,28},{36,40... | collective-permute-start | bytes 73736 | tf_op jit(solution)/shard_map/ppermute | solution.py:125
  168.0 6.2 %collective-permute-start.14 = (f32[64,96]{1,0:T(8,128)S(1)}, f32[64,96]{1,0:T(8,128)S(1)}, u32[]{:S(2)}, u32[]{:S(2)}) collective-permute-start(f32[64,96]{1,0:T(8,128)S(1)} %get-tuple-element.77), channel_id=1, source_target_pairs={{0,1},{1,0},{2,3},{3,2},{4,5},{5,4},{6,7},{7,6},{8,9},{9,8},{10,11... | collective-permute-start | bytes 73736 | tf_op jit(solution)/shard_map/ppermute | solution.py:125
  200.0 26.7 %all-to-all-start.8 = ((f32[16,1,96]{2,1,0:T(1,128)}), f32[16,1,96]{2,1,0:T(1,128)S(1)}, u32[]{:S(2)}, u32[]{:S(2)}) async-start(f32[16,1,96]{2,1,0:T(1,128)} %broadcast_in_dim.136), calls=%async_computation.8 | async-start | bytes 16384 | tf_op jit(solution)/shard_map/all_to_all | solution.py:247
  218.2 9.0 %collective-permute-start.16 = (f32[64,96]{1,0:T(8,128)S(1)}, f32[64,96]{1,0:T(8,128)S(1)}, u32[]{:S(2)}, u32[]{:S(2)}) collective-permute-start(f32[64,96]{1,0:T(8,128)S(1)} %get-tuple-element.83), channel_id=1, source_target_pairs={{0,4},{4,0},{8,12},{12,8},{16,20},{20,16},{24,28},{28,24},{32,36},... | collective-permute-start | bytes 73736 | tf_op jit(solution)/shard_map/ppermute | solution.py:125
  220.2 7.0 %collective-permute-start.17 = (f32[64,96]{1,0:T(8,128)S(1)}, f32[64,96]{1,0:T(8,128)S(1)}, u32[]{:S(2)}, u32[]{:S(2)}) collective-permute-start(f32[64,96]{1,0:T(8,128)S(1)} %get-tuple-element.84), channel_id=1, source_target_pairs={{4,8},{8,4},{12,16},{16,12},{20,24},{24,20},{28,32},{32,28},{36,40... | collective-permute-start | bytes 73736 | tf_op jit(solution)/shard_map/ppermute | solution.py:125
  251.2 12.6 %collective-permute-start.20 = (f32[64,96]{1,0:T(8,128)S(1)}, f32[64,96]{1,0:T(8,128)S(1)}, u32[]{:S(2)}, u32[]{:S(2)}) collective-permute-start(f32[64,96]{1,0:T(8,128)S(1)} %get-tuple-element.89), channel_id=1, source_target_pairs={{0,4},{4,0},{8,12},{12,8},{16,20},{20,16},{24,28},{28,24},{32,36},... | collective-permute-start | bytes 73736 | tf_op jit(solution)/shard_map/ppermute | solution.py:125
  253.1 10.7 %collective-permute-start.21 = (f32[64,96]{1,0:T(8,128)S(1)}, f32[64,96]{1,0:T(8,128)S(1)}, u32[]{:S(2)}, u32[]{:S(2)}) collective-permute-start(f32[64,96]{1,0:T(8,128)S(1)} %get-tuple-element.90), channel_id=1, source_target_pairs={{4,8},{8,4},{12,16},{16,12},{20,24},{24,20},{28,32},{32,28},{36,40... | collective-permute-start | bytes 73736 | tf_op jit(solution)/shard_map/ppermute | solution.py:125
  257.7 6.8 %collective-permute-start.22 = (f32[64,96]{1,0:T(8,128)S(1)}, f32[64,96]{1,0:T(8,128)S(1)}, u32[]{:S(2)}, u32[]{:S(2)}) collective-permute-start(f32[64,96]{1,0:T(8,128)S(1)} %get-tuple-element.91), channel_id=1, source_target_pairs={{0,1},{1,0},{2,3},{3,2},{4,5},{5,4},{6,7},{7,6},{8,9},{9,8},{10,11... | collective-permute-start | bytes 73736 | tf_op jit(solution)/shard_map/ppermute | solution.py:125
  283.8 13.7 %collective-permute-start.24 = (f32[64,96]{1,0:T(8,128)S(1)}, f32[64,96]{1,0:T(8,128)S(1)}, u32[]{:S(2)}, u32[]{:S(2)}) collective-permute-start(f32[64,96]{1,0:T(8,128)S(1)} %get-tuple-element.95), channel_id=1, source_target_pairs={{0,4},{4,0},{8,12},{12,8},{16,20},{20,16},{24,28},{28,24},{32,36},... | collective-permute-start | bytes 73736 | tf_op jit(solution)/shard_map/ppermute | solution.py:125
  285.8 11.8 %collective-permute-start.25 = (f32[64,96]{1,0:T(8,128)S(1)}, f32[64,96]{1,0:T(8,128)S(1)}, u32[]{:S(2)}, u32[]{:S(2)}) collective-permute-start(f32[64,96]{1,0:T(8,128)S(1)} %get-tuple-element.96), channel_id=1, source_target_pairs={{4,8},{8,4},{12,16},{16,12},{20,24},{24,20},{28,32},{32,28},{36,40... | collective-permute-start | bytes 73736 | tf_op jit(solution)/shard_map/ppermute | solution.py:125
  291.6 6.6 %collective-permute-start.26 = (f32[64,96]{1,0:T(8,128)S(1)}, f32[64,96]{1,0:T(8,128)S(1)}, u32[]{:S(2)}, u32[]{:S(2)}) collective-permute-start(f32[64,96]{1,0:T(8,128)S(1)} %get-tuple-element.97), channel_id=1, source_target_pairs={{0,1},{1,0},{2,3},{3,2},{4,5},{5,4},{6,7},{7,6},{8,9},{9,8},{10,11... | collective-permute-start | bytes 73736 | tf_op jit(solution)/shard_map/ppermute | solution.py:125
  299.6 15.3 %all-to-all-start.11 = ((bf16[8,64,384]{2,1,0:T(8,128)(2,1)}), bf16[8,64,384]{2,1,0:T(8,128)(2,1)S(1)}, u32[]{:S(2)}, u32[]{:S(2)}) async-start(bf16[8,64,384]{2,1,0:T(8,128)(2,1)} %get-tuple-element.99), calls=%async_computation.11 | async-start | bytes 786432 | tf_op jit(solution)/shard_map/all_to_all | solution.py:247
  320.3 12.5 %collective-permute-start.28 = (f32[64,96]{1,0:T(8,128)S(1)}, f32[64,96]{1,0:T(8,128)S(1)}, u32[]{:S(2)}, u32[]{:S(2)}) collective-permute-start(f32[64,96]{1,0:T(8,128)S(1)} %get-tuple-element.101), channel_id=1, source_target_pairs={{0,4},{4,8},{8,12},{12,16},{16,20},{20,24},{24,28},{28,32},{32,36}... | collective-permute-start | bytes 73736 | tf_op jit(solution)/shard_map/ppermute | solution.py:125
  327.2 6.6 %collective-permute-start.29 = (f32[64,96]{1,0:T(8,128)S(1)}, f32[64,96]{1,0:T(8,128)S(1)}, u32[]{:S(2)}, u32[]{:S(2)}) collective-permute-start(f32[64,96]{1,0:T(8,128)S(1)} %get-tuple-element.102), channel_id=1, source_target_pairs={{0,1},{1,2},{2,3},{4,5},{5,6},{6,7},{8,9},{9,10},{10,11},{12,13},{... | collective-permute-start | bytes 73736 | tf_op jit(solution)/shard_map/ppermute | solution.py:125
  336.6 9.7 %all-to-all-start.12 = ((f32[8,1,48]{2,1,0:T(1,128)}), f32[8,1,48]{2,1,0:T(1,128)S(1)}, u32[]{:S(2)}, u32[]{:S(2)}) async-start(f32[8,1,48]{2,1,0:T(1,128)} %copy.106), calls=%async_computation.12 | async-start | bytes 8192 | tf_op jit(solution)/shard_map/all_to_all | solution.py:247
  346.9 7.7 %all-to-all-start.13 = ((f32[4,1,48]{2,1,0:T(1,128)}), f32[4,1,48]{2,1,0:T(1,128)S(1)}, u32[]{:S(2)}, u32[]{:S(2)}) async-start(f32[4,1,48]{2,1,0:T(1,128)} %broadcast_in_dim.139), calls=%async_computation.13 | async-start | bytes 4096 | tf_op jit(solution)/shard_map/all_to_all | solution.py:247
  355.2 13.0 %all-to-all-start.14 = ((f32[16,1,48]{2,1,0:T(1,128)}), f32[16,1,48]{2,1,0:T(1,128)S(1)}, u32[]{:S(2)}, u32[]{:S(2)}) async-start(f32[16,1,48]{2,1,0:T(1,128)} %broadcast_in_dim.140), calls=%async_computation.14 | async-start | bytes 16384 | tf_op jit(solution)/shard_map/all_to_all | solution.py:247
  371.4 9.9 %all-to-all-start.15 = ((f32[8,1,216]{2,1,0:T(1,128)}), f32[8,1,216]{2,1,0:T(1,128)S(1)}, u32[]{:S(2)}, u32[]{:S(2)}) async-start(f32[8,1,216]{2,1,0:T(1,128)} %all_to_all.78), calls=%async_computation.15 | async-start | bytes 16384 | tf_op jit(solution)/shard_map/all_to_all | solution.py:247
  (22 other events, 130.0 us)

commit v3 on v2

--- a/solution.py
+++ b/solution.py
@@ -51,6 +51,10 @@
         stiffness.reshape(faces, n_freq, run, width),
         mass_matrix.reshape(faces, n_freq, run, width),
     )
+
+
+def odd_masks(odd_ref, shape):
+    return [jnp.broadcast_to(odd_ref[i : i + 1, : shape[1]], shape) > 0.5 for i in range(2)]
 
 
 def apply_kernel(sign, faces, by_slot, sides, *refs):
@@ -88,7 +92,7 @@
         face_refs[0][...] = east
         face_refs[1][...] = north
         return
-    odd_x, odd_y = odd_ref[0] == 1, odd_ref[1] == 1
+    odd_x, odd_y = odd_masks(odd_ref, west.shape)
     face_refs[0][...] = jnp.where(odd_x, west, east)
     face_refs[1][...] = jnp.where(odd_x, east, west)
     face_refs[2][...] = jnp.where(odd_y, south, north)
@@ -107,7 +111,7 @@
             vmem,
             pl.BlockSpec(memory_space=pltpu.HBM),
             vmem,
-            pl.BlockSpec(memory_space=pltpu.SMEM),
+            vmem,
         ],
         out_specs=[vmem] * (1 + n_out),
         out_shape=[jax.ShapeDtypeStruct((count, width), F32)]
@@ -157,8 +161,8 @@
         weight_ref, at = refs[at], at + 1
     outs = list(refs[at:])
     if n_halo == faces:
-        odd_x, odd_y = odd_ref[0] == 1, odd_ref[1] == 1
         near_x, far_x, near_y, far_y = halo
+        odd_x, odd_y = odd_masks(odd_ref, near_x.shape)
         halo = [
             jnp.where(odd_x, near_x, far_x),
             jnp.where(odd_x, far_x, near_x),
@@ -172,22 +176,23 @@
     count, width = vector.shape
     known = [ref[...] for ref in earlier]
     if combine:
-        vector = vector * coefs_ref[:, len(combine) : len(combine) + 1]
-        for slot, which in enumerate(combine):
-            vector = vector + known[which] * coefs_ref[:, slot : slot + 1]
+        vector = known[0] - coefs_ref[...] * vector
     known.append(vector)
     if keep:
         outs.pop(0)[...] = vector
     sums = None
     if products:
-        weight = jnp.broadcast_to(weight_ref[...], (8, width))
+        weighted = {left: known[left] * weight_ref[...] for left, _ in products}
+        ones = jnp.ones((8, 128), F32)
         high = -(-len(products) // 8) * 8
         place = lax.broadcasted_iota(jnp.int32, (high, count), 0)
         sums = jnp.zeros((high, count), F32)
         for slot, (left, right) in enumerate(products):
+            value = weighted[left] * known[right]
+            value = sum(value[:, k : k + 128] for k in range(0, width, 128))
             value = lax.dot_general(
-                weight,
-                known[left] * known[right],
+                ones,
+                value,
                 (((1,), (1,)), ((), ())),
                 precision=lax.Precision.HIGHEST,
                 preferred_element_type=F32,
@@ -214,13 +219,13 @@
 
 
 def finish(
-    local, halos, odd, n_freq, faces, earlier=(), combine=(), coefs=None, products=(),
+    local, halos, odd, n_freq, faces, earlier=(), scale=None, products=(),
     weight=None, keep=True, send=True,
 ):
     count, width = local.shape
     args = [odd, local, *halos, *earlier]
-    if combine:
-        args.append(coefs)
+    if scale is not None:
+        args.append(scale)
     if products:
         args.append(weight)
     shapes = []
@@ -231,11 +236,11 @@
         shapes.append(jax.ShapeDtypeStruct((n_freq, count + high, width), BF))
     elif products:
         shapes.append(jax.ShapeDtypeStruct((high, count), F32))
-    plan = (tuple(combine), tuple(products), keep, send, len(halos))
+    plan = (scale is not None, tuple(products), keep, send, len(halos))
     vmem = pl.BlockSpec(memory_space=pltpu.VMEM)
     return pl.pallas_call(
         functools.partial(finish_kernel, plan, faces, len(earlier), n_freq),
-        in_specs=[pl.BlockSpec(memory_space=pltpu.SMEM)] + [vmem] * (len(args) - 1),
+        in_specs=[vmem] * len(args),
         out_specs=[vmem] * len(shapes),
         out_shape=shapes,
         compiler_params=params(),
@@ -271,27 +276,22 @@
     return out
 
 
-def unit(at, one):
-    return [one if i == at else None for i in range(4)]
-
-
-def last_scalars(alpha0, beta0, alpha1, g, w):
-    one = jnp.ones_like(alpha0)
-    res0, res1, res2, lead = (unit(i, one) for i in range(4))
-    dir1 = combo(res1, beta0, res0)
-    gamma2 = g[(2, 2)]
-    beta1 = gamma2 / g[(1, 1)]
-    dir2 = combo(res2, beta1, dir1)
-    alpha2 = gamma2 / quad(w, dir2)
-    image = combo(lead, beta1 / alpha1, combo(res1, -1.0, res2))
-    res3 = combo(res2, -alpha2, image)
-    gamma3 = quad(g, res3)
-    dir3 = combo(res3, gamma3 / gamma2, dir2)
-    alpha3 = gamma3 / quad(w, dir3)
-    answer = combo([alpha0, None, None, None], alpha1, dir1)
-    answer = combo(answer, alpha2, dir2)
-    answer = combo(answer, alpha3, dir3)
-    return answer, gamma3
+def solve(theta, g, w):
+    one = jnp.ones_like(theta)
+    residual = direction = [one, None, None, None]
+    answer = [None] * 4
+    gamma = quad(g, residual)
+    for iteration in range(4):
+        alpha = gamma / quad(w, direction)
+        answer = combo(answer, alpha, direction)
+        if iteration < 3:
+            below = [None] + direction[:3]
+            image = combo([None if c is None else theta * c for c in direction], -theta, below)
+            residual = combo(residual, -alpha, image)
+            gamma_next = quad(g, residual)
+            direction = combo(residual, gamma_next / gamma, direction)
+            gamma = gamma_next
+    return answer, gamma
 
 
 def body(stiffness, mass_matrix, omega_table, assignment, adjoint_load, forward_state, owner_index):
@@ -311,6 +311,7 @@
     packet = jnp.concatenate([load, jnp.broadcast_to(tags, (own, 128))], axis=1)
     field = exchange(jnp.broadcast_to(packet[None], (n_freq, *packet.shape)), "freq")
     pair = arrange(stiffness[0, 0], mass_matrix[0, 0], faces, n_freq)
+    pair = pltpu.with_memory_space_constraint(pair, pltpu.HBM)
     slot_tags = field[:, :, order].reshape(count).astype(jnp.int32)
     matches = slot_tags[:, None] == jnp.arange(omega_table.shape[0], dtype=jnp.int32)[None, :]
     omega_rows = jnp.sum(jnp.where(matches, omega_table[None, :], 0.0), axis=1, keepdims=True)
@@ -330,7 +331,8 @@
     once = jnp.where(face_weight < 1.0, jnp.array([1.0, 0.0, 1.0, 0.0], F32), 1.0)
     weight_once = jnp.repeat(once, run)[None, :]
 
-    odd = jnp.stack([lax.rem(lax.axis_index(axis), 2) for axis in ("sx", "sy")]).astype(jnp.int32)
+    odd = jnp.stack([lax.rem(lax.axis_index(axis), 2) for axis in ("sx", "sy")]).astype(F32)
+    odd = jnp.broadcast_to(odd[:, None], (2, 128))
 
     def step(field, sign, by_slot=False, **how):
         local, *face_vals = apply_local(field, pair, omega_rows, odd, sign, faces, by_slot)
@@ -339,68 +341,65 @@
     def by_slots(sums, n_products):
         return jnp.sum(sums[:n_products].reshape(n_products, n_freq, 2, slots), axis=2)
 
-    def spread(sent, n_products):
+    def freq_sums(sent, n_products):
         sums = sum(
             jnp.sum(sent[:, count:, k * count : (k + 1) * count].astype(F32), axis=0)
             for k in range(3)
         )
-        sums = by_slots(sums, n_products)
-        flat = total(total(sums.reshape(-1), "sy"), "sx")
-        return flat.reshape(n_products, n_freq, slots)
+        return by_slots(sums, n_products)
 
     def to_rows(values):
-        wide = jnp.stack(values, axis=-1)[:, None]
-        return jnp.broadcast_to(wide, (n_freq, 2, slots, len(values))).reshape(count, len(values))
-
-    u0, send = step(field, -1.0, by_slot=True)
+        return jnp.broadcast_to(values[:, None], (n_freq, 2, slots)).reshape(count, 1)
+
+    (u0, send) = step(field, -1.0, by_slot=True)
     sent0 = exchange(send, "freq")
-    w0, send = step(sent0, 1.0, earlier=(u0,), products=((0, 0), (1, 1)), weight=weight)
+    (send,) = step(
+        sent0, 1.0, earlier=(u0,), products=((0, 0), (1, 1)), weight=weight, keep=False
+    )
     sent = exchange(send, "freq")
-    gamma0, delta0 = spread(sent, 2)
-    alpha0 = gamma0 / delta0
-    coefs = to_rows([jnp.ones_like(alpha0), -alpha0])
-    u1, send = step(sent, -1.0, earlier=(u0,), combine=(0,), coefs=coefs)
+    flat = total(total(freq_sums(sent, 2).reshape(-1), "sy"), "sx")
+    gamma0, delta0 = flat.reshape(2, n_freq, slots)
+    scale = to_rows(gamma0 / delta0)
+    u1, send = step(sent, -1.0, earlier=(u0,), scale=scale)
     sent1 = exchange(send, "freq")
-    w1, send = step(
-        sent1, 1.0, earlier=(u1, w0), products=((0, 0), (1, 2), (2, 2)), weight=weight
-    )
-    sent = exchange(send, "freq")
-    gamma1, cross, image1 = spread(sent, 3)
-    beta0 = gamma1 / gamma0
-    alpha1 = gamma1 / (image1 + beta0 * (2.0 * cross + beta0 * delta0))
-    ratio = alpha1 * beta0 / alpha0
-    coefs = to_rows([-ratio, 1.0 + ratio, -alpha1])
-    u2, send = step(sent, -1.0, earlier=(u0, u1), combine=(0, 1), coefs=coefs)
+    (send,) = step(sent1, 1.0, keep=False)
+    u2, send = step(exchange(send, "freq"), -1.0, earlier=(u1,), scale=scale)
     sent2 = exchange(send, "freq")
-    w2, send = step(sent2, 1.0)
-    u3, send = step(exchange(send, "freq"), -1.0)
+    (send,) = step(sent2, 1.0, keep=False)
+    keys = ((0, 1), (0, 2), (0, 3), (1, 1), (1, 2), (1, 3), (2, 2), (2, 3), (3, 3))
+    at = {2: 0, 0: 1, 1: 2, 3: 3}
+    (send,) = step(
+        exchange(send, "freq"), -1.0, earlier=(u2, u0, u1), scale=scale,
+        products=tuple((at[i], at[j]) for i, j in keys), weight=weight, keep=False,
+    )
     sent3 = exchange(send, "freq")
     local, *face_vals = apply_local(sent3, pair, omega_rows, odd, 1.0, faces, sides=True)
-    later_g = ((1, 2), (2, 2), (1, 3), (2, 3), (3, 3))
-    later_w = ((0, 2), (1, 2), (2, 2), (0, 3), (1, 3), (2, 3), (3, 3))
-    products = tuple((i - 1, j - 1) for i, j in later_g) + tuple((3 + i, 3 + j) for i, j in later_w)
     (sums,) = finish(
-        local, pass_faces(face_vals), odd, n_freq, faces, earlier=(u1, u2, u3, w0, w1, w2),
-        products=products, weight=weight_once, keep=False, send=False,
-    )
-    sums = by_slots(sums, len(products))
-    sums = jnp.swapaxes(sums, 0, 1).reshape(n_freq, len(products) * slots)
-    ours = jnp.sum(exchange(sums, "freq"), axis=0)
-    ours = total(total(ours, "sy"), "sx").reshape(len(products), slots)
-    earlier = jnp.stack([alpha0, beta0, alpha1, gamma1, delta0, cross, image1])
-    mine = lax.dynamic_index_in_dim(earlier, me, 1, keepdims=False)
-    g = {(1, 1): mine[3]}
-    w = {(0, 0): mine[4], (0, 1): mine[5], (1, 1): mine[6]}
-    for at, key in enumerate(later_g):
-        g[key] = ours[at]
-    for at, key in enumerate(later_w):
-        w[key] = ours[len(later_g) + at]
-    answer, gamma = last_scalars(mine[0], mine[1], mine[2], g, w)
+        local, pass_faces(face_vals), odd, n_freq, faces, products=((0, 0),), weight=weight_once,
+        keep=False, send=False,
+    )
+    sums = jnp.sum(exchange(by_slots(sums, 1)[0], "freq"), axis=0)
+    others = lax.dynamic_index_in_dim(freq_sums(sent3, len(keys)), me, 1, keepdims=False)
+    sums = jnp.concatenate([others, sums[None]], axis=0).reshape(-1)
+    sums = total(total(sums, "sy"), "sx").reshape(len(keys) + 1, slots)
+    own_gamma = lax.dynamic_index_in_dim(gamma0, me, 0, keepdims=False)
+    own_delta = lax.dynamic_index_in_dim(delta0, me, 0, keepdims=False)
+    theta = own_delta / own_gamma
+    g = {key: sums[k] for k, key in enumerate(keys)}
+    g[(0, 0)] = own_gamma
+    w = {
+        (i, j): theta * (g[(i, j)] - g[(min(i + 1, j), max(i + 1, j))])
+        for i in range(3)
+        for j in range(i, 4)
+    }
+    w[(0, 0)] = own_delta
+    w[(3, 3)] = sums[len(keys)]
+    answer, gamma = solve(theta, g, w)
     residual_level = jnp.log(gamma / float(n_sub * 2 * order))
 
     adjoint = 0.0
     for values, sent in zip(answer, (sent0, sent1, sent2, sent3)):
-        block = lax.dynamic_slice_in_dim(sent, me * own, own, axis=1)[:, :, :width].astype(F32)
+        block = lax.dynamic_slice_in_dim(sent, me * own, own, axis=1).astype(F32)
         adjoint = adjoint + block * jnp.tile(values, 2)[None, :, None]
     adjoint = adjoint.reshape(n_freq, 2, slots, faces, run)
     adjoint = jnp.transpose(adjoint, (2, 1, 3, 0, 4)).reshape(slots, 2, faces, face_len)

time: 384 us -> 344 us (0.90)
  local copies, waits for them, and re-layouts: 30.6 us -> 12.2 us
  blocking collectives: 96.8 us -> 80.3 us
  Pallas kernels: 39.1 us -> 30.8 us
    all_to_all x7 -> x6, blocking collectives: 96.8 us -> 80.3 us  [exchange(): return lax.all_to_all(blocks, axis, 0, 0, tiled=False)]
    unnamed x34 -> x14, local copies, waits for them, and re-layouts: 22 us -> 5.46 us
    ppermute x30, starting transfers between devices: 94 us -> 109 us  [permute(): lax.ppermute(values, axis, pairs)]
    all_to_all x9 -> x8, starting transfers between devices: 55.6 us -> 43.4 us  [exchange(): return lax.all_to_all(blocks, axis, 0, 0, tiled=False)]
    pallas_call x8, Pallas kernels: 8.82 us -> 3.47 us  [finish(): pl.pallas_call(functools.partial(finish_kernel, plan, faces, len(earlier)...]
    all_to_all x9 -> x8, waiting for transfers between devices: 52.8 us -> 53.1 us  [exchange(): return lax.all_to_all(blocks, axis, 0, 0, tiled=False)]
  transfers between devices with their start and end apart: 39 -> 38, of which waited for: 15 -> 15; matrix products, arithmetic and copies ran while one was open for 1% -> 1% of each run, Pallas kernels for 3% -> 2%
where the time goes in v3:
time: 344 us; the launch traced here: 342 us
  starting transfers between devices  153 us (44%)
  blocking collectives  80.3 us (23%)
  waiting for transfers between devices  59.4 us (17%)
  Pallas kernels  30.8 us (9%)
  local copies, waits for them, and re-layouts  12.2 us (4%)
  other arithmetic  4.73 us (1%)
    ppermute x30, starting transfers between devices, permute(): lax.ppermute(values, axis, pairs)  109 us
    all_to_all x6, blocking collectives, exchange(): return lax.all_to_all(blocks, axis, 0, 0, tiled=False)  80.3 us
    all_to_all x8, waiting for transfers between devices, exchange(): return lax.all_to_all(blocks, axis, 0, 0, tiled=False)  53.1 us
    all_to_all x8, starting transfers between devices, exchange(): return lax.all_to_all(blocks, axis, 0, 0, tiled=False)  43.4 us
    pallas_call x8, Pallas kernels, apply_local(): pl.pallas_call(functools.partial(apply_kernel, sign, faces, by_slot, side...  22.5 us
  transfers between devices with their start and end apart: 38, of which 15 were waited for; matrix products, arithmetic and copies ran while one was open for 1% of the time, Pallas kernels for 2%

profile of v3, /device:TPU:1, one launch (start us, length us, event | category | flops | bytes accessed | tf_op | source)
XLA Modules:
  0.0 342.3 jit_solution(8655247120451349931)
XLA Ops:
  3.5 10.9 %all-to-all-start = ((bf16[8,8,3200]{2,1,0:T(8,128)(2,1)}), bf16[8,8,3200]{2,1,0:T(8,128)(2,1)S(1)}, u32[]{:S(2)}, u32[]{:S(2)}) async-start(bf16[8,8,3200]{2,1,0:T(8,128)(2,1)} %broadcast_in_dim.117), calls=%async_computation | async-start | bytes 819200 | tf_op jit(solution)/shard_map/all_to_all | solution.py:252
  17.7 4.9 %arrange.1.refs_1_ = bf16[8,384,768]{2,1,0:T(8,128)(2,1)S(1)} custom-call(bf16[4,8,96,384]{3,2,1,0:T(8,128)(2,1)S(1)} %bitcast.40, bf16[4,8,96,384]{3,2,1,0:T(8,128)(2,1)S(1)} %bitcast.41), custom_call_target="tpu_custom_call" | custom-call | tf_op jit(solution)/shard_map/arrange/pallas_call | solution.py:41
  24.8 4.3 %all-to-all-done.refs_0_ = bf16[8,8,3200]{2,1,0:T(8,128)(2,1)S(1)} async-done(((bf16[8,8,3200]{2,1,0:T(8,128)(2,1)}), bf16[8,8,3200]{2,1,0:T(8,128)(2,1)S(1)}, u32[]{:S(2)}, u32[]{:S(2)}) %all-to-all-start) | async-done | bytes 409632 | tf_op jit(solution)/shard_map/all_to_all | solution.py:252
  44.3 3.5 %all-to-all-start.1 = ((bf16[8,64,384]{2,1,0:T(8,128)(2,1)}), bf16[8,64,384]{2,1,0:T(8,128)(2,1)S(1)}, u32[]{:S(2)}, u32[]{:S(2)}) async-start(bf16[8,64,384]{2,1,0:T(8,128)(2,1)} %get-tuple-element.52), calls=%async_computation.1 | async-start | bytes 786432 | tf_op jit(solution)/shard_map/all_to_all | solution.py:252
  47.8 14.1 %all-to-all-done.1.refs_0_ = bf16[8,64,384]{2,1,0:T(8,128)(2,1)S(1)} async-done(((bf16[8,64,384]{2,1,0:T(8,128)(2,1)}), bf16[8,64,384]{2,1,0:T(8,128)(2,1)S(1)}, u32[]{:S(2)}, u32[]{:S(2)}) %all-to-all-start.1) | async-done | bytes 393248 | tf_op jit(solution)/shard_map/all_to_all | solution.py:252
  67.0 4.4 %collective-permute-start.5 = (f32[64,96]{1,0:T(8,128)S(1)}, f32[64,96]{1,0:T(8,128)S(1)}, u32[]{:S(2)}, u32[]{:S(2)}) collective-permute-start(f32[64,96]{1,0:T(8,128)S(1)} %get-tuple-element.55), channel_id=1, source_target_pairs={{4,8},{8,4},{12,16},{16,12},{20,24},{24,20},{28,32},{32,28},{36,40... | collective-permute-start | bytes 73736 | tf_op jit(solution)/shard_map/ppermute | solution.py:129
  71.5 5.7 %collective-permute-start.6 = (f32[64,96]{1,0:T(8,128)S(1)}, f32[64,96]{1,0:T(8,128)S(1)}, u32[]{:S(2)}, u32[]{:S(2)}) collective-permute-start(f32[64,96]{1,0:T(8,128)S(1)} %get-tuple-element.56), channel_id=1, source_target_pairs={{0,1},{1,0},{2,3},{3,2},{4,5},{5,4},{6,7},{7,6},{8,9},{9,8},{10,11... | collective-permute-start | bytes 73736 | tf_op jit(solution)/shard_map/ppermute | solution.py:129
  78.8 16.1 %all_to_all.83.refs_0_ = bf16[8,72,384]{2,1,0:T(8,128)(2,1)S(1)} all-to-all(bf16[8,72,384]{2,1,0:T(8,128)(2,1)S(1)} %finish.9), channel_id=1, replica_groups=mesh['freq'=8,'sx'=16,'sy'=4] {'freq'}, dimensions={0} | all-to-all | bytes 884736 | tf_op jit(solution)/shard_map/all_to_all | solution.py:252
  95.3 11.0 %all_to_all.84 = f32[4,1,64]{2,1,0:T(1,128)S(1)} all-to-all(f32[4,1,64]{2,1,0:T(1,128)S(1)} %broadcast_in_dim.123), channel_id=1, replica_groups=mesh['freq'=8,'sx'=16,'sy'=4] {'sy'}, dimensions={0} | all-to-all | bytes 2048 | tf_op jit(solution)/shard_map/all_to_all | solution.py:252
  106.9 8.9 %all-to-all-start.4 = ((f32[16,1,64]{2,1,0:T(1,128)}), f32[16,1,64]{2,1,0:T(1,128)S(1)}, u32[]{:S(2)}, u32[]{:S(2)}) async-start(f32[16,1,64]{2,1,0:T(1,128)} %broadcast_in_dim.124), calls=%async_computation.4 | async-start | bytes 16384 | tf_op jit(solution)/shard_map/all_to_all | solution.py:252
  129.2 13.8 %all_to_all.85.refs_0_ = bf16[8,64,384]{2,1,0:T(8,128)(2,1)S(1)} all-to-all(bf16[8,64,384]{2,1,0:T(8,128)(2,1)S(1)} %get-tuple-element.64), channel_id=1, replica_groups=mesh['freq'=8,'sx'=16,'sy'=4] {'freq'}, dimensions={0} | all-to-all | bytes 786432 | tf_op jit(solution)/shard_map/all_to_all | solution.py:252
  147.7 7.8 %collective-permute-start.13 = (f32[64,96]{1,0:T(8,128)S(1)}, f32[64,96]{1,0:T(8,128)S(1)}, u32[]{:S(2)}, u32[]{:S(2)}) collective-permute-start(f32[64,96]{1,0:T(8,128)S(1)} %get-tuple-element.67), channel_id=1, source_target_pairs={{4,8},{8,4},{12,16},{16,12},{20,24},{24,20},{28,32},{32,28},{36,40... | collective-permute-start | bytes 73736 | tf_op jit(solution)/shard_map/ppermute | solution.py:129
  155.5 4.9 %collective-permute-start.14 = (f32[64,96]{1,0:T(8,128)S(1)}, f32[64,96]{1,0:T(8,128)S(1)}, u32[]{:S(2)}, u32[]{:S(2)}) collective-permute-start(f32[64,96]{1,0:T(8,128)S(1)} %get-tuple-element.68), channel_id=1, source_target_pairs={{0,1},{1,0},{2,3},{3,2},{4,5},{5,4},{6,7},{7,6},{8,9},{9,8},{10,11... | collective-permute-start | bytes 73736 | tf_op jit(solution)/shard_map/ppermute | solution.py:129
  161.8 13.1 %all_to_all.86.refs_0_ = bf16[8,64,384]{2,1,0:T(8,128)(2,1)S(1)} all-to-all(bf16[8,64,384]{2,1,0:T(8,128)(2,1)S(1)} %finish.11), channel_id=1, replica_groups=mesh['freq'=8,'sx'=16,'sy'=4] {'freq'}, dimensions={0} | all-to-all | bytes 786432 | tf_op jit(solution)/shard_map/all_to_all | solution.py:252
  179.7 8.0 %collective-permute-start.17 = (f32[64,96]{1,0:T(8,128)S(1)}, f32[64,96]{1,0:T(8,128)S(1)}, u32[]{:S(2)}, u32[]{:S(2)}) collective-permute-start(f32[64,96]{1,0:T(8,128)S(1)} %get-tuple-element.72), channel_id=1, source_target_pairs={{4,8},{8,4},{12,16},{16,12},{20,24},{24,20},{28,32},{32,28},{36,40... | collective-permute-start | bytes 73736 | tf_op jit(solution)/shard_map/ppermute | solution.py:129
  187.7 5.3 %collective-permute-start.18 = (f32[64,96]{1,0:T(8,128)S(1)}, f32[64,96]{1,0:T(8,128)S(1)}, u32[]{:S(2)}, u32[]{:S(2)}) collective-permute-start(f32[64,96]{1,0:T(8,128)S(1)} %get-tuple-element.73), channel_id=1, source_target_pairs={{0,1},{1,0},{2,3},{3,2},{4,5},{5,4},{6,7},{7,6},{8,9},{9,8},{10,11... | collective-permute-start | bytes 73736 | tf_op jit(solution)/shard_map/ppermute | solution.py:129
  194.7 13.1 %all_to_all.87.refs_0_ = bf16[8,64,384]{2,1,0:T(8,128)(2,1)S(1)} all-to-all(bf16[8,64,384]{2,1,0:T(8,128)(2,1)S(1)} %get-tuple-element.76), channel_id=1, replica_groups=mesh['freq'=8,'sx'=16,'sy'=4] {'freq'}, dimensions={0} | all-to-all | bytes 786432 | tf_op jit(solution)/shard_map/all_to_all | solution.py:252
  212.5 7.9 %collective-permute-start.21 = (f32[64,96]{1,0:T(8,128)S(1)}, f32[64,96]{1,0:T(8,128)S(1)}, u32[]{:S(2)}, u32[]{:S(2)}) collective-permute-start(f32[64,96]{1,0:T(8,128)S(1)} %get-tuple-element.79), channel_id=1, source_target_pairs={{4,8},{8,4},{12,16},{16,12},{20,24},{24,20},{28,32},{32,28},{36,40... | collective-permute-start | bytes 73736 | tf_op jit(solution)/shard_map/ppermute | solution.py:129
  220.5 5.4 %collective-permute-start.22 = (f32[64,96]{1,0:T(8,128)S(1)}, f32[64,96]{1,0:T(8,128)S(1)}, u32[]{:S(2)}, u32[]{:S(2)}) collective-permute-start(f32[64,96]{1,0:T(8,128)S(1)} %get-tuple-element.80), channel_id=1, source_target_pairs={{0,1},{1,0},{2,3},{3,2},{4,5},{5,4},{6,7},{7,6},{8,9},{9,8},{10,11... | collective-permute-start | bytes 73736 | tf_op jit(solution)/shard_map/ppermute | solution.py:129
  227.5 13.1 %all_to_all.88.refs_0_ = bf16[8,64,384]{2,1,0:T(8,128)(2,1)S(1)} all-to-all(bf16[8,64,384]{2,1,0:T(8,128)(2,1)S(1)} %finish.13), channel_id=1, replica_groups=mesh['freq'=8,'sx'=16,'sy'=4] {'freq'}, dimensions={0} | all-to-all | bytes 786432 | tf_op jit(solution)/shard_map/all_to_all | solution.py:252
  245.4 8.0 %collective-permute-start.25 = (f32[64,96]{1,0:T(8,128)S(1)}, f32[64,96]{1,0:T(8,128)S(1)}, u32[]{:S(2)}, u32[]{:S(2)}) collective-permute-start(f32[64,96]{1,0:T(8,128)S(1)} %get-tuple-element.84), channel_id=1, source_target_pairs={{4,8},{8,4},{12,16},{16,12},{20,24},{24,20},{28,32},{32,28},{36,40... | collective-permute-start | bytes 73736 | tf_op jit(solution)/shard_map/ppermute | solution.py:129
  253.4 5.6 %collective-permute-start.26 = (f32[64,96]{1,0:T(8,128)S(1)}, f32[64,96]{1,0:T(8,128)S(1)}, u32[]{:S(2)}, u32[]{:S(2)}) collective-permute-start(f32[64,96]{1,0:T(8,128)S(1)} %get-tuple-element.85), channel_id=1, source_target_pairs={{0,1},{1,0},{2,3},{3,2},{4,5},{5,4},{6,7},{7,6},{8,9},{9,8},{10,11... | collective-permute-start | bytes 73736 | tf_op jit(solution)/shard_map/ppermute | solution.py:129
  261.8 3.5 %all-to-all-start.9 = ((bf16[8,80,384]{2,1,0:T(8,128)(2,1)}), bf16[8,80,384]{2,1,0:T(8,128)(2,1)S(1)}, u32[]{:S(2)}, u32[]{:S(2)}) async-start(bf16[8,80,384]{2,1,0:T(8,128)(2,1)} %finish.14), calls=%async_computation.9 | async-start | bytes 983040 | tf_op jit(solution)/shard_map/all_to_all | solution.py:252
  265.4 11.5 %all-to-all-done.9.refs_0_ = bf16[8,80,384]{2,1,0:T(8,128)(2,1)S(1)} async-done(((bf16[8,80,384]{2,1,0:T(8,128)(2,1)}), bf16[8,80,384]{2,1,0:T(8,128)(2,1)S(1)}, u32[]{:S(2)}, u32[]{:S(2)}) %all-to-all-start.9) | async-done | bytes 491552 | tf_op jit(solution)/shard_map/all_to_all | solution.py:252
  279.8 9.1 %collective-permute-start.28 = (f32[64,96]{1,0:T(8,128)S(1)}, f32[64,96]{1,0:T(8,128)S(1)}, u32[]{:S(2)}, u32[]{:S(2)}) collective-permute-start(f32[64,96]{1,0:T(8,128)S(1)} %get-tuple-element.89), channel_id=1, source_target_pairs={{0,4},{4,8},{8,12},{12,16},{16,20},{20,24},{24,28},{28,32},{32,36}... | collective-permute-start | bytes 73736 | tf_op jit(solution)/shard_map/ppermute | solution.py:129
  288.9 5.3 %collective-permute-start.29 = (f32[64,96]{1,0:T(8,128)S(1)}, f32[64,96]{1,0:T(8,128)S(1)}, u32[]{:S(2)}, u32[]{:S(2)}) collective-permute-start(f32[64,96]{1,0:T(8,128)S(1)} %get-tuple-element.90), channel_id=1, source_target_pairs={{0,1},{1,2},{2,3},{4,5},{5,6},{6,7},{8,9},{9,10},{10,11},{12,13},{... | collective-permute-start | bytes 73736 | tf_op jit(solution)/shard_map/ppermute | solution.py:129
  299.5 6.4 %all-to-all-done.10 = f32[8,1,4]{2,1,0:T(1,128)S(1)} async-done(((f32[8,1,4]{2,1,0:T(1,128)}), f32[8,1,4]{2,1,0:T(1,128)S(1)}, u32[]{:S(2)}, u32[]{:S(2)}) %all-to-all-start.10) | async-done | bytes 160 | tf_op jit(solution)/shard_map/all_to_all | solution.py:252
  306.9 4.5 %all-to-all-start.11 = ((f32[4,1,40]{2,1,0:T(1,128)}), f32[4,1,40]{2,1,0:T(1,128)S(1)}, u32[]{:S(2)}, u32[]{:S(2)}) async-start(f32[4,1,40]{2,1,0:T(1,128)} %broadcast_in_dim.129), calls=%async_computation.11 | async-start | bytes 4096 | tf_op jit(solution)/shard_map/all_to_all | solution.py:252
  311.4 4.0 %all-to-all-done.11 = f32[4,1,40]{2,1,0:T(1,128)S(1)} async-done(((f32[4,1,40]{2,1,0:T(1,128)}), f32[4,1,40]{2,1,0:T(1,128)S(1)}, u32[]{:S(2)}, u32[]{:S(2)}) %all-to-all-start.11) | async-done | bytes 672 | tf_op jit(solution)/shard_map/all_to_all | solution.py:252
  316.1 5.5 %all-to-all-start.12 = ((f32[16,1,40]{2,1,0:T(1,128)}), f32[16,1,40]{2,1,0:T(1,128)S(1)}, u32[]{:S(2)}, u32[]{:S(2)}) async-start(f32[16,1,40]{2,1,0:T(1,128)} %broadcast_in_dim.130), calls=%async_computation.12 | async-start | bytes 16384 | tf_op jit(solution)/shard_map/all_to_all | solution.py:252
  321.6 7.0 %all-to-all-done.12 = f32[16,1,40]{2,1,0:T(1,128)S(1)} async-done(((f32[16,1,40]{2,1,0:T(1,128)}), f32[16,1,40]{2,1,0:T(1,128)S(1)}, u32[]{:S(2)}, u32[]{:S(2)}) %all-to-all-start.12) | async-done | bytes 2592 | tf_op jit(solution)/shard_map/all_to_all | solution.py:252
  335.9 5.8 %all-to-all-done.13 = f32[8,1,216]{2,1,0:T(1,128)S(1)} async-done(((f32[8,1,216]{2,1,0:T(1,128)}), f32[8,1,216]{2,1,0:T(1,128)S(1)}, u32[]{:S(2)}, u32[]{:S(2)}) %all-to-all-start.13) | async-done | bytes 6944 | tf_op jit(solution)/shard_map/all_to_all | solution.py:252
  (162 shorter events, 88.7 us)
Async XLA Ops:
  3.5 25.5 %all-to-all-start = ((bf16[8,8,3200]{2,1,0:T(8,128)(2,1)}), bf16[8,8,3200]{2,1,0:T(8,128)(2,1)S(1)}, u32[]{:S(2)}, u32[]{:S(2)}) async-start(bf16[8,8,3200]{2,1,0:T(8,128)(2,1)} %broadcast_in_dim.117), calls=%async_computation | async-start | bytes 819200 | tf_op jit(solution)/shard_map/all_to_all | solution.py:252
  32.4 10.1 %collective-permute-start = (f32[64,96]{1,0:T(8,128)S(1)}, f32[64,96]{1,0:T(8,128)S(1)}, u32[]{:S(2)}, u32[]{:S(2)}) collective-permute-start(f32[64,96]{1,0:T(8,128)S(1)} %get-tuple-element.48), channel_id=1, source_target_pairs={{0,4},{4,0},{8,12},{12,8},{16,20},{20,16},{24,28},{28,24},{32,36},... | collective-permute-start | bytes 73736 | tf_op jit(solution)/shard_map/ppermute | solution.py:129
  35.6 6.9 %collective-permute-start.1 = (f32[64,96]{1,0:T(8,128)S(1)}, f32[64,96]{1,0:T(8,128)S(1)}, u32[]{:S(2)}, u32[]{:S(2)}) collective-permute-start(f32[64,96]{1,0:T(8,128)S(1)} %get-tuple-element.49), channel_id=1, source_target_pairs={{4,8},{8,4},{12,16},{16,12},{20,24},{24,20},{28,32},{32,28},{36,40... | collective-permute-start | bytes 73736 | tf_op jit(solution)/shard_map/ppermute | solution.py:129
  38.7 4.7 %collective-permute-start.2 = (f32[64,96]{1,0:T(8,128)S(1)}, f32[64,96]{1,0:T(8,128)S(1)}, u32[]{:S(2)}, u32[]{:S(2)}) collective-permute-start(f32[64,96]{1,0:T(8,128)S(1)} %get-tuple-element.50), channel_id=1, source_target_pairs={{0,1},{1,0},{2,3},{3,2},{4,5},{5,4},{6,7},{7,6},{8,9},{9,8},{10,11... | collective-permute-start | bytes 73736 | tf_op jit(solution)/shard_map/ppermute | solution.py:129
  44.3 17.6 %all-to-all-start.1 = ((bf16[8,64,384]{2,1,0:T(8,128)(2,1)}), bf16[8,64,384]{2,1,0:T(8,128)(2,1)S(1)}, u32[]{:S(2)}, u32[]{:S(2)}) async-start(bf16[8,64,384]{2,1,0:T(8,128)(2,1)} %get-tuple-element.52), calls=%async_computation.1 | async-start | bytes 786432 | tf_op jit(solution)/shard_map/all_to_all | solution.py:252
  64.7 13.4 %collective-permute-start.4 = (f32[64,96]{1,0:T(8,128)S(1)}, f32[64,96]{1,0:T(8,128)S(1)}, u32[]{:S(2)}, u32[]{:S(2)}) collective-permute-start(f32[64,96]{1,0:T(8,128)S(1)} %get-tuple-element.54), channel_id=1, source_target_pairs={{0,4},{4,0},{8,12},{12,8},{16,20},{20,16},{24,28},{28,24},{32,36},... | collective-permute-start | bytes 73736 | tf_op jit(solution)/shard_map/ppermute | solution.py:129
  67.0 11.1 %collective-permute-start.5 = (f32[64,96]{1,0:T(8,128)S(1)}, f32[64,96]{1,0:T(8,128)S(1)}, u32[]{:S(2)}, u32[]{:S(2)}) collective-permute-start(f32[64,96]{1,0:T(8,128)S(1)} %get-tuple-element.55), channel_id=1, source_target_pairs={{4,8},{8,4},{12,16},{16,12},{20,24},{24,20},{28,32},{32,28},{36,40... | collective-permute-start | bytes 73736 | tf_op jit(solution)/shard_map/ppermute | solution.py:129
  71.5 7.0 %collective-permute-start.6 = (f32[64,96]{1,0:T(8,128)S(1)}, f32[64,96]{1,0:T(8,128)S(1)}, u32[]{:S(2)}, u32[]{:S(2)}) collective-permute-start(f32[64,96]{1,0:T(8,128)S(1)} %get-tuple-element.56), channel_id=1, source_target_pairs={{0,1},{1,0},{2,3},{3,2},{4,5},{5,4},{6,7},{7,6},{8,9},{9,8},{10,11... | collective-permute-start | bytes 73736 | tf_op jit(solution)/shard_map/ppermute | solution.py:129
  106.9 20.4 %all-to-all-start.4 = ((f32[16,1,64]{2,1,0:T(1,128)}), f32[16,1,64]{2,1,0:T(1,128)S(1)}, u32[]{:S(2)}, u32[]{:S(2)}) async-start(f32[16,1,64]{2,1,0:T(1,128)} %broadcast_in_dim.124), calls=%async_computation.4 | async-start | bytes 16384 | tf_op jit(solution)/shard_map/all_to_all | solution.py:252
  118.7 9.0 %collective-permute-start.10 = (f32[64,96]{1,0:T(8,128)S(1)}, f32[64,96]{1,0:T(8,128)S(1)}, u32[]{:S(2)}, u32[]{:S(2)}) collective-permute-start(f32[64,96]{1,0:T(8,128)S(1)} %get-tuple-element.62), channel_id=1, source_target_pairs={{0,1},{1,0},{2,3},{3,2},{4,5},{5,4},{6,7},{7,6},{8,9},{9,8},{10,11... | collective-permute-start | bytes 73736 | tf_op jit(solution)/shard_map/ppermute | solution.py:129
  120.9 6.8 %collective-permute-start.11 = (f32[64,96]{1,0:T(8,128)S(1)}, f32[64,96]{1,0:T(8,128)S(1)}, u32[]{:S(2)}, u32[]{:S(2)}) collective-permute-start(f32[64,96]{1,0:T(8,128)S(1)} %get-tuple-element.63), channel_id=1, source_target_pairs={{1,2},{2,1},{5,6},{6,5},{9,10},{10,9},{13,14},{14,13},{17,18},{18,... | collective-permute-start | bytes 73736 | tf_op jit(solution)/shard_map/ppermute | solution.py:129
  121.5 6.1 %collective-permute-start.8 = (f32[64,96]{1,0:T(8,128)S(1)}, f32[64,96]{1,0:T(8,128)S(1)}, u32[]{:S(2)}, u32[]{:S(2)}) collective-permute-start(f32[64,96]{1,0:T(8,128)S(1)} %get-tuple-element.60), channel_id=1, source_target_pairs={{0,4},{4,0},{8,12},{12,8},{16,20},{20,16},{24,28},{28,24},{32,36},... | collective-permute-start | bytes 73736 | tf_op jit(solution)/shard_map/ppermute | solution.py:129
  123.8 5.2 %collective-permute-start.9 = (f32[64,96]{1,0:T(8,128)S(1)}, f32[64,96]{1,0:T(8,128)S(1)}, u32[]{:S(2)}, u32[]{:S(2)}) collective-permute-start(f32[64,96]{1,0:T(8,128)S(1)} %get-tuple-element.61), channel_id=1, source_target_pairs={{4,8},{8,4},{12,16},{16,12},{20,24},{24,20},{28,32},{32,28},{36,40... | collective-permute-start | bytes 73736 | tf_op jit(solution)/shard_map/ppermute | solution.py:129
  145.8 15.3 %collective-permute-start.12 = (f32[64,96]{1,0:T(8,128)S(1)}, f32[64,96]{1,0:T(8,128)S(1)}, u32[]{:S(2)}, u32[]{:S(2)}) collective-permute-start(f32[64,96]{1,0:T(8,128)S(1)} %get-tuple-element.66), channel_id=1, source_target_pairs={{0,4},{4,0},{8,12},{12,8},{16,20},{20,16},{24,28},{28,24},{32,36},... | collective-permute-start | bytes 73736 | tf_op jit(solution)/shard_map/ppermute | solution.py:129
  147.7 13.4 %collective-permute-start.13 = (f32[64,96]{1,0:T(8,128)S(1)}, f32[64,96]{1,0:T(8,128)S(1)}, u32[]{:S(2)}, u32[]{:S(2)}) collective-permute-start(f32[64,96]{1,0:T(8,128)S(1)} %get-tuple-element.67), channel_id=1, source_target_pairs={{4,8},{8,4},{12,16},{16,12},{20,24},{24,20},{28,32},{32,28},{36,40... | collective-permute-start | bytes 73736 | tf_op jit(solution)/shard_map/ppermute | solution.py:129
  155.5 6.2 %collective-permute-start.14 = (f32[64,96]{1,0:T(8,128)S(1)}, f32[64,96]{1,0:T(8,128)S(1)}, u32[]{:S(2)}, u32[]{:S(2)}) collective-permute-start(f32[64,96]{1,0:T(8,128)S(1)} %get-tuple-element.68), channel_id=1, source_target_pairs={{0,1},{1,0},{2,3},{3,2},{4,5},{5,4},{6,7},{7,6},{8,9},{9,8},{10,11... | collective-permute-start | bytes 73736 | tf_op jit(solution)/shard_map/ppermute | solution.py:129
  177.8 15.8 %collective-permute-start.16 = (f32[64,96]{1,0:T(8,128)S(1)}, f32[64,96]{1,0:T(8,128)S(1)}, u32[]{:S(2)}, u32[]{:S(2)}) collective-permute-start(f32[64,96]{1,0:T(8,128)S(1)} %get-tuple-element.71), channel_id=1, source_target_pairs={{0,4},{4,0},{8,12},{12,8},{16,20},{20,16},{24,28},{28,24},{32,36},... | collective-permute-start | bytes 73736 | tf_op jit(solution)/shard_map/ppermute | solution.py:129
  179.7 13.9 %collective-permute-start.17 = (f32[64,96]{1,0:T(8,128)S(1)}, f32[64,96]{1,0:T(8,128)S(1)}, u32[]{:S(2)}, u32[]{:S(2)}) collective-permute-start(f32[64,96]{1,0:T(8,128)S(1)} %get-tuple-element.72), channel_id=1, source_target_pairs={{4,8},{8,4},{12,16},{16,12},{20,24},{24,20},{28,32},{32,28},{36,40... | collective-permute-start | bytes 73736 | tf_op jit(solution)/shard_map/ppermute | solution.py:129
  187.7 6.8 %collective-permute-start.18 = (f32[64,96]{1,0:T(8,128)S(1)}, f32[64,96]{1,0:T(8,128)S(1)}, u32[]{:S(2)}, u32[]{:S(2)}) collective-permute-start(f32[64,96]{1,0:T(8,128)S(1)} %get-tuple-element.73), channel_id=1, source_target_pairs={{0,1},{1,0},{2,3},{3,2},{4,5},{5,4},{6,7},{7,6},{8,9},{9,8},{10,11... | collective-permute-start | bytes 73736 | tf_op jit(solution)/shard_map/ppermute | solution.py:129
  210.6 15.9 %collective-permute-start.20 = (f32[64,96]{1,0:T(8,128)S(1)}, f32[64,96]{1,0:T(8,128)S(1)}, u32[]{:S(2)}, u32[]{:S(2)}) collective-permute-start(f32[64,96]{1,0:T(8,128)S(1)} %get-tuple-element.78), channel_id=1, source_target_pairs={{0,4},{4,0},{8,12},{12,8},{16,20},{20,16},{24,28},{28,24},{32,36},... | collective-permute-start | bytes 73736 | tf_op jit(solution)/shard_map/ppermute | solution.py:129
  212.5 14.0 %collective-permute-start.21 = (f32[64,96]{1,0:T(8,128)S(1)}, f32[64,96]{1,0:T(8,128)S(1)}, u32[]{:S(2)}, u32[]{:S(2)}) collective-permute-start(f32[64,96]{1,0:T(8,128)S(1)} %get-tuple-element.79), channel_id=1, source_target_pairs={{4,8},{8,4},{12,16},{16,12},{20,24},{24,20},{28,32},{32,28},{36,40... | collective-permute-start | bytes 73736 | tf_op jit(solution)/shard_map/ppermute | solution.py:129
  220.5 6.9 %collective-permute-start.22 = (f32[64,96]{1,0:T(8,128)S(1)}, f32[64,96]{1,0:T(8,128)S(1)}, u32[]{:S(2)}, u32[]{:S(2)}) collective-permute-start(f32[64,96]{1,0:T(8,128)S(1)} %get-tuple-element.80), channel_id=1, source_target_pairs={{0,1},{1,0},{2,3},{3,2},{4,5},{5,4},{6,7},{7,6},{8,9},{9,8},{10,11... | collective-permute-start | bytes 73736 | tf_op jit(solution)/shard_map/ppermute | solution.py:129
  243.5 16.2 %collective-permute-start.24 = (f32[64,96]{1,0:T(8,128)S(1)}, f32[64,96]{1,0:T(8,128)S(1)}, u32[]{:S(2)}, u32[]{:S(2)}) collective-permute-start(f32[64,96]{1,0:T(8,128)S(1)} %get-tuple-element.83), channel_id=1, source_target_pairs={{0,4},{4,0},{8,12},{12,8},{16,20},{20,16},{24,28},{28,24},{32,36},... | collective-permute-start | bytes 73736 | tf_op jit(solution)/shard_map/ppermute | solution.py:129
  245.4 14.3 %collective-permute-start.25 = (f32[64,96]{1,0:T(8,128)S(1)}, f32[64,96]{1,0:T(8,128)S(1)}, u32[]{:S(2)}, u32[]{:S(2)}) collective-permute-start(f32[64,96]{1,0:T(8,128)S(1)} %get-tuple-element.84), channel_id=1, source_target_pairs={{4,8},{8,4},{12,16},{16,12},{20,24},{24,20},{28,32},{32,28},{36,40... | collective-permute-start | bytes 73736 | tf_op jit(solution)/shard_map/ppermute | solution.py:129
  253.4 6.9 %collective-permute-start.26 = (f32[64,96]{1,0:T(8,128)S(1)}, f32[64,96]{1,0:T(8,128)S(1)}, u32[]{:S(2)}, u32[]{:S(2)}) collective-permute-start(f32[64,96]{1,0:T(8,128)S(1)} %get-tuple-element.85), channel_id=1, source_target_pairs={{0,1},{1,0},{2,3},{3,2},{4,5},{5,4},{6,7},{7,6},{8,9},{9,8},{10,11... | collective-permute-start | bytes 73736 | tf_op jit(solution)/shard_map/ppermute | solution.py:129
  261.8 15.2 %all-to-all-start.9 = ((bf16[8,80,384]{2,1,0:T(8,128)(2,1)}), bf16[8,80,384]{2,1,0:T(8,128)(2,1)S(1)}, u32[]{:S(2)}, u32[]{:S(2)}) async-start(bf16[8,80,384]{2,1,0:T(8,128)(2,1)} %finish.14), calls=%async_computation.9 | async-start | bytes 983040 | tf_op jit(solution)/shard_map/all_to_all | solution.py:252
  279.8 14.6 %collective-permute-start.28 = (f32[64,96]{1,0:T(8,128)S(1)}, f32[64,96]{1,0:T(8,128)S(1)}, u32[]{:S(2)}, u32[]{:S(2)}) collective-permute-start(f32[64,96]{1,0:T(8,128)S(1)} %get-tuple-element.89), channel_id=1, source_target_pairs={{0,4},{4,8},{8,12},{12,16},{16,20},{20,24},{24,28},{28,32},{32,36}... | collective-permute-start | bytes 73736 | tf_op jit(solution)/shard_map/ppermute | solution.py:129
  288.9 6.3 %collective-permute-start.29 = (f32[64,96]{1,0:T(8,128)S(1)}, f32[64,96]{1,0:T(8,128)S(1)}, u32[]{:S(2)}, u32[]{:S(2)}) collective-permute-start(f32[64,96]{1,0:T(8,128)S(1)} %get-tuple-element.90), channel_id=1, source_target_pairs={{0,1},{1,2},{2,3},{4,5},{5,6},{6,7},{8,9},{9,10},{10,11},{12,13},{... | collective-permute-start | bytes 73736 | tf_op jit(solution)/shard_map/ppermute | solution.py:129
  296.2 9.7 %all-to-all-start.10 = ((f32[8,1,4]{2,1,0:T(1,128)}), f32[8,1,4]{2,1,0:T(1,128)S(1)}, u32[]{:S(2)}, u32[]{:S(2)}) async-start(f32[8,1,4]{2,1,0:T(1,128)} %bitcast.27), calls=%async_computation.10 | async-start | bytes 8192 | tf_op jit(solution)/shard_map/all_to_all | solution.py:252
  306.9 8.6 %all-to-all-start.11 = ((f32[4,1,40]{2,1,0:T(1,128)}), f32[4,1,40]{2,1,0:T(1,128)S(1)}, u32[]{:S(2)}, u32[]{:S(2)}) async-start(f32[4,1,40]{2,1,0:T(1,128)} %broadcast_in_dim.129), calls=%async_computation.11 | async-start | bytes 4096 | tf_op jit(solution)/shard_map/all_to_all | solution.py:252
  316.1 12.5 %all-to-all-start.12 = ((f32[16,1,40]{2,1,0:T(1,128)}), f32[16,1,40]{2,1,0:T(1,128)S(1)}, u32[]{:S(2)}, u32[]{:S(2)}) async-start(f32[16,1,40]{2,1,0:T(1,128)} %broadcast_in_dim.130), calls=%async_computation.12 | async-start | bytes 16384 | tf_op jit(solution)/shard_map/all_to_all | solution.py:252
  331.8 9.8 %all-to-all-start.13 = ((f32[8,1,216]{2,1,0:T(1,128)}), f32[8,1,216]{2,1,0:T(1,128)S(1)}, u32[]{:S(2)}, u32[]{:S(2)}) async-start(f32[8,1,216]{2,1,0:T(1,128)} %all_to_all.68), calls=%async_computation.13 | async-start | bytes 16384 | tf_op jit(solution)/shard_map/all_to_all | solution.py:252
  (13 other events, 147.7 us)

commit v4 on v3

--- a/solution.py
+++ b/solution.py
@@ -18,7 +18,7 @@
     return pltpu.CompilerParams(vmem_limit_bytes=24 * 1024 * 1024)
 
 
-def arrange_kernel(stiff_ref, mass_ref, out_ref, order_ref):
+def arrange_kernel(stiff_ref, mass_ref, stiff_out, mass_out, order_ref):
     faces, _, run, width = stiff_ref.shape
 
     @pl.when(pl.program_id(0) == 0)
@@ -28,10 +28,10 @@
         wanted = faces * lax.rem(target, run) + lax.div(target, run)
         order_ref[...] = jnp.where(source == wanted, 1.0, 0.0).astype(BF)
 
-    for at, ref in enumerate((stiff_ref, mass_ref)):
+    for ref, out_ref in ((stiff_ref, stiff_out), (mass_ref, mass_out)):
         rows = ref[...].reshape(faces * run, width)
         moved = jnp.dot(rows, order_ref[...], preferred_element_type=F32)
-        out_ref[0, :, at * width : (at + 1) * width] = moved.astype(BF)
+        out_ref[0] = moved.astype(BF)
 
 
 def arrange(stiffness, mass_matrix, faces, n_freq):
@@ -42,8 +42,8 @@
         arrange_kernel,
         grid=(n_freq,),
         in_specs=[block, block],
-        out_specs=pl.BlockSpec((1, width, 2 * width), lambda d: (d, 0, 0)),
-        out_shape=jax.ShapeDtypeStruct((n_freq, width, 2 * width), BF),
+        out_specs=[pl.BlockSpec((1, width, width), lambda d: (d, 0, 0))] * 2,
+        out_shape=[jax.ShapeDtypeStruct((n_freq, width, width), BF)] * 2,
         scratch_shapes=[pltpu.VMEM((width, width), BF)],
         compiler_params=params(),
         name="arrange",
@@ -58,27 +58,31 @@
 
 
 def apply_kernel(sign, faces, by_slot, sides, *refs):
-    field_ref, pair_ref, omega_ref, odd_ref, local_ref = refs[:5]
-    face_refs = refs[5:-2]
+    field_ref, stiff_ref, mass_ref, omega_ref, odd_ref, local_ref = refs[:6]
+    face_refs = refs[6:-2]
     held_ref, sems = refs[-2:]
-    n_freq = pair_ref.shape[0]
+    n_freq = stiff_ref.shape[0]
     count, width = local_ref.shape
     copies = [
-        pltpu.make_async_copy(pair_ref.at[d], held_ref.at[d], sems.at[d]) for d in range(n_freq)
+        pltpu.make_async_copy(mass_ref.at[d], held_ref.at[d], sems.at[d]) for d in range(n_freq)
     ]
     for copy in copies:
         copy.start()
-    total_sum = None
-    for d in range(n_freq):
-        if by_slot:
-            rows = field_ref[:, :, d * width : (d + 1) * width].reshape(count, width)
-        else:
-            rows = field_ref[d, :count, :]
-        copies[d].wait()
-        product = jnp.dot(rows, held_ref[d], preferred_element_type=F32)
-        total_sum = product if total_sum is None else total_sum + product
-    stiff_part = total_sum[:, :width]
-    mass_part = total_sum[:, width:]
+    def product(matrix_ref, arrive):
+        result = None
+        for d in range(n_freq):
+            if by_slot:
+                rows = field_ref[:, :, d * width : (d + 1) * width].reshape(count, width)
+            else:
+                rows = field_ref[d, :count, :]
+            if arrive:
+                copies[d].wait()
+            part = jnp.dot(rows, matrix_ref[d], preferred_element_type=F32)
+            result = part if result is None else result + part
+        return result
+
+    stiff_part = product(stiff_ref, False)
+    mass_part = product(held_ref, True)
     row = lax.broadcasted_iota(jnp.int32, (count, width), 0)
     real = lax.rem(row, 8) < 4
     other = jnp.where(
@@ -100,7 +104,7 @@
 
 
 def apply_local(field, pair, omega_rows, odd, sign, faces, by_slot=False, sides=False):
-    n_freq, width, double = pair.shape
+    n_freq, width, _ = pair[0].shape
     count = omega_rows.shape[0]
     run = width // faces
     n_out = 2 if sides else faces
@@ -108,6 +112,7 @@
     return pl.pallas_call(
         functools.partial(apply_kernel, sign, faces, by_slot, sides),
         in_specs=[
+            vmem,
             vmem,
             pl.BlockSpec(memory_space=pltpu.HBM),
             vmem,
@@ -117,12 +122,12 @@
         out_shape=[jax.ShapeDtypeStruct((count, width), F32)]
         + [jax.ShapeDtypeStruct((count, run), F32)] * n_out,
         scratch_shapes=[
-            pltpu.VMEM((n_freq, width, double), BF),
+            pltpu.VMEM((n_freq, width, width), BF),
             pltpu.SemaphoreType.DMA((n_freq,)),
         ],
         compiler_params=params(),
         name="apply_local",
-    )(field, pair, omega_rows, odd)
+    )(field, *pair, omega_rows, odd)
 
 
 def permute(values, axis, pairs):
@@ -130,13 +135,14 @@
 
 
 def swap_faces(face_vals):
-    out = []
-    for axis, (near, far) in (("sx", face_vals[:2]), ("sy", face_vals[2:])):
+    out = {}
+    for axis, (near, far) in (("sy", face_vals[2:]), ("sx", face_vals[:2])):
         count = lax.axis_size(axis)
         low = [(i, i ^ 1) for i in range(count)]
         high = [(i, ((i + 1) ^ 1) - 1) for i in range(1, count - 1)]
-        out += [permute(near, axis, low), permute(far, axis, high)]
-    return out
+        with jax.named_scope("halo_" + axis):
+            out[axis] = [permute(near, axis, low), permute(far, axis, high)]
+    return out["sy"] + out["sx"]
 
 
 def pass_faces(face_vals):
@@ -161,7 +167,7 @@
         weight_ref, at = refs[at], at + 1
     outs = list(refs[at:])
     if n_halo == faces:
-        near_x, far_x, near_y, far_y = halo
+        near_y, far_y, near_x, far_x = halo
         odd_x, odd_y = odd_masks(odd_ref, near_x.shape)
         halo = [
             jnp.where(odd_x, near_x, far_x),
@@ -310,8 +316,11 @@
     tags = jnp.broadcast_to(assignment.astype(BF)[None, :], (2, slots)).reshape(own, 1)
     packet = jnp.concatenate([load, jnp.broadcast_to(tags, (own, 128))], axis=1)
     field = exchange(jnp.broadcast_to(packet[None], (n_freq, *packet.shape)), "freq")
-    pair = arrange(stiffness[0, 0], mass_matrix[0, 0], faces, n_freq)
-    pair = pltpu.with_memory_space_constraint(pair, pltpu.HBM)
+    stiff, mass = arrange(stiffness[0, 0], mass_matrix[0, 0], faces, n_freq)
+    pair = (
+        pltpu.with_memory_space_constraint(stiff, pltpu.VMEM),
+        pltpu.with_memory_space_constraint(mass, pltpu.HBM),
+    )
     slot_tags = field[:, :, order].reshape(count).astype(jnp.int32)
     matches = slot_tags[:, None] == jnp.arange(omega_table.shape[0], dtype=jnp.int32)[None, :]
     omega_rows = jnp.sum(jnp.where(matches, omega_table[None, :], 0.0), axis=1, keepdims=True)

time: 344 us -> 352 us (1.023)
  starting transfers between devices: 153 us -> 158 us
  waiting for transfers between devices: 59.4 us -> 63.3 us
    all_to_all x8, starting transfers between devices: 43.4 us -> 52.3 us  [exchange(): return lax.all_to_all(blocks, axis, 0, 0, tiled=False)]
    ppermute x30, waiting for transfers between devices: 6.33 us -> 13.1 us  [permute(): lax.ppermute(values, axis, pairs)]
where the time goes in v4:
time: 352 us; the launch traced here: 350 us
  starting transfers between devices  158 us (45%)
  blocking collectives  78 us (22%)
  waiting for transfers between devices  63.3 us (18%)
  Pallas kernels  29.4 us (8%)
  local copies, waits for them, and re-layouts  13.6 us (4%)
  other arithmetic  5.55 us (2%)
    ppermute x30, starting transfers between devices, permute(): lax.ppermute(values, axis, pairs)  106 us
    all_to_all x6, blocking collectives, exchange(): return lax.all_to_all(blocks, axis, 0, 0, tiled=False)  78 us
    all_to_all x8, starting transfers between devices, exchange(): return lax.all_to_all(blocks, axis, 0, 0, tiled=False)  52.3 us
    all_to_all x8, waiting for transfers between devices, exchange(): return lax.all_to_all(blocks, axis, 0, 0, tiled=False)  50.2 us
    pallas_call x8, Pallas kernels, apply_local(): pl.pallas_call(functools.partial(apply_kernel, sign, faces, by_slot, side...  21.1 us
    ppermute x30, waiting for transfers between devices, permute(): lax.ppermute(values, axis, pairs)  13.1 us
  transfers between devices with their start and end apart: 38, of which 15 were waited for; matrix products, arithmetic and copies ran while one was open for 1% of the time, Pallas kernels for 2%

profile of v4, /device:TPU:1, one launch (start us, length us, event | category | flops | bytes accessed | tf_op | source)
XLA Modules:
  0.0 350.4 jit_solution(4578482162282393724)
XLA Ops:
  3.5 10.9 %all-to-all-start = ((bf16[8,8,3200]{2,1,0:T(8,128)(2,1)}), bf16[8,8,3200]{2,1,0:T(8,128)(2,1)S(1)}, u32[]{:S(2)}, u32[]{:S(2)}) async-start(bf16[8,8,3200]{2,1,0:T(8,128)(2,1)} %broadcast_in_dim.117), calls=%async_computation | async-start | bytes 819200 | tf_op jit(solution)/shard_map/all_to_all | solution.py:258
  17.7 4.9 %arrange.1 = (bf16[8,384,384]{2,1,0:T(8,128)(2,1)S(1)}, bf16[8,384,384]{2,1,0:T(8,128)(2,1)S(1)}) custom-call(bf16[4,8,96,384]{3,2,1,0:T(8,128)(2,1)S(1)} %bitcast.40, bf16[4,8,96,384]{3,2,1,0:T(8,128)(2,1)S(1)} %bitcast.41), custom_call_target="tpu_custom_call" | custom-call | tf_op jit(solution)/shard_map/arrange/pallas_call | solution.py:41
  24.1 5.0 %all-to-all-done.refs_0_ = bf16[8,8,3200]{2,1,0:T(8,128)(2,1)S(1)} async-done(((bf16[8,8,3200]{2,1,0:T(8,128)(2,1)}), bf16[8,8,3200]{2,1,0:T(8,128)(2,1)S(1)}, u32[]{:S(2)}, u32[]{:S(2)}) %all-to-all-start) | async-done | bytes 409632 | tf_op jit(solution)/shard_map/all_to_all | solution.py:258
  35.9 3.5 collective-permute-start.2
  49.0 11.2 %all-to-all-done.1.refs_0_ = bf16[8,64,384]{2,1,0:T(8,128)(2,1)S(1)} async-done(((bf16[8,64,384]{2,1,0:T(8,128)(2,1)}), bf16[8,64,384]{2,1,0:T(8,128)(2,1)S(1)}, u32[]{:S(2)}, u32[]{:S(2)}) %all-to-all-start.1) | async-done | bytes 393248 | tf_op jit(solution)/shard_map/all_to_all | solution.py:258
  62.7 5.6 %collective-permute-start.4 = (f32[64,96]{1,0:T(8,128)S(1)}, f32[64,96]{1,0:T(8,128)S(1)}, u32[]{:S(2)}, u32[]{:S(2)}) collective-permute-start(f32[64,96]{1,0:T(8,128)S(1)} %get-tuple-element.58), channel_id=1, source_target_pairs={{0,1},{1,0},{2,3},{3,2},{4,5},{5,4},{6,7},{7,6},{8,9},{9,8},{10,11... | collective-permute-start | bytes 73736 | tf_op jit(solution)/shard_map/halo_sy/ppermute | solution.py:134
  70.9 7.7 %collective-permute-start.7 = (f32[64,96]{1,0:T(8,128)S(1)}, f32[64,96]{1,0:T(8,128)S(1)}, u32[]{:S(2)}, u32[]{:S(2)}) collective-permute-start(f32[64,96]{1,0:T(8,128)S(1)} %get-tuple-element.61), channel_id=1, source_target_pairs={{4,8},{8,4},{12,16},{16,12},{20,24},{24,20},{28,32},{32,28},{36,40... | collective-permute-start | bytes 73736 | tf_op jit(solution)/shard_map/halo_sx/ppermute | solution.py:134
  80.8 13.7 %all_to_all.83.refs_0_ = bf16[8,72,384]{2,1,0:T(8,128)(2,1)S(1)} all-to-all(bf16[8,72,384]{2,1,0:T(8,128)(2,1)S(1)} %finish.9), channel_id=1, replica_groups=mesh['freq'=8,'sx'=16,'sy'=4] {'freq'}, dimensions={0} | all-to-all | bytes 884736 | tf_op jit(solution)/shard_map/all_to_all | solution.py:258
  94.8 8.3 %all_to_all.84 = f32[4,1,64]{2,1,0:T(1,128)S(1)} all-to-all(f32[4,1,64]{2,1,0:T(1,128)S(1)} %broadcast_in_dim.123), channel_id=1, replica_groups=mesh['freq'=8,'sx'=16,'sy'=4] {'sy'}, dimensions={0} | all-to-all | bytes 2048 | tf_op jit(solution)/shard_map/all_to_all | solution.py:258
  103.7 14.8 %all-to-all-start.4 = ((f32[16,1,64]{2,1,0:T(1,128)}), f32[16,1,64]{2,1,0:T(1,128)S(1)}, u32[]{:S(2)}, u32[]{:S(2)}) async-start(f32[16,1,64]{2,1,0:T(1,128)} %broadcast_in_dim.124), calls=%async_computation.4 | async-start | bytes 16384 | tf_op jit(solution)/shard_map/all_to_all | solution.py:258
  123.9 3.6 %collective-permute-start.11 = (f32[64,96]{1,0:T(8,128)}, f32[64,96]{1,0:T(8,128)S(1)}, u32[]{:S(2)}, u32[]{:S(2)}) collective-permute-start(f32[64,96]{1,0:T(8,128)} %get-tuple-element.67), channel_id=1, source_target_pairs={{4,8},{8,4},{12,16},{16,12},{20,24},{24,20},{28,32},{32,28},{36,40... | collective-permute-start | bytes 73736 | tf_op jit(solution)/shard_map/halo_sx/ppermute | solution.py:134
  133.8 16.5 %all_to_all.85.refs_0_ = bf16[8,64,384]{2,1,0:T(8,128)(2,1)S(1)} all-to-all(bf16[8,64,384]{2,1,0:T(8,128)(2,1)S(1)} %get-tuple-element.68), channel_id=1, replica_groups=mesh['freq'=8,'sx'=16,'sy'=4] {'freq'}, dimensions={0} | all-to-all | bytes 786432 | tf_op jit(solution)/shard_map/all_to_all | solution.py:258
  152.9 5.6 %collective-permute-start.12 = (f32[64,96]{1,0:T(8,128)S(1)}, f32[64,96]{1,0:T(8,128)S(1)}, u32[]{:S(2)}, u32[]{:S(2)}) collective-permute-start(f32[64,96]{1,0:T(8,128)S(1)} %get-tuple-element.70), channel_id=1, source_target_pairs={{0,1},{1,0},{2,3},{3,2},{4,5},{5,4},{6,7},{7,6},{8,9},{9,8},{10,11... | collective-permute-start | bytes 73736 | tf_op jit(solution)/shard_map/halo_sy/ppermute | solution.py:134
  161.8 4.0 %collective-permute-start.15 = (f32[64,96]{1,0:T(8,128)S(1)}, f32[64,96]{1,0:T(8,128)S(1)}, u32[]{:S(2)}, u32[]{:S(2)}) collective-permute-start(f32[64,96]{1,0:T(8,128)S(1)} %get-tuple-element.73), channel_id=1, source_target_pairs={{4,8},{8,4},{12,16},{16,12},{20,24},{24,20},{28,32},{32,28},{36,40... | collective-permute-start | bytes 73736 | tf_op jit(solution)/shard_map/halo_sx/ppermute | solution.py:134
  167.6 13.4 %all_to_all.86.refs_0_ = bf16[8,64,384]{2,1,0:T(8,128)(2,1)S(1)} all-to-all(bf16[8,64,384]{2,1,0:T(8,128)(2,1)S(1)} %finish.11), channel_id=1, replica_groups=mesh['freq'=8,'sx'=16,'sy'=4] {'freq'}, dimensions={0} | all-to-all | bytes 786432 | tf_op jit(solution)/shard_map/all_to_all | solution.py:258
  183.4 3.7 %collective-permute-start.16 = (f32[64,96]{1,0:T(8,128)S(1)}, f32[64,96]{1,0:T(8,128)S(1)}, u32[]{:S(2)}, u32[]{:S(2)}) collective-permute-start(f32[64,96]{1,0:T(8,128)S(1)} %get-tuple-element.75), channel_id=1, source_target_pairs={{0,1},{1,0},{2,3},{3,2},{4,5},{5,4},{6,7},{7,6},{8,9},{9,8},{10,11... | collective-permute-start | bytes 73736 | tf_op jit(solution)/shard_map/halo_sy/ppermute | solution.py:134
  189.7 8.3 %collective-permute-start.19 = (f32[64,96]{1,0:T(8,128)S(1)}, f32[64,96]{1,0:T(8,128)S(1)}, u32[]{:S(2)}, u32[]{:S(2)}) collective-permute-start(f32[64,96]{1,0:T(8,128)S(1)} %get-tuple-element.78), channel_id=1, source_target_pairs={{4,8},{8,4},{12,16},{16,12},{20,24},{24,20},{28,32},{32,28},{36,40... | collective-permute-start | bytes 73736 | tf_op jit(solution)/shard_map/halo_sx/ppermute | solution.py:134
  200.1 13.1 %all_to_all.87.refs_0_ = bf16[8,64,384]{2,1,0:T(8,128)(2,1)S(1)} all-to-all(bf16[8,64,384]{2,1,0:T(8,128)(2,1)S(1)} %get-tuple-element.80), channel_id=1, replica_groups=mesh['freq'=8,'sx'=16,'sy'=4] {'freq'}, dimensions={0} | all-to-all | bytes 786432 | tf_op jit(solution)/shard_map/all_to_all | solution.py:258
  215.9 4.3 %collective-permute-start.20 = (f32[64,96]{1,0:T(8,128)S(1)}, f32[64,96]{1,0:T(8,128)S(1)}, u32[]{:S(2)}, u32[]{:S(2)}) collective-permute-start(f32[64,96]{1,0:T(8,128)S(1)} %get-tuple-element.82), channel_id=1, source_target_pairs={{0,1},{1,0},{2,3},{3,2},{4,5},{5,4},{6,7},{7,6},{8,9},{9,8},{10,11... | collective-permute-start | bytes 73736 | tf_op jit(solution)/shard_map/halo_sy/ppermute | solution.py:134
  222.8 8.5 %collective-permute-start.23 = (f32[64,96]{1,0:T(8,128)S(1)}, f32[64,96]{1,0:T(8,128)S(1)}, u32[]{:S(2)}, u32[]{:S(2)}) collective-permute-start(f32[64,96]{1,0:T(8,128)S(1)} %get-tuple-element.85), channel_id=1, source_target_pairs={{4,8},{8,4},{12,16},{16,12},{20,24},{24,20},{28,32},{32,28},{36,40... | collective-permute-start | bytes 73736 | tf_op jit(solution)/shard_map/halo_sx/ppermute | solution.py:134
  233.3 13.1 %all_to_all.88.refs_0_ = bf16[8,64,384]{2,1,0:T(8,128)(2,1)S(1)} all-to-all(bf16[8,64,384]{2,1,0:T(8,128)(2,1)S(1)} %finish.13), channel_id=1, replica_groups=mesh['freq'=8,'sx'=16,'sy'=4] {'freq'}, dimensions={0} | all-to-all | bytes 786432 | tf_op jit(solution)/shard_map/all_to_all | solution.py:258
  249.0 3.6 %collective-permute-start.24 = (f32[64,96]{1,0:T(8,128)S(1)}, f32[64,96]{1,0:T(8,128)S(1)}, u32[]{:S(2)}, u32[]{:S(2)}) collective-permute-start(f32[64,96]{1,0:T(8,128)S(1)} %get-tuple-element.87), channel_id=1, source_target_pairs={{0,1},{1,0},{2,3},{3,2},{4,5},{5,4},{6,7},{7,6},{8,9},{9,8},{10,11... | collective-permute-start | bytes 73736 | tf_op jit(solution)/shard_map/halo_sy/ppermute | solution.py:134
  255.2 8.5 %collective-permute-start.27 = (f32[64,96]{1,0:T(8,128)S(1)}, f32[64,96]{1,0:T(8,128)S(1)}, u32[]{:S(2)}, u32[]{:S(2)}) collective-permute-start(f32[64,96]{1,0:T(8,128)S(1)} %get-tuple-element.90), channel_id=1, source_target_pairs={{4,8},{8,4},{12,16},{16,12},{20,24},{24,20},{28,32},{32,28},{36,40... | collective-permute-start | bytes 73736 | tf_op jit(solution)/shard_map/halo_sx/ppermute | solution.py:134
  267.0 3.5 all-to-all-start.9
  270.7 11.5 %all-to-all-done.9.refs_0_ = bf16[8,80,384]{2,1,0:T(8,128)(2,1)S(1)} async-done(((bf16[8,80,384]{2,1,0:T(8,128)(2,1)}), bf16[8,80,384]{2,1,0:T(8,128)(2,1)S(1)}, u32[]{:S(2)}, u32[]{:S(2)}) %all-to-all-start.9) | async-done | bytes 491552 | tf_op jit(solution)/shard_map/all_to_all | solution.py:258
  284.7 9.6 %collective-permute-start.28 = (f32[64,96]{1,0:T(8,128)S(1)}, f32[64,96]{1,0:T(8,128)S(1)}, u32[]{:S(2)}, u32[]{:S(2)}) collective-permute-start(f32[64,96]{1,0:T(8,128)S(1)} %get-tuple-element.93), channel_id=1, source_target_pairs={{0,4},{4,8},{8,12},{12,16},{16,20},{20,24},{24,28},{28,32},{32,36}... | collective-permute-start | bytes 73736 | tf_op jit(solution)/shard_map/ppermute | solution.py:134
  294.3 4.2 %collective-permute-start.29 = (f32[64,96]{1,0:T(8,128)S(1)}, f32[64,96]{1,0:T(8,128)S(1)}, u32[]{:S(2)}, u32[]{:S(2)}) collective-permute-start(f32[64,96]{1,0:T(8,128)S(1)} %get-tuple-element.94), channel_id=1, source_target_pairs={{0,1},{1,2},{2,3},{4,5},{5,6},{6,7},{8,9},{9,10},{10,11},{12,13},{... | collective-permute-start | bytes 73736 | tf_op jit(solution)/shard_map/ppermute | solution.py:134
  303.8 6.4 %all-to-all-done.10 = f32[8,1,4]{2,1,0:T(1,128)S(1)} async-done(((f32[8,1,4]{2,1,0:T(1,128)}), f32[8,1,4]{2,1,0:T(1,128)S(1)}, u32[]{:S(2)}, u32[]{:S(2)}) %all-to-all-start.10) | async-done | bytes 160 | tf_op jit(solution)/shard_map/all_to_all | solution.py:258
  311.1 3.8 %all-to-all-start.11 = ((f32[4,1,40]{2,1,0:T(1,128)}), f32[4,1,40]{2,1,0:T(1,128)S(1)}, u32[]{:S(2)}, u32[]{:S(2)}) async-start(f32[4,1,40]{2,1,0:T(1,128)} %broadcast_in_dim.129), calls=%async_computation.11 | async-start | bytes 4096 | tf_op jit(solution)/shard_map/all_to_all | solution.py:258
  319.6 9.3 %all-to-all-start.12 = ((f32[16,1,40]{2,1,0:T(1,128)}), f32[16,1,40]{2,1,0:T(1,128)S(1)}, u32[]{:S(2)}, u32[]{:S(2)}) async-start(f32[16,1,40]{2,1,0:T(1,128)} %broadcast_in_dim.130), calls=%async_computation.12 | async-start | bytes 16384 | tf_op jit(solution)/shard_map/all_to_all | solution.py:258
  328.9 7.0 %all-to-all-done.12 = f32[16,1,40]{2,1,0:T(1,128)S(1)} async-done(((f32[16,1,40]{2,1,0:T(1,128)}), f32[16,1,40]{2,1,0:T(1,128)S(1)}, u32[]{:S(2)}, u32[]{:S(2)}) %all-to-all-start.12) | async-done | bytes 2592 | tf_op jit(solution)/shard_map/all_to_all | solution.py:258
  344.0 5.8 %all-to-all-done.13 = f32[8,1,216]{2,1,0:T(1,128)S(1)} async-done(((f32[8,1,216]{2,1,0:T(1,128)}), f32[8,1,216]{2,1,0:T(1,128)S(1)}, u32[]{:S(2)}, u32[]{:S(2)}) %all-to-all-start.13) | async-done | bytes 6944 | tf_op jit(solution)/shard_map/all_to_all | solution.py:258
  (168 shorter events, 96.3 us)
Async XLA Ops:
  3.5 25.5 %all-to-all-start = ((bf16[8,8,3200]{2,1,0:T(8,128)(2,1)}), bf16[8,8,3200]{2,1,0:T(8,128)(2,1)S(1)}, u32[]{:S(2)}, u32[]{:S(2)}) async-start(bf16[8,8,3200]{2,1,0:T(8,128)(2,1)} %broadcast_in_dim.117), calls=%async_computation | async-start | bytes 819200 | tf_op jit(solution)/shard_map/all_to_all | solution.py:258
  32.1 10.4 %collective-permute-start = (f32[64,96]{1,0:T(8,128)S(1)}, f32[64,96]{1,0:T(8,128)S(1)}, u32[]{:S(2)}, u32[]{:S(2)}) collective-permute-start(f32[64,96]{1,0:T(8,128)S(1)} %get-tuple-element.52), channel_id=1, source_target_pairs={{0,1},{1,0},{2,3},{3,2},{4,5},{5,4},{6,7},{7,6},{8,9},{9,8},{10,11... | collective-permute-start | bytes 73736 | tf_op jit(solution)/shard_map/halo_sy/ppermute | solution.py:134
  35.2 7.3 %collective-permute-start.1 = (f32[64,96]{1,0:T(8,128)S(1)}, f32[64,96]{1,0:T(8,128)S(1)}, u32[]{:S(2)}, u32[]{:S(2)}) collective-permute-start(f32[64,96]{1,0:T(8,128)S(1)} %get-tuple-element.53), channel_id=1, source_target_pairs={{1,2},{2,1},{5,6},{6,5},{9,10},{10,9},{13,14},{14,13},{17,18},{18,... | collective-permute-start | bytes 73736 | tf_op jit(solution)/shard_map/halo_sy/ppermute | solution.py:134
  45.5 14.7 %all-to-all-start.1 = ((bf16[8,64,384]{2,1,0:T(8,128)(2,1)}), bf16[8,64,384]{2,1,0:T(8,128)(2,1)S(1)}, u32[]{:S(2)}, u32[]{:S(2)}) async-start(bf16[8,64,384]{2,1,0:T(8,128)(2,1)} %get-tuple-element.56), calls=%async_computation.1 | async-start | bytes 786432 | tf_op jit(solution)/shard_map/all_to_all | solution.py:258
  62.7 16.1 %collective-permute-start.4 = (f32[64,96]{1,0:T(8,128)S(1)}, f32[64,96]{1,0:T(8,128)S(1)}, u32[]{:S(2)}, u32[]{:S(2)}) collective-permute-start(f32[64,96]{1,0:T(8,128)S(1)} %get-tuple-element.58), channel_id=1, source_target_pairs={{0,1},{1,0},{2,3},{3,2},{4,5},{5,4},{6,7},{7,6},{8,9},{9,8},{10,11... | collective-permute-start | bytes 73736 | tf_op jit(solution)/shard_map/halo_sy/ppermute | solution.py:134
  68.3 10.5 %collective-permute-start.5 = (f32[64,96]{1,0:T(8,128)S(1)}, f32[64,96]{1,0:T(8,128)S(1)}, u32[]{:S(2)}, u32[]{:S(2)}) collective-permute-start(f32[64,96]{1,0:T(8,128)S(1)} %get-tuple-element.59), channel_id=1, source_target_pairs={{1,2},{2,1},{5,6},{6,5},{9,10},{10,9},{13,14},{14,13},{17,18},{18,... | collective-permute-start | bytes 73736 | tf_op jit(solution)/shard_map/halo_sy/ppermute | solution.py:134
  69.0 9.9 %collective-permute-start.6 = (f32[64,96]{1,0:T(8,128)S(1)}, f32[64,96]{1,0:T(8,128)S(1)}, u32[]{:S(2)}, u32[]{:S(2)}) collective-permute-start(f32[64,96]{1,0:T(8,128)S(1)} %get-tuple-element.60), channel_id=1, source_target_pairs={{0,4},{4,0},{8,12},{12,8},{16,20},{20,16},{24,28},{28,24},{32,36},... | collective-permute-start | bytes 73736 | tf_op jit(solution)/shard_map/halo_sx/ppermute | solution.py:134
  70.9 9.5 %collective-permute-start.7 = (f32[64,96]{1,0:T(8,128)S(1)}, f32[64,96]{1,0:T(8,128)S(1)}, u32[]{:S(2)}, u32[]{:S(2)}) collective-permute-start(f32[64,96]{1,0:T(8,128)S(1)} %get-tuple-element.61), channel_id=1, source_target_pairs={{4,8},{8,4},{12,16},{16,12},{20,24},{24,20},{28,32},{32,28},{36,40... | collective-permute-start | bytes 73736 | tf_op jit(solution)/shard_map/halo_sx/ppermute | solution.py:134
  103.7 26.6 %all-to-all-start.4 = ((f32[16,1,64]{2,1,0:T(1,128)}), f32[16,1,64]{2,1,0:T(1,128)S(1)}, u32[]{:S(2)}, u32[]{:S(2)}) async-start(f32[16,1,64]{2,1,0:T(1,128)} %broadcast_in_dim.124), calls=%async_computation.4 | async-start | bytes 16384 | tf_op jit(solution)/shard_map/all_to_all | solution.py:258
  121.9 8.8 %collective-permute-start.10 = (f32[64,96]{1,0:T(8,128)}, f32[64,96]{1,0:T(8,128)S(1)}, u32[]{:S(2)}, u32[]{:S(2)}) collective-permute-start(f32[64,96]{1,0:T(8,128)} %get-tuple-element.66), channel_id=1, source_target_pairs={{0,4},{4,0},{8,12},{12,8},{16,20},{20,16},{24,28},{28,24},{32,36},... | collective-permute-start | bytes 73736 | tf_op jit(solution)/shard_map/halo_sx/ppermute | solution.py:134
  123.9 6.8 %collective-permute-start.11 = (f32[64,96]{1,0:T(8,128)}, f32[64,96]{1,0:T(8,128)S(1)}, u32[]{:S(2)}, u32[]{:S(2)}) collective-permute-start(f32[64,96]{1,0:T(8,128)} %get-tuple-element.67), channel_id=1, source_target_pairs={{4,8},{8,4},{12,16},{16,12},{20,24},{24,20},{28,32},{32,28},{36,40... | collective-permute-start | bytes 73736 | tf_op jit(solution)/shard_map/halo_sx/ppermute | solution.py:134
  152.9 12.9 %collective-permute-start.12 = (f32[64,96]{1,0:T(8,128)S(1)}, f32[64,96]{1,0:T(8,128)S(1)}, u32[]{:S(2)}, u32[]{:S(2)}) collective-permute-start(f32[64,96]{1,0:T(8,128)S(1)} %get-tuple-element.70), channel_id=1, source_target_pairs={{0,1},{1,0},{2,3},{3,2},{4,5},{5,4},{6,7},{7,6},{8,9},{9,8},{10,11... | collective-permute-start | bytes 73736 | tf_op jit(solution)/shard_map/halo_sy/ppermute | solution.py:134
  158.6 7.3 %collective-permute-start.13 = (f32[64,96]{1,0:T(8,128)S(1)}, f32[64,96]{1,0:T(8,128)S(1)}, u32[]{:S(2)}, u32[]{:S(2)}) collective-permute-start(f32[64,96]{1,0:T(8,128)S(1)} %get-tuple-element.71), channel_id=1, source_target_pairs={{1,2},{2,1},{5,6},{6,5},{9,10},{10,9},{13,14},{14,13},{17,18},{18,... | collective-permute-start | bytes 73736 | tf_op jit(solution)/shard_map/halo_sy/ppermute | solution.py:134
  159.2 6.6 %collective-permute-start.14 = (f32[64,96]{1,0:T(8,128)S(1)}, f32[64,96]{1,0:T(8,128)S(1)}, u32[]{:S(2)}, u32[]{:S(2)}) collective-permute-start(f32[64,96]{1,0:T(8,128)S(1)} %get-tuple-element.72), channel_id=1, source_target_pairs={{0,4},{4,0},{8,12},{12,8},{16,20},{20,16},{24,28},{28,24},{32,36},... | collective-permute-start | bytes 73736 | tf_op jit(solution)/shard_map/halo_sx/ppermute | solution.py:134
  183.4 14.6 %collective-permute-start.16 = (f32[64,96]{1,0:T(8,128)S(1)}, f32[64,96]{1,0:T(8,128)S(1)}, u32[]{:S(2)}, u32[]{:S(2)}) collective-permute-start(f32[64,96]{1,0:T(8,128)S(1)} %get-tuple-element.75), channel_id=1, source_target_pairs={{0,1},{1,0},{2,3},{3,2},{4,5},{5,4},{6,7},{7,6},{8,9},{9,8},{10,11... | collective-permute-start | bytes 73736 | tf_op jit(solution)/shard_map/halo_sy/ppermute | solution.py:134
  187.1 11.0 %collective-permute-start.17 = (f32[64,96]{1,0:T(8,128)S(1)}, f32[64,96]{1,0:T(8,128)S(1)}, u32[]{:S(2)}, u32[]{:S(2)}) collective-permute-start(f32[64,96]{1,0:T(8,128)S(1)} %get-tuple-element.76), channel_id=1, source_target_pairs={{1,2},{2,1},{5,6},{6,5},{9,10},{10,9},{13,14},{14,13},{17,18},{18,... | collective-permute-start | bytes 73736 | tf_op jit(solution)/shard_map/halo_sy/ppermute | solution.py:134
  187.8 10.3 %collective-permute-start.18 = (f32[64,96]{1,0:T(8,128)S(1)}, f32[64,96]{1,0:T(8,128)S(1)}, u32[]{:S(2)}, u32[]{:S(2)}) collective-permute-start(f32[64,96]{1,0:T(8,128)S(1)} %get-tuple-element.77), channel_id=1, source_target_pairs={{0,4},{4,0},{8,12},{12,8},{16,20},{20,16},{24,28},{28,24},{32,36},... | collective-permute-start | bytes 73736 | tf_op jit(solution)/shard_map/halo_sx/ppermute | solution.py:134
  189.7 10.2 %collective-permute-start.19 = (f32[64,96]{1,0:T(8,128)S(1)}, f32[64,96]{1,0:T(8,128)S(1)}, u32[]{:S(2)}, u32[]{:S(2)}) collective-permute-start(f32[64,96]{1,0:T(8,128)S(1)} %get-tuple-element.78), channel_id=1, source_target_pairs={{4,8},{8,4},{12,16},{16,12},{20,24},{24,20},{28,32},{32,28},{36,40... | collective-permute-start | bytes 73736 | tf_op jit(solution)/shard_map/halo_sx/ppermute | solution.py:134
  215.9 15.5 %collective-permute-start.20 = (f32[64,96]{1,0:T(8,128)S(1)}, f32[64,96]{1,0:T(8,128)S(1)}, u32[]{:S(2)}, u32[]{:S(2)}) collective-permute-start(f32[64,96]{1,0:T(8,128)S(1)} %get-tuple-element.82), channel_id=1, source_target_pairs={{0,1},{1,0},{2,3},{3,2},{4,5},{5,4},{6,7},{7,6},{8,9},{9,8},{10,11... | collective-permute-start | bytes 73736 | tf_op jit(solution)/shard_map/halo_sy/ppermute | solution.py:134
  220.2 11.1 %collective-permute-start.21 = (f32[64,96]{1,0:T(8,128)S(1)}, f32[64,96]{1,0:T(8,128)S(1)}, u32[]{:S(2)}, u32[]{:S(2)}) collective-permute-start(f32[64,96]{1,0:T(8,128)S(1)} %get-tuple-element.83), channel_id=1, source_target_pairs={{1,2},{2,1},{5,6},{6,5},{9,10},{10,9},{13,14},{14,13},{17,18},{18,... | collective-permute-start | bytes 73736 | tf_op jit(solution)/shard_map/halo_sy/ppermute | solution.py:134
  220.9 10.5 %collective-permute-start.22 = (f32[64,96]{1,0:T(8,128)S(1)}, f32[64,96]{1,0:T(8,128)S(1)}, u32[]{:S(2)}, u32[]{:S(2)}) collective-permute-start(f32[64,96]{1,0:T(8,128)S(1)} %get-tuple-element.84), channel_id=1, source_target_pairs={{0,4},{4,0},{8,12},{12,8},{16,20},{20,16},{24,28},{28,24},{32,36},... | collective-permute-start | bytes 73736 | tf_op jit(solution)/shard_map/halo_sx/ppermute | solution.py:134
  222.8 10.4 %collective-permute-start.23 = (f32[64,96]{1,0:T(8,128)S(1)}, f32[64,96]{1,0:T(8,128)S(1)}, u32[]{:S(2)}, u32[]{:S(2)}) collective-permute-start(f32[64,96]{1,0:T(8,128)S(1)} %get-tuple-element.85), channel_id=1, source_target_pairs={{4,8},{8,4},{12,16},{16,12},{20,24},{24,20},{28,32},{32,28},{36,40... | collective-permute-start | bytes 73736 | tf_op jit(solution)/shard_map/halo_sx/ppermute | solution.py:134
  249.0 14.8 %collective-permute-start.24 = (f32[64,96]{1,0:T(8,128)S(1)}, f32[64,96]{1,0:T(8,128)S(1)}, u32[]{:S(2)}, u32[]{:S(2)}) collective-permute-start(f32[64,96]{1,0:T(8,128)S(1)} %get-tuple-element.87), channel_id=1, source_target_pairs={{0,1},{1,0},{2,3},{3,2},{4,5},{5,4},{6,7},{7,6},{8,9},{9,8},{10,11... | collective-permute-start | bytes 73736 | tf_op jit(solution)/shard_map/halo_sy/ppermute | solution.py:134
  252.6 11.1 %collective-permute-start.25 = (f32[64,96]{1,0:T(8,128)S(1)}, f32[64,96]{1,0:T(8,128)S(1)}, u32[]{:S(2)}, u32[]{:S(2)}) collective-permute-start(f32[64,96]{1,0:T(8,128)S(1)} %get-tuple-element.88), channel_id=1, source_target_pairs={{1,2},{2,1},{5,6},{6,5},{9,10},{10,9},{13,14},{14,13},{17,18},{18,... | collective-permute-start | bytes 73736 | tf_op jit(solution)/shard_map/halo_sy/ppermute | solution.py:134
  253.3 10.5 %collective-permute-start.26 = (f32[64,96]{1,0:T(8,128)S(1)}, f32[64,96]{1,0:T(8,128)S(1)}, u32[]{:S(2)}, u32[]{:S(2)}) collective-permute-start(f32[64,96]{1,0:T(8,128)S(1)} %get-tuple-element.89), channel_id=1, source_target_pairs={{0,4},{4,0},{8,12},{12,8},{16,20},{20,16},{24,28},{28,24},{32,36},... | collective-permute-start | bytes 73736 | tf_op jit(solution)/shard_map/halo_sx/ppermute | solution.py:134
  255.2 10.3 %collective-permute-start.27 = (f32[64,96]{1,0:T(8,128)S(1)}, f32[64,96]{1,0:T(8,128)S(1)}, u32[]{:S(2)}, u32[]{:S(2)}) collective-permute-start(f32[64,96]{1,0:T(8,128)S(1)} %get-tuple-element.90), channel_id=1, source_target_pairs={{4,8},{8,4},{12,16},{16,12},{20,24},{24,20},{28,32},{32,28},{36,40... | collective-permute-start | bytes 73736 | tf_op jit(solution)/shard_map/halo_sx/ppermute | solution.py:134
  267.0 15.2 %all-to-all-start.9 = ((bf16[8,80,384]{2,1,0:T(8,128)(2,1)}), bf16[8,80,384]{2,1,0:T(8,128)(2,1)S(1)}, u32[]{:S(2)}, u32[]{:S(2)}) async-start(bf16[8,80,384]{2,1,0:T(8,128)(2,1)} %finish.14), calls=%async_computation.9 | async-start | bytes 983040 | tf_op jit(solution)/shard_map/all_to_all | solution.py:258
  284.7 14.0 %collective-permute-start.28 = (f32[64,96]{1,0:T(8,128)S(1)}, f32[64,96]{1,0:T(8,128)S(1)}, u32[]{:S(2)}, u32[]{:S(2)}) collective-permute-start(f32[64,96]{1,0:T(8,128)S(1)} %get-tuple-element.93), channel_id=1, source_target_pairs={{0,4},{4,8},{8,12},{12,16},{16,20},{20,24},{24,28},{28,32},{32,36}... | collective-permute-start | bytes 73736 | tf_op jit(solution)/shard_map/ppermute | solution.py:134
  300.4 9.7 %all-to-all-start.10 = ((f32[8,1,4]{2,1,0:T(1,128)}), f32[8,1,4]{2,1,0:T(1,128)S(1)}, u32[]{:S(2)}, u32[]{:S(2)}) async-start(f32[8,1,4]{2,1,0:T(1,128)} %bitcast.27), calls=%async_computation.10 | async-start | bytes 8192 | tf_op jit(solution)/shard_map/all_to_all | solution.py:258
  311.1 7.9 %all-to-all-start.11 = ((f32[4,1,40]{2,1,0:T(1,128)}), f32[4,1,40]{2,1,0:T(1,128)S(1)}, u32[]{:S(2)}, u32[]{:S(2)}) async-start(f32[4,1,40]{2,1,0:T(1,128)} %broadcast_in_dim.129), calls=%async_computation.11 | async-start | bytes 4096 | tf_op jit(solution)/shard_map/all_to_all | solution.py:258
  319.6 16.3 %all-to-all-start.12 = ((f32[16,1,40]{2,1,0:T(1,128)}), f32[16,1,40]{2,1,0:T(1,128)S(1)}, u32[]{:S(2)}, u32[]{:S(2)}) async-start(f32[16,1,40]{2,1,0:T(1,128)} %broadcast_in_dim.130), calls=%async_computation.12 | async-start | bytes 16384 | tf_op jit(solution)/shard_map/all_to_all | solution.py:258
  340.0 9.8 %all-to-all-start.13 = ((f32[8,1,216]{2,1,0:T(1,128)}), f32[8,1,216]{2,1,0:T(1,128)S(1)}, u32[]{:S(2)}, u32[]{:S(2)}) async-start(f32[8,1,216]{2,1,0:T(1,128)} %all_to_all.68), calls=%async_computation.13 | async-start | bytes 16384 | tf_op jit(solution)/shard_map/all_to_all | solution.py:258
  (16 other events, 127.1 us)

commit v5 on v3

--- a/solution.py
+++ b/solution.py
@@ -31,19 +31,19 @@
     for at, ref in enumerate((stiff_ref, mass_ref)):
         rows = ref[...].reshape(faces * run, width)
         moved = jnp.dot(rows, order_ref[...], preferred_element_type=F32)
-        out_ref[0, :, at * width : (at + 1) * width] = moved.astype(BF)
-
-
-def arrange(stiffness, mass_matrix, faces, n_freq):
+        out_ref[:, at * width : (at + 1) * width] = moved.astype(BF)
+
+
+def arrange(stiffness, mass_matrix, faces, n_freq, first, count):
     order, width = stiffness.shape
     run = order // (faces * n_freq)
-    block = pl.BlockSpec((faces, 1, run, width), lambda d: (0, d, 0, 0))
+    block = pl.BlockSpec((faces, 1, run, width), lambda d: (0, first + d, 0, 0))
     return pl.pallas_call(
         arrange_kernel,
-        grid=(n_freq,),
+        grid=(count,),
         in_specs=[block, block],
-        out_specs=pl.BlockSpec((1, width, 2 * width), lambda d: (d, 0, 0)),
-        out_shape=jax.ShapeDtypeStruct((n_freq, width, 2 * width), BF),
+        out_specs=pl.BlockSpec((width, 2 * width), lambda d: (d, 0)),
+        out_shape=jax.ShapeDtypeStruct((count * width, 2 * width), BF),
         scratch_shapes=[pltpu.VMEM((width, width), BF)],
         compiler_params=params(),
         name="arrange",
@@ -58,27 +58,37 @@
 
 
 def apply_kernel(sign, faces, by_slot, sides, *refs):
-    field_ref, pair_ref, omega_ref, odd_ref, local_ref = refs[:5]
-    face_refs = refs[5:-2]
+    field_ref, near_ref, far_ref, omega_ref, odd_ref, local_ref = refs[:6]
+    face_refs = refs[6:-2]
     held_ref, sems = refs[-2:]
-    n_freq = pair_ref.shape[0]
     count, width = local_ref.shape
-    copies = [
-        pltpu.make_async_copy(pair_ref.at[d], held_ref.at[d], sems.at[d]) for d in range(n_freq)
-    ]
-    for copy in copies:
-        copy.start()
-    total_sum = None
-    for d in range(n_freq):
+    half = near_ref.shape[0] // width
+    block = min(2, half)
+    copies = []
+    for at in range(0, half, block):
+        rows = pl.ds(at * width, block * width)
+        copies.append(pltpu.make_async_copy(far_ref.at[rows], held_ref.at[rows], sems.at[at]))
+        copies[-1].start()
+
+    def rows_of(first):
         if by_slot:
-            rows = field_ref[:, :, d * width : (d + 1) * width].reshape(count, width)
-        else:
-            rows = field_ref[d, :count, :]
-        copies[d].wait()
-        product = jnp.dot(rows, held_ref[d], preferred_element_type=F32)
-        total_sum = product if total_sum is None else total_sum + product
-    stiff_part = total_sum[:, :width]
-    mass_part = total_sum[:, width:]
+            taken = field_ref[:, :, first * width : (first + block) * width]
+            return taken.reshape(count, block * width)
+        return jnp.concatenate([field_ref[first + k, :count, :] for k in range(block)], axis=1)
+
+    result = None
+    for first in range(0, 2 * half, block):
+        ref, at = (near_ref, first) if first < half else (held_ref, first - half)
+        if first >= half:
+            copies[at // block].wait()
+        part = jnp.dot(
+            rows_of(first),
+            ref[at * width : (at + block) * width, :],
+            preferred_element_type=F32,
+        )
+        result = part if result is None else result + part
+    stiff_part = result[:, :width]
+    mass_part = result[:, width:]
     row = lax.broadcasted_iota(jnp.int32, (count, width), 0)
     real = lax.rem(row, 8) < 4
     other = jnp.where(
@@ -100,7 +110,8 @@
 
 
 def apply_local(field, pair, omega_rows, odd, sign, faces, by_slot=False, sides=False):
-    n_freq, width, double = pair.shape
+    length, double = pair[0].shape
+    width = double // 2
     count = omega_rows.shape[0]
     run = width // faces
     n_out = 2 if sides else faces
@@ -108,6 +119,7 @@
     return pl.pallas_call(
         functools.partial(apply_kernel, sign, faces, by_slot, sides),
         in_specs=[
+            vmem,
             vmem,
             pl.BlockSpec(memory_space=pltpu.HBM),
             vmem,
@@ -117,12 +129,12 @@
         out_shape=[jax.ShapeDtypeStruct((count, width), F32)]
         + [jax.ShapeDtypeStruct((count, run), F32)] * n_out,
         scratch_shapes=[
-            pltpu.VMEM((n_freq, width, double), BF),
-            pltpu.SemaphoreType.DMA((n_freq,)),
+            pltpu.VMEM((length, double), BF),
+            pltpu.SemaphoreType.DMA((length // width,)),
         ],
         compiler_params=params(),
         name="apply_local",
-    )(field, pair, omega_rows, odd)
+    )(field, *pair, omega_rows, odd)
 
 
 def permute(values, axis, pairs):
@@ -130,13 +142,14 @@
 
 
 def swap_faces(face_vals):
-    out = []
+    out = {}
     for axis, (near, far) in (("sx", face_vals[:2]), ("sy", face_vals[2:])):
         count = lax.axis_size(axis)
         low = [(i, i ^ 1) for i in range(count)]
         high = [(i, ((i + 1) ^ 1) - 1) for i in range(1, count - 1)]
-        out += [permute(near, axis, low), permute(far, axis, high)]
-    return out
+        with jax.named_scope("halo_" + axis):
+            out[axis] = [permute(near, axis, low), permute(far, axis, high)]
+    return out["sx"] + out["sy"]
 
 
 def pass_faces(face_vals):
@@ -310,8 +323,13 @@
     tags = jnp.broadcast_to(assignment.astype(BF)[None, :], (2, slots)).reshape(own, 1)
     packet = jnp.concatenate([load, jnp.broadcast_to(tags, (own, 128))], axis=1)
     field = exchange(jnp.broadcast_to(packet[None], (n_freq, *packet.shape)), "freq")
-    pair = arrange(stiffness[0, 0], mass_matrix[0, 0], faces, n_freq)
-    pair = pltpu.with_memory_space_constraint(pair, pltpu.HBM)
+    half = n_freq // 2
+    pair = tuple(
+        pltpu.with_memory_space_constraint(
+            arrange(stiffness[0, 0], mass_matrix[0, 0], faces, n_freq, first, half), place
+        )
+        for first, place in ((0, pltpu.VMEM), (half, pltpu.HBM))
+    )
     slot_tags = field[:, :, order].reshape(count).astype(jnp.int32)
     matches = slot_tags[:, None] == jnp.arange(omega_table.shape[0], dtype=jnp.int32)[None, :]
     omega_rows = jnp.sum(jnp.where(matches, omega_table[None, :], 0.0), axis=1, keepdims=True)
@@ -378,10 +396,13 @@
         local, pass_faces(face_vals), odd, n_freq, faces, products=((0, 0),), weight=weight_once,
         keep=False, send=False,
     )
-    sums = jnp.sum(exchange(by_slots(sums, 1)[0], "freq"), axis=0)
-    others = lax.dynamic_index_in_dim(freq_sums(sent3, len(keys)), me, 1, keepdims=False)
-    sums = jnp.concatenate([others, sums[None]], axis=0).reshape(-1)
-    sums = total(total(sums, "sy"), "sx").reshape(len(keys) + 1, slots)
+    sums = jnp.concatenate([freq_sums(sent3, len(keys)) / n_freq, by_slots(sums, 1)], axis=0)
+    sums = jnp.swapaxes(sums, 0, 1).reshape(n_freq, 1, (len(keys) + 1) * slots)
+    size_y = lax.axis_size("sy")
+    sums = jnp.broadcast_to(sums, (n_freq, size_y, sums.shape[2]))
+    sums = sums.reshape(n_freq * size_y, sums.shape[2])
+    sums = jnp.sum(exchange(sums, ("freq", "sy")), axis=0)
+    sums = total(sums, "sx").reshape(len(keys) + 1, slots)
     own_gamma = lax.dynamic_index_in_dim(gamma0, me, 0, keepdims=False)
     own_delta = lax.dynamic_index_in_dim(delta0, me, 0, keepdims=False)
     theta = own_delta / own_gamma

time: 344 us -> 336 us (0.977)
  Pallas kernels: 30.8 us -> 26.7 us
  starting transfers between devices: 153 us -> 149 us
    pallas_call x8, Pallas kernels: 22.5 us -> 18.2 us  [apply_local(): pl.pallas_call(functools.partial(apply_kernel, sign, faces, by_slot, side...]
    all_to_all x8 -> x7, starting transfers between devices: 43.4 us -> 39.4 us  [exchange(): return lax.all_to_all(blocks, axis, 0, 0, tiled=False)]
    all_to_all x8 -> x7, waiting for transfers between devices: 53.1 us -> 51.7 us  [exchange(): return lax.all_to_all(blocks, axis, 0, 0, tiled=False)]
  transfers between devices with their start and end apart: 38 -> 37, of which waited for: 15 -> 14; matrix products, arithmetic and copies ran while one was open for 1% -> 0% of each run, Pallas kernels for 2% -> 2%
where the time goes in v5:
time: 336 us; the launch traced here: 334 us
  starting transfers between devices  149 us (44%)
  blocking collectives  80.3 us (24%)
  waiting for transfers between devices  58.5 us (17%)
  Pallas kernels  26.7 us (8%)
  local copies, waits for them, and re-layouts  13 us (4%)
  other arithmetic  4.97 us (1%)
    ppermute x30, starting transfers between devices, permute(): lax.ppermute(values, axis, pairs)  109 us
    all_to_all x6, blocking collectives, exchange(): return lax.all_to_all(blocks, axis, 0, 0, tiled=False)  80.3 us
    all_to_all x7, waiting for transfers between devices, exchange(): return lax.all_to_all(blocks, axis, 0, 0, tiled=False)  51.7 us
    all_to_all x7, starting transfers between devices, exchange(): return lax.all_to_all(blocks, axis, 0, 0, tiled=False)  39.4 us
    pallas_call x8, Pallas kernels, apply_local(): pl.pallas_call(functools.partial(apply_kernel, sign, faces, by_slot, side...  18.2 us
    ppermute x30, waiting for transfers between devices, permute(): lax.ppermute(values, axis, pairs)  6.74 us
  transfers between devices with their start and end apart: 37, of which 14 were waited for; matrix products, arithmetic and copies ran while one was open for 0% of the time, Pallas kernels for 2%

profile of v5, /device:TPU:1, one launch (start us, length us, event | category | flops | bytes accessed | tf_op | source)
XLA Modules:
  0.0 334.3 jit_solution(13525849962915481397)
XLA Ops:
  3.5 10.9 %all-to-all-start = ((bf16[8,8,3200]{2,1,0:T(8,128)(2,1)}), bf16[8,8,3200]{2,1,0:T(8,128)(2,1)S(1)}, u32[]{:S(2)}, u32[]{:S(2)}) async-start(bf16[8,8,3200]{2,1,0:T(8,128)(2,1)} %broadcast_in_dim.114), calls=%async_computation | async-start | bytes 819200 | tf_op jit(solution)/shard_map/all_to_all | solution.py:265
  24.2 4.8 %all-to-all-done.refs_0_ = bf16[8,8,3200]{2,1,0:T(8,128)(2,1)S(1)} async-done(((bf16[8,8,3200]{2,1,0:T(8,128)(2,1)}), bf16[8,8,3200]{2,1,0:T(8,128)(2,1)S(1)}, u32[]{:S(2)}, u32[]{:S(2)}) %all-to-all-start) | async-done | bytes 409632 | tf_op jit(solution)/shard_map/all_to_all | solution.py:265
  43.6 3.5 %all-to-all-start.1 = ((bf16[8,64,384]{2,1,0:T(8,128)(2,1)}), bf16[8,64,384]{2,1,0:T(8,128)(2,1)S(1)}, u32[]{:S(2)}, u32[]{:S(2)}) async-start(bf16[8,64,384]{2,1,0:T(8,128)(2,1)} %get-tuple-element.52), calls=%async_computation.1 | async-start | bytes 786432 | tf_op jit(solution)/shard_map/all_to_all | solution.py:265
  47.1 14.1 %all-to-all-done.1.refs_0_ = bf16[8,64,384]{2,1,0:T(8,128)(2,1)S(1)} async-done(((bf16[8,64,384]{2,1,0:T(8,128)(2,1)}), bf16[8,64,384]{2,1,0:T(8,128)(2,1)S(1)}, u32[]{:S(2)}, u32[]{:S(2)}) %all-to-all-start.1) | async-done | bytes 393248 | tf_op jit(solution)/shard_map/all_to_all | solution.py:265
  65.7 4.4 %collective-permute-start.5 = (f32[64,96]{1,0:T(8,128)S(1)}, f32[64,96]{1,0:T(8,128)S(1)}, u32[]{:S(2)}, u32[]{:S(2)}) collective-permute-start(f32[64,96]{1,0:T(8,128)S(1)} %get-tuple-element.55), channel_id=1, source_target_pairs={{4,8},{8,4},{12,16},{16,12},{20,24},{24,20},{28,32},{32,28},{36,40... | collective-permute-start | bytes 73736 | tf_op jit(solution)/shard_map/halo_sx/ppermute | solution.py:141
  70.1 5.7 %collective-permute-start.6 = (f32[64,96]{1,0:T(8,128)S(1)}, f32[64,96]{1,0:T(8,128)S(1)}, u32[]{:S(2)}, u32[]{:S(2)}) collective-permute-start(f32[64,96]{1,0:T(8,128)S(1)} %get-tuple-element.56), channel_id=1, source_target_pairs={{0,1},{1,0},{2,3},{3,2},{4,5},{5,4},{6,7},{7,6},{8,9},{9,8},{10,11... | collective-permute-start | bytes 73736 | tf_op jit(solution)/shard_map/halo_sy/ppermute | solution.py:141
  77.5 16.1 %all_to_all.77.refs_0_ = bf16[8,72,384]{2,1,0:T(8,128)(2,1)S(1)} all-to-all(bf16[8,72,384]{2,1,0:T(8,128)(2,1)S(1)} %finish.9), channel_id=1, replica_groups=mesh['freq'=8,'sx'=16,'sy'=4] {'freq'}, dimensions={0} | all-to-all | bytes 884736 | tf_op jit(solution)/shard_map/all_to_all | solution.py:265
  93.9 11.0 %all_to_all.78 = f32[4,1,64]{2,1,0:T(1,128)S(1)} all-to-all(f32[4,1,64]{2,1,0:T(1,128)S(1)} %broadcast_in_dim.120), channel_id=1, replica_groups=mesh['freq'=8,'sx'=16,'sy'=4] {'sy'}, dimensions={0} | all-to-all | bytes 2048 | tf_op jit(solution)/shard_map/all_to_all | solution.py:265
  105.6 8.9 %all-to-all-start.4 = ((f32[16,1,64]{2,1,0:T(1,128)}), f32[16,1,64]{2,1,0:T(1,128)S(1)}, u32[]{:S(2)}, u32[]{:S(2)}) async-start(f32[16,1,64]{2,1,0:T(1,128)} %broadcast_in_dim.121), calls=%async_computation.4 | async-start | bytes 16384 | tf_op jit(solution)/shard_map/all_to_all | solution.py:265
  122.7 3.4 %collective-permute-start.9 = (f32[64,96]{1,0:T(8,128)}, f32[64,96]{1,0:T(8,128)S(1)}, u32[]{:S(2)}, u32[]{:S(2)}) collective-permute-start(f32[64,96]{1,0:T(8,128)} %get-tuple-element.61), channel_id=1, source_target_pairs={{4,8},{8,4},{12,16},{16,12},{20,24},{24,20},{28,32},{32,28},{36,40... | collective-permute-start | bytes 73736 | tf_op jit(solution)/shard_map/halo_sx/ppermute | solution.py:141
  129.6 13.7 %all_to_all.79.refs_0_ = bf16[8,64,384]{2,1,0:T(8,128)(2,1)S(1)} all-to-all(bf16[8,64,384]{2,1,0:T(8,128)(2,1)S(1)} %get-tuple-element.64), channel_id=1, replica_groups=mesh['freq'=8,'sx'=16,'sy'=4] {'freq'}, dimensions={0} | all-to-all | bytes 786432 | tf_op jit(solution)/shard_map/all_to_all | solution.py:265
  147.6 7.8 %collective-permute-start.13 = (f32[64,96]{1,0:T(8,128)S(1)}, f32[64,96]{1,0:T(8,128)S(1)}, u32[]{:S(2)}, u32[]{:S(2)}) collective-permute-start(f32[64,96]{1,0:T(8,128)S(1)} %get-tuple-element.67), channel_id=1, source_target_pairs={{4,8},{8,4},{12,16},{16,12},{20,24},{24,20},{28,32},{32,28},{36,40... | collective-permute-start | bytes 73736 | tf_op jit(solution)/shard_map/halo_sx/ppermute | solution.py:141
  155.4 4.9 %collective-permute-start.14 = (f32[64,96]{1,0:T(8,128)S(1)}, f32[64,96]{1,0:T(8,128)S(1)}, u32[]{:S(2)}, u32[]{:S(2)}) collective-permute-start(f32[64,96]{1,0:T(8,128)S(1)} %get-tuple-element.68), channel_id=1, source_target_pairs={{0,1},{1,0},{2,3},{3,2},{4,5},{5,4},{6,7},{7,6},{8,9},{9,8},{10,11... | collective-permute-start | bytes 73736 | tf_op jit(solution)/shard_map/halo_sy/ppermute | solution.py:141
  161.7 13.1 %all_to_all.80.refs_0_ = bf16[8,64,384]{2,1,0:T(8,128)(2,1)S(1)} all-to-all(bf16[8,64,384]{2,1,0:T(8,128)(2,1)S(1)} %finish.11), channel_id=1, replica_groups=mesh['freq'=8,'sx'=16,'sy'=4] {'freq'}, dimensions={0} | all-to-all | bytes 786432 | tf_op jit(solution)/shard_map/all_to_all | solution.py:265
  178.9 8.0 %collective-permute-start.17 = (f32[64,96]{1,0:T(8,128)S(1)}, f32[64,96]{1,0:T(8,128)S(1)}, u32[]{:S(2)}, u32[]{:S(2)}) collective-permute-start(f32[64,96]{1,0:T(8,128)S(1)} %get-tuple-element.72), channel_id=1, source_target_pairs={{4,8},{8,4},{12,16},{16,12},{20,24},{24,20},{28,32},{32,28},{36,40... | collective-permute-start | bytes 73736 | tf_op jit(solution)/shard_map/halo_sx/ppermute | solution.py:141
  186.9 5.3 %collective-permute-start.18 = (f32[64,96]{1,0:T(8,128)S(1)}, f32[64,96]{1,0:T(8,128)S(1)}, u32[]{:S(2)}, u32[]{:S(2)}) collective-permute-start(f32[64,96]{1,0:T(8,128)S(1)} %get-tuple-element.73), channel_id=1, source_target_pairs={{0,1},{1,0},{2,3},{3,2},{4,5},{5,4},{6,7},{7,6},{8,9},{9,8},{10,11... | collective-permute-start | bytes 73736 | tf_op jit(solution)/shard_map/halo_sy/ppermute | solution.py:141
  193.9 13.1 %all_to_all.81.refs_0_ = bf16[8,64,384]{2,1,0:T(8,128)(2,1)S(1)} all-to-all(bf16[8,64,384]{2,1,0:T(8,128)(2,1)S(1)} %get-tuple-element.76), channel_id=1, replica_groups=mesh['freq'=8,'sx'=16,'sy'=4] {'freq'}, dimensions={0} | all-to-all | bytes 786432 | tf_op jit(solution)/shard_map/all_to_all | solution.py:265
  211.2 8.0 %collective-permute-start.21 = (f32[64,96]{1,0:T(8,128)S(1)}, f32[64,96]{1,0:T(8,128)S(1)}, u32[]{:S(2)}, u32[]{:S(2)}) collective-permute-start(f32[64,96]{1,0:T(8,128)S(1)} %get-tuple-element.79), channel_id=1, source_target_pairs={{4,8},{8,4},{12,16},{16,12},{20,24},{24,20},{28,32},{32,28},{36,40... | collective-permute-start | bytes 73736 | tf_op jit(solution)/shard_map/halo_sx/ppermute | solution.py:141
  219.2 5.4 %collective-permute-start.22 = (f32[64,96]{1,0:T(8,128)S(1)}, f32[64,96]{1,0:T(8,128)S(1)}, u32[]{:S(2)}, u32[]{:S(2)}) collective-permute-start(f32[64,96]{1,0:T(8,128)S(1)} %get-tuple-element.80), channel_id=1, source_target_pairs={{0,1},{1,0},{2,3},{3,2},{4,5},{5,4},{6,7},{7,6},{8,9},{9,8},{10,11... | collective-permute-start | bytes 73736 | tf_op jit(solution)/shard_map/halo_sy/ppermute | solution.py:141
  226.2 13.1 %all_to_all.82.refs_0_ = bf16[8,64,384]{2,1,0:T(8,128)(2,1)S(1)} all-to-all(bf16[8,64,384]{2,1,0:T(8,128)(2,1)S(1)} %finish.13), channel_id=1, replica_groups=mesh['freq'=8,'sx'=16,'sy'=4] {'freq'}, dimensions={0} | all-to-all | bytes 786432 | tf_op jit(solution)/shard_map/all_to_all | solution.py:265
  243.4 7.9 %collective-permute-start.25 = (f32[64,96]{1,0:T(8,128)S(1)}, f32[64,96]{1,0:T(8,128)S(1)}, u32[]{:S(2)}, u32[]{:S(2)}) collective-permute-start(f32[64,96]{1,0:T(8,128)S(1)} %get-tuple-element.84), channel_id=1, source_target_pairs={{4,8},{8,4},{12,16},{16,12},{20,24},{24,20},{28,32},{32,28},{36,40... | collective-permute-start | bytes 73736 | tf_op jit(solution)/shard_map/halo_sx/ppermute | solution.py:141
  251.3 5.7 %collective-permute-start.26 = (f32[64,96]{1,0:T(8,128)S(1)}, f32[64,96]{1,0:T(8,128)S(1)}, u32[]{:S(2)}, u32[]{:S(2)}) collective-permute-start(f32[64,96]{1,0:T(8,128)S(1)} %get-tuple-element.85), channel_id=1, source_target_pairs={{0,1},{1,0},{2,3},{3,2},{4,5},{5,4},{6,7},{7,6},{8,9},{9,8},{10,11... | collective-permute-start | bytes 73736 | tf_op jit(solution)/shard_map/halo_sy/ppermute | solution.py:141
  259.8 3.7 %all-to-all-start.9 = ((bf16[8,80,384]{2,1,0:T(8,128)(2,1)}), bf16[8,80,384]{2,1,0:T(8,128)(2,1)S(1)}, u32[]{:S(2)}, u32[]{:S(2)}) async-start(bf16[8,80,384]{2,1,0:T(8,128)(2,1)} %finish.14), calls=%async_computation.9 | async-start | bytes 983040 | tf_op jit(solution)/shard_map/all_to_all | solution.py:265
  263.6 11.5 %all-to-all-done.9.refs_0_ = bf16[8,80,384]{2,1,0:T(8,128)(2,1)S(1)} async-done(((bf16[8,80,384]{2,1,0:T(8,128)(2,1)}), bf16[8,80,384]{2,1,0:T(8,128)(2,1)S(1)}, u32[]{:S(2)}, u32[]{:S(2)}) %all-to-all-start.9) | async-done | bytes 491552 | tf_op jit(solution)/shard_map/all_to_all | solution.py:265
  277.6 9.1 %collective-permute-start.28 = (f32[64,96]{1,0:T(8,128)S(1)}, f32[64,96]{1,0:T(8,128)S(1)}, u32[]{:S(2)}, u32[]{:S(2)}) collective-permute-start(f32[64,96]{1,0:T(8,128)S(1)} %get-tuple-element.89), channel_id=1, source_target_pairs={{0,4},{4,8},{8,12},{12,16},{16,20},{20,24},{24,28},{28,32},{32,36}... | collective-permute-start | bytes 73736 | tf_op jit(solution)/shard_map/ppermute | solution.py:141
  286.7 5.3 %collective-permute-start.29 = (f32[64,96]{1,0:T(8,128)S(1)}, f32[64,96]{1,0:T(8,128)S(1)}, u32[]{:S(2)}, u32[]{:S(2)}) collective-permute-start(f32[64,96]{1,0:T(8,128)S(1)} %get-tuple-element.90), channel_id=1, source_target_pairs={{0,1},{1,2},{2,3},{4,5},{5,6},{6,7},{8,9},{9,10},{10,11},{12,13},{... | collective-permute-start | bytes 73736 | tf_op jit(solution)/shard_map/ppermute | solution.py:141
  294.4 4.9 %all-to-all-start.10 = ((f32[32,1,40]{2,1,0:T(1,128)}), f32[32,1,40]{2,1,0:T(1,128)S(1)}, u32[]{:S(2)}, u32[]{:S(2)}) async-start(f32[32,1,40]{2,1,0:T(1,128)} %bitcast.20), calls=%async_computation.10 | async-start | bytes 32768 | tf_op jit(solution)/shard_map/all_to_all | solution.py:265
  299.3 8.5 %all-to-all-done.10 = f32[32,1,40]{2,1,0:T(1,128)S(1)} async-done(((f32[32,1,40]{2,1,0:T(1,128)}), f32[32,1,40]{2,1,0:T(1,128)S(1)}, u32[]{:S(2)}, u32[]{:S(2)}) %all-to-all-start.10) | async-done | bytes 5152 | tf_op jit(solution)/shard_map/all_to_all | solution.py:265
  308.5 4.3 %all-to-all-start.11 = ((f32[16,1,40]{2,1,0:T(1,128)}), f32[16,1,40]{2,1,0:T(1,128)S(1)}, u32[]{:S(2)}, u32[]{:S(2)}) async-start(f32[16,1,40]{2,1,0:T(1,128)} %broadcast_in_dim.126), calls=%async_computation.11 | async-start | bytes 16384 | tf_op jit(solution)/shard_map/all_to_all | solution.py:265
  312.8 7.0 %all-to-all-done.11 = f32[16,1,40]{2,1,0:T(1,128)S(1)} async-done(((f32[16,1,40]{2,1,0:T(1,128)}), f32[16,1,40]{2,1,0:T(1,128)S(1)}, u32[]{:S(2)}, u32[]{:S(2)}) %all-to-all-start.11) | async-done | bytes 2592 | tf_op jit(solution)/shard_map/all_to_all | solution.py:265
  323.9 3.3 all-to-all-start.12
  327.9 5.8 %all-to-all-done.12 = f32[8,1,216]{2,1,0:T(1,128)S(1)} async-done(((f32[8,1,216]{2,1,0:T(1,128)}), f32[8,1,216]{2,1,0:T(1,128)S(1)}, u32[]{:S(2)}, u32[]{:S(2)}) %all-to-all-start.12) | async-done | bytes 6944 | tf_op jit(solution)/shard_map/all_to_all | solution.py:265
  (168 shorter events, 80.7 us)
Async XLA Ops:
  3.5 25.5 %all-to-all-start = ((bf16[8,8,3200]{2,1,0:T(8,128)(2,1)}), bf16[8,8,3200]{2,1,0:T(8,128)(2,1)S(1)}, u32[]{:S(2)}, u32[]{:S(2)}) async-start(bf16[8,8,3200]{2,1,0:T(8,128)(2,1)} %broadcast_in_dim.114), calls=%async_computation | async-start | bytes 819200 | tf_op jit(solution)/shard_map/all_to_all | solution.py:265
  31.7 10.1 %collective-permute-start = (f32[64,96]{1,0:T(8,128)S(1)}, f32[64,96]{1,0:T(8,128)S(1)}, u32[]{:S(2)}, u32[]{:S(2)}) collective-permute-start(f32[64,96]{1,0:T(8,128)S(1)} %get-tuple-element.48), channel_id=1, source_target_pairs={{0,4},{4,0},{8,12},{12,8},{16,20},{20,16},{24,28},{28,24},{32,36},... | collective-permute-start | bytes 73736 | tf_op jit(solution)/shard_map/halo_sx/ppermute | solution.py:141
  35.0 6.9 %collective-permute-start.1 = (f32[64,96]{1,0:T(8,128)S(1)}, f32[64,96]{1,0:T(8,128)S(1)}, u32[]{:S(2)}, u32[]{:S(2)}) collective-permute-start(f32[64,96]{1,0:T(8,128)S(1)} %get-tuple-element.49), channel_id=1, source_target_pairs={{4,8},{8,4},{12,16},{16,12},{20,24},{24,20},{28,32},{32,28},{36,40... | collective-permute-start | bytes 73736 | tf_op jit(solution)/shard_map/halo_sx/ppermute | solution.py:141
  38.1 4.7 %collective-permute-start.2 = (f32[64,96]{1,0:T(8,128)S(1)}, f32[64,96]{1,0:T(8,128)S(1)}, u32[]{:S(2)}, u32[]{:S(2)}) collective-permute-start(f32[64,96]{1,0:T(8,128)S(1)} %get-tuple-element.50), channel_id=1, source_target_pairs={{0,1},{1,0},{2,3},{3,2},{4,5},{5,4},{6,7},{7,6},{8,9},{9,8},{10,11... | collective-permute-start | bytes 73736 | tf_op jit(solution)/shard_map/halo_sy/ppermute | solution.py:141
  43.6 17.6 %all-to-all-start.1 = ((bf16[8,64,384]{2,1,0:T(8,128)(2,1)}), bf16[8,64,384]{2,1,0:T(8,128)(2,1)S(1)}, u32[]{:S(2)}, u32[]{:S(2)}) async-start(bf16[8,64,384]{2,1,0:T(8,128)(2,1)} %get-tuple-element.52), calls=%async_computation.1 | async-start | bytes 786432 | tf_op jit(solution)/shard_map/all_to_all | solution.py:265
  63.4 13.4 %collective-permute-start.4 = (f32[64,96]{1,0:T(8,128)S(1)}, f32[64,96]{1,0:T(8,128)S(1)}, u32[]{:S(2)}, u32[]{:S(2)}) collective-permute-start(f32[64,96]{1,0:T(8,128)S(1)} %get-tuple-element.54), channel_id=1, source_target_pairs={{0,4},{4,0},{8,12},{12,8},{16,20},{20,16},{24,28},{28,24},{32,36},... | collective-permute-start | bytes 73736 | tf_op jit(solution)/shard_map/halo_sx/ppermute | solution.py:141
  65.7 11.1 %collective-permute-start.5 = (f32[64,96]{1,0:T(8,128)S(1)}, f32[64,96]{1,0:T(8,128)S(1)}, u32[]{:S(2)}, u32[]{:S(2)}) collective-permute-start(f32[64,96]{1,0:T(8,128)S(1)} %get-tuple-element.55), channel_id=1, source_target_pairs={{4,8},{8,4},{12,16},{16,12},{20,24},{24,20},{28,32},{32,28},{36,40... | collective-permute-start | bytes 73736 | tf_op jit(solution)/shard_map/halo_sx/ppermute | solution.py:141
  70.1 7.0 %collective-permute-start.6 = (f32[64,96]{1,0:T(8,128)S(1)}, f32[64,96]{1,0:T(8,128)S(1)}, u32[]{:S(2)}, u32[]{:S(2)}) collective-permute-start(f32[64,96]{1,0:T(8,128)S(1)} %get-tuple-element.56), channel_id=1, source_target_pairs={{0,1},{1,0},{2,3},{3,2},{4,5},{5,4},{6,7},{7,6},{8,9},{9,8},{10,11... | collective-permute-start | bytes 73736 | tf_op jit(solution)/shard_map/halo_sy/ppermute | solution.py:141
  105.6 20.5 %all-to-all-start.4 = ((f32[16,1,64]{2,1,0:T(1,128)}), f32[16,1,64]{2,1,0:T(1,128)S(1)}, u32[]{:S(2)}, u32[]{:S(2)}) async-start(f32[16,1,64]{2,1,0:T(1,128)} %broadcast_in_dim.121), calls=%async_computation.4 | async-start | bytes 16384 | tf_op jit(solution)/shard_map/all_to_all | solution.py:265
  117.5 9.0 %collective-permute-start.10 = (f32[64,96]{1,0:T(8,128)}, f32[64,96]{1,0:T(8,128)S(1)}, u32[]{:S(2)}, u32[]{:S(2)}) collective-permute-start(f32[64,96]{1,0:T(8,128)} %get-tuple-element.62), channel_id=1, source_target_pairs={{0,1},{1,0},{2,3},{3,2},{4,5},{5,4},{6,7},{7,6},{8,9},{9,8},{10,11... | collective-permute-start | bytes 73736 | tf_op jit(solution)/shard_map/halo_sy/ppermute | solution.py:141
  119.7 6.8 %collective-permute-start.11 = (f32[64,96]{1,0:T(8,128)}, f32[64,96]{1,0:T(8,128)S(1)}, u32[]{:S(2)}, u32[]{:S(2)}) collective-permute-start(f32[64,96]{1,0:T(8,128)} %get-tuple-element.63), channel_id=1, source_target_pairs={{1,2},{2,1},{5,6},{6,5},{9,10},{10,9},{13,14},{14,13},{17,18},{18,... | collective-permute-start | bytes 73736 | tf_op jit(solution)/shard_map/halo_sy/ppermute | solution.py:141
  120.3 6.1 %collective-permute-start.8 = (f32[64,96]{1,0:T(8,128)}, f32[64,96]{1,0:T(8,128)S(1)}, u32[]{:S(2)}, u32[]{:S(2)}) collective-permute-start(f32[64,96]{1,0:T(8,128)} %get-tuple-element.60), channel_id=1, source_target_pairs={{0,4},{4,0},{8,12},{12,8},{16,20},{20,16},{24,28},{28,24},{32,36},... | collective-permute-start | bytes 73736 | tf_op jit(solution)/shard_map/halo_sx/ppermute | solution.py:141
  122.7 5.4 %collective-permute-start.9 = (f32[64,96]{1,0:T(8,128)}, f32[64,96]{1,0:T(8,128)S(1)}, u32[]{:S(2)}, u32[]{:S(2)}) collective-permute-start(f32[64,96]{1,0:T(8,128)} %get-tuple-element.61), channel_id=1, source_target_pairs={{4,8},{8,4},{12,16},{16,12},{20,24},{24,20},{28,32},{32,28},{36,40... | collective-permute-start | bytes 73736 | tf_op jit(solution)/shard_map/halo_sx/ppermute | solution.py:141
  145.7 15.3 %collective-permute-start.12 = (f32[64,96]{1,0:T(8,128)S(1)}, f32[64,96]{1,0:T(8,128)S(1)}, u32[]{:S(2)}, u32[]{:S(2)}) collective-permute-start(f32[64,96]{1,0:T(8,128)S(1)} %get-tuple-element.66), channel_id=1, source_target_pairs={{0,4},{4,0},{8,12},{12,8},{16,20},{20,16},{24,28},{28,24},{32,36},... | collective-permute-start | bytes 73736 | tf_op jit(solution)/shard_map/halo_sx/ppermute | solution.py:141
  147.6 13.4 %collective-permute-start.13 = (f32[64,96]{1,0:T(8,128)S(1)}, f32[64,96]{1,0:T(8,128)S(1)}, u32[]{:S(2)}, u32[]{:S(2)}) collective-permute-start(f32[64,96]{1,0:T(8,128)S(1)} %get-tuple-element.67), channel_id=1, source_target_pairs={{4,8},{8,4},{12,16},{16,12},{20,24},{24,20},{28,32},{32,28},{36,40... | collective-permute-start | bytes 73736 | tf_op jit(solution)/shard_map/halo_sx/ppermute | solution.py:141
  155.4 6.2 %collective-permute-start.14 = (f32[64,96]{1,0:T(8,128)S(1)}, f32[64,96]{1,0:T(8,128)S(1)}, u32[]{:S(2)}, u32[]{:S(2)}) collective-permute-start(f32[64,96]{1,0:T(8,128)S(1)} %get-tuple-element.68), channel_id=1, source_target_pairs={{0,1},{1,0},{2,3},{3,2},{4,5},{5,4},{6,7},{7,6},{8,9},{9,8},{10,11... | collective-permute-start | bytes 73736 | tf_op jit(solution)/shard_map/halo_sy/ppermute | solution.py:141
  177.0 15.8 %collective-permute-start.16 = (f32[64,96]{1,0:T(8,128)S(1)}, f32[64,96]{1,0:T(8,128)S(1)}, u32[]{:S(2)}, u32[]{:S(2)}) collective-permute-start(f32[64,96]{1,0:T(8,128)S(1)} %get-tuple-element.71), channel_id=1, source_target_pairs={{0,4},{4,0},{8,12},{12,8},{16,20},{20,16},{24,28},{28,24},{32,36},... | collective-permute-start | bytes 73736 | tf_op jit(solution)/shard_map/halo_sx/ppermute | solution.py:141
  178.9 13.9 %collective-permute-start.17 = (f32[64,96]{1,0:T(8,128)S(1)}, f32[64,96]{1,0:T(8,128)S(1)}, u32[]{:S(2)}, u32[]{:S(2)}) collective-permute-start(f32[64,96]{1,0:T(8,128)S(1)} %get-tuple-element.72), channel_id=1, source_target_pairs={{4,8},{8,4},{12,16},{16,12},{20,24},{24,20},{28,32},{32,28},{36,40... | collective-permute-start | bytes 73736 | tf_op jit(solution)/shard_map/halo_sx/ppermute | solution.py:141
  186.9 6.8 %collective-permute-start.18 = (f32[64,96]{1,0:T(8,128)S(1)}, f32[64,96]{1,0:T(8,128)S(1)}, u32[]{:S(2)}, u32[]{:S(2)}) collective-permute-start(f32[64,96]{1,0:T(8,128)S(1)} %get-tuple-element.73), channel_id=1, source_target_pairs={{0,1},{1,0},{2,3},{3,2},{4,5},{5,4},{6,7},{7,6},{8,9},{9,8},{10,11... | collective-permute-start | bytes 73736 | tf_op jit(solution)/shard_map/halo_sy/ppermute | solution.py:141
  192.1 1.6 collective-permute-start.19
  209.3 15.9 %collective-permute-start.20 = (f32[64,96]{1,0:T(8,128)S(1)}, f32[64,96]{1,0:T(8,128)S(1)}, u32[]{:S(2)}, u32[]{:S(2)}) collective-permute-start(f32[64,96]{1,0:T(8,128)S(1)} %get-tuple-element.78), channel_id=1, source_target_pairs={{0,4},{4,0},{8,12},{12,8},{16,20},{20,16},{24,28},{28,24},{32,36},... | collective-permute-start | bytes 73736 | tf_op jit(solution)/shard_map/halo_sx/ppermute | solution.py:141
  211.2 14.0 %collective-permute-start.21 = (f32[64,96]{1,0:T(8,128)S(1)}, f32[64,96]{1,0:T(8,128)S(1)}, u32[]{:S(2)}, u32[]{:S(2)}) collective-permute-start(f32[64,96]{1,0:T(8,128)S(1)} %get-tuple-element.79), channel_id=1, source_target_pairs={{4,8},{8,4},{12,16},{16,12},{20,24},{24,20},{28,32},{32,28},{36,40... | collective-permute-start | bytes 73736 | tf_op jit(solution)/shard_map/halo_sx/ppermute | solution.py:141
  219.2 6.9 %collective-permute-start.22 = (f32[64,96]{1,0:T(8,128)S(1)}, f32[64,96]{1,0:T(8,128)S(1)}, u32[]{:S(2)}, u32[]{:S(2)}) collective-permute-start(f32[64,96]{1,0:T(8,128)S(1)} %get-tuple-element.80), channel_id=1, source_target_pairs={{0,1},{1,0},{2,3},{3,2},{4,5},{5,4},{6,7},{7,6},{8,9},{9,8},{10,11... | collective-permute-start | bytes 73736 | tf_op jit(solution)/shard_map/halo_sy/ppermute | solution.py:141
  241.5 16.2 %collective-permute-start.24 = (f32[64,96]{1,0:T(8,128)S(1)}, f32[64,96]{1,0:T(8,128)S(1)}, u32[]{:S(2)}, u32[]{:S(2)}) collective-permute-start(f32[64,96]{1,0:T(8,128)S(1)} %get-tuple-element.83), channel_id=1, source_target_pairs={{0,4},{4,0},{8,12},{12,8},{16,20},{20,16},{24,28},{28,24},{32,36},... | collective-permute-start | bytes 73736 | tf_op jit(solution)/shard_map/halo_sx/ppermute | solution.py:141
  243.4 14.3 %collective-permute-start.25 = (f32[64,96]{1,0:T(8,128)S(1)}, f32[64,96]{1,0:T(8,128)S(1)}, u32[]{:S(2)}, u32[]{:S(2)}) collective-permute-start(f32[64,96]{1,0:T(8,128)S(1)} %get-tuple-element.84), channel_id=1, source_target_pairs={{4,8},{8,4},{12,16},{16,12},{20,24},{24,20},{28,32},{32,28},{36,40... | collective-permute-start | bytes 73736 | tf_op jit(solution)/shard_map/halo_sx/ppermute | solution.py:141
  251.3 7.0 %collective-permute-start.26 = (f32[64,96]{1,0:T(8,128)S(1)}, f32[64,96]{1,0:T(8,128)S(1)}, u32[]{:S(2)}, u32[]{:S(2)}) collective-permute-start(f32[64,96]{1,0:T(8,128)S(1)} %get-tuple-element.85), channel_id=1, source_target_pairs={{0,1},{1,0},{2,3},{3,2},{4,5},{5,4},{6,7},{7,6},{8,9},{9,8},{10,11... | collective-permute-start | bytes 73736 | tf_op jit(solution)/shard_map/halo_sy/ppermute | solution.py:141
  259.8 15.4 %all-to-all-start.9 = ((bf16[8,80,384]{2,1,0:T(8,128)(2,1)}), bf16[8,80,384]{2,1,0:T(8,128)(2,1)S(1)}, u32[]{:S(2)}, u32[]{:S(2)}) async-start(bf16[8,80,384]{2,1,0:T(8,128)(2,1)} %finish.14), calls=%async_computation.9 | async-start | bytes 983040 | tf_op jit(solution)/shard_map/all_to_all | solution.py:265
  277.6 14.4 %collective-permute-start.28 = (f32[64,96]{1,0:T(8,128)S(1)}, f32[64,96]{1,0:T(8,128)S(1)}, u32[]{:S(2)}, u32[]{:S(2)}) collective-permute-start(f32[64,96]{1,0:T(8,128)S(1)} %get-tuple-element.89), channel_id=1, source_target_pairs={{0,4},{4,8},{8,12},{12,16},{16,20},{20,24},{24,28},{28,32},{32,36}... | collective-permute-start | bytes 73736 | tf_op jit(solution)/shard_map/ppermute | solution.py:141
  286.7 6.3 %collective-permute-start.29 = (f32[64,96]{1,0:T(8,128)S(1)}, f32[64,96]{1,0:T(8,128)S(1)}, u32[]{:S(2)}, u32[]{:S(2)}) collective-permute-start(f32[64,96]{1,0:T(8,128)S(1)} %get-tuple-element.90), channel_id=1, source_target_pairs={{0,1},{1,2},{2,3},{4,5},{5,6},{6,7},{8,9},{9,10},{10,11},{12,13},{... | collective-permute-start | bytes 73736 | tf_op jit(solution)/shard_map/ppermute | solution.py:141
  294.4 13.5 %all-to-all-start.10 = ((f32[32,1,40]{2,1,0:T(1,128)}), f32[32,1,40]{2,1,0:T(1,128)S(1)}, u32[]{:S(2)}, u32[]{:S(2)}) async-start(f32[32,1,40]{2,1,0:T(1,128)} %bitcast.20), calls=%async_computation.10 | async-start | bytes 32768 | tf_op jit(solution)/shard_map/all_to_all | solution.py:265
  308.5 11.3 %all-to-all-start.11 = ((f32[16,1,40]{2,1,0:T(1,128)}), f32[16,1,40]{2,1,0:T(1,128)S(1)}, u32[]{:S(2)}, u32[]{:S(2)}) async-start(f32[16,1,40]{2,1,0:T(1,128)} %broadcast_in_dim.126), calls=%async_computation.11 | async-start | bytes 16384 | tf_op jit(solution)/shard_map/all_to_all | solution.py:265
  323.9 9.8 %all-to-all-start.12 = ((f32[8,1,216]{2,1,0:T(1,128)}), f32[8,1,216]{2,1,0:T(1,128)S(1)}, u32[]{:S(2)}, u32[]{:S(2)}) async-start(f32[8,1,216]{2,1,0:T(1,128)} %all_to_all.63), calls=%async_computation.12 | async-start | bytes 16384 | tf_op jit(solution)/shard_map/all_to_all | solution.py:265
  (16 other events, 104.0 us)

commit v6 on v5

--- a/solution.py
+++ b/solution.py
@@ -48,9 +48,43 @@
         compiler_params=params(),
         name="arrange",
     )(
-        stiffness.reshape(faces, n_freq, run, width),
-        mass_matrix.reshape(faces, n_freq, run, width),
-    )
+        *(
+            pltpu.with_memory_space_constraint(matrix.reshape(faces, n_freq, run, width), pltpu.HBM)
+            for matrix in (stiffness, mass_matrix)
+        )
+    )
+
+
+def packet_kernel(load_ref, tags_ref, out_ref):
+    slots, parts, faces, length = load_ref.shape
+    n_freq = out_ref.shape[0]
+    run = length // n_freq
+    by_face = [
+        jnp.concatenate(
+            [load_ref[k, p, f : f + 1, :] for p in range(parts) for k in range(slots)], axis=0
+        )
+        for f in range(faces)
+    ]
+    pieces = [
+        by_face[f][:, d * run : (d + 1) * run] for d in range(n_freq) for f in range(faces)
+    ]
+    packet = jnp.concatenate(pieces + [tags_ref[...]], axis=1).astype(BF)
+    for d in range(n_freq):
+        out_ref[d] = packet
+
+
+def packet_of(load, tags, n_freq):
+    slots, parts, faces, length = load.shape
+    own = slots * parts
+    vmem = pl.BlockSpec(memory_space=pltpu.VMEM)
+    return pl.pallas_call(
+        packet_kernel,
+        in_specs=[vmem, vmem],
+        out_specs=vmem,
+        out_shape=jax.ShapeDtypeStruct((n_freq, own, faces * length + 128), BF),
+        compiler_params=params(),
+        name="packet",
+    )(load, tags)
 
 
 def odd_masks(odd_ref, shape):
@@ -318,11 +352,9 @@
     own = 2 * slots
     me = lax.axis_index("freq")
 
-    load = jnp.swapaxes(adjoint_load[0, 0].astype(BF), 0, 1).reshape(own, faces, n_freq, run)
-    load = jnp.swapaxes(load, 1, 2).reshape(own, order)
-    tags = jnp.broadcast_to(assignment.astype(BF)[None, :], (2, slots)).reshape(own, 1)
-    packet = jnp.concatenate([load, jnp.broadcast_to(tags, (own, 128))], axis=1)
-    field = exchange(jnp.broadcast_to(packet[None], (n_freq, *packet.shape)), "freq")
+    tags = jnp.broadcast_to(assignment.astype(F32)[None, :], (2, slots)).reshape(own, 1)
+    packet = packet_of(adjoint_load[0, 0], jnp.broadcast_to(tags, (own, 128)), n_freq)
+    field = exchange(packet, "freq")
     half = n_freq // 2
     pair = tuple(
         pltpu.with_memory_space_constraint(

time: 336 us -> 336 us (level)
  Pallas kernels: 26.7 us -> 30.3 us
  local copies, waits for them, and re-layouts: 13 us -> 9.46 us
  transfers between devices with their start and end apart: 37 -> 37, of which waited for: 14 -> 14; matrix products, arithmetic and copies ran while one was open for 0% -> 0% of each run, Pallas kernels for 2% -> 3%
where the time goes in v6:
time: 336 us; the launch traced here: 334 us
  starting transfers between devices  149 us (44%)
  blocking collectives  80.3 us (24%)
  waiting for transfers between devices  58.6 us (17%)
  Pallas kernels  30.3 us (9%)
  local copies, waits for them, and re-layouts  9.46 us (3%)
  other arithmetic  4.05 us (1%)
    ppermute x30, starting transfers between devices, permute(): lax.ppermute(values, axis, pairs)  108 us
    all_to_all x6, blocking collectives, exchange(): return lax.all_to_all(blocks, axis, 0, 0, tiled=False)  80.3 us
    all_to_all x7, waiting for transfers between devices, exchange(): return lax.all_to_all(blocks, axis, 0, 0, tiled=False)  51.8 us
    all_to_all x7, starting transfers between devices, exchange(): return lax.all_to_all(blocks, axis, 0, 0, tiled=False)  40.5 us
    pallas_call x8, Pallas kernels, apply_local(): pl.pallas_call(functools.partial(apply_kernel, sign, faces, by_slot, side...  18.2 us
    pallas_call x2, Pallas kernels, arrange(): pl.pallas_call(arrange_kernel, grid=(count,), in_specs=[block, block], ou...  7.7 us
    ppermute x30, waiting for transfers between devices, permute(): lax.ppermute(values, axis, pairs)  6.75 us
  transfers between devices with their start and end apart: 37, of which 14 were waited for; matrix products, arithmetic and copies ran while one was open for 0% of the time, Pallas kernels for 3%

profile of v6, /device:TPU:1, one launch (start us, length us, event | category | flops | bytes accessed | tf_op | source)
XLA Modules:
  0.0 333.8 jit_solution(13124898538898929467)
XLA Ops:
  3.2 10.9 %all-to-all-start = ((bf16[8,8,3200]{2,1,0:T(8,128)(2,1)}), bf16[8,8,3200]{2,1,0:T(8,128)(2,1)S(1)}, u32[]{:S(2)}, u32[]{:S(2)}) async-start(bf16[8,8,3200]{2,1,0:T(8,128)(2,1)} %packet.1), calls=%async_computation | async-start | bytes 819200 | tf_op jit(solution)/shard_map/all_to_all | solution.py:299
  14.1 3.9 %arrange.2.refs_1_ = bf16[1536,768]{1,0:T(8,128)(2,1)S(1)} custom-call(bf16[4,8,96,384]{3,2,1,0:T(8,128)(2,1)} %bitcast.35, bf16[4,8,96,384]{3,2,1,0:T(8,128)(2,1)} %bitcast.37), custom_call_target="tpu_custom_call" | custom-call | tf_op jit(solution)/shard_map/arrange/pallas_call | solution.py:41
  18.0 3.8 %arrange.3.refs_2_ = bf16[1536,768]{1,0:T(8,128)(2,1)S(1)} custom-call(bf16[4,8,96,384]{3,2,1,0:T(8,128)(2,1)} %bitcast.36, bf16[4,8,96,384]{3,2,1,0:T(8,128)(2,1)} %bitcast.38), custom_call_target="tpu_custom_call" | custom-call | tf_op jit(solution)/shard_map/arrange/pallas_call | solution.py:41
  23.3 5.4 %all-to-all-done.refs_0_ = bf16[8,8,3200]{2,1,0:T(8,128)(2,1)S(1)} async-done(((bf16[8,8,3200]{2,1,0:T(8,128)(2,1)}), bf16[8,8,3200]{2,1,0:T(8,128)(2,1)S(1)}, u32[]{:S(2)}, u32[]{:S(2)}) %all-to-all-start) | async-done | bytes 409632 | tf_op jit(solution)/shard_map/all_to_all | solution.py:299
  43.4 3.5 %all-to-all-start.1 = ((bf16[8,64,384]{2,1,0:T(8,128)(2,1)}), bf16[8,64,384]{2,1,0:T(8,128)(2,1)S(1)}, u32[]{:S(2)}, u32[]{:S(2)}) async-start(bf16[8,64,384]{2,1,0:T(8,128)(2,1)} %get-tuple-element.52), calls=%async_computation.1 | async-start | bytes 786432 | tf_op jit(solution)/shard_map/all_to_all | solution.py:299
  46.9 14.1 %all-to-all-done.1.refs_0_ = bf16[8,64,384]{2,1,0:T(8,128)(2,1)S(1)} async-done(((bf16[8,64,384]{2,1,0:T(8,128)(2,1)}), bf16[8,64,384]{2,1,0:T(8,128)(2,1)S(1)}, u32[]{:S(2)}, u32[]{:S(2)}) %all-to-all-start.1) | async-done | bytes 393248 | tf_op jit(solution)/shard_map/all_to_all | solution.py:299
  65.5 4.4 %collective-permute-start.5 = (f32[64,96]{1,0:T(8,128)S(1)}, f32[64,96]{1,0:T(8,128)S(1)}, u32[]{:S(2)}, u32[]{:S(2)}) collective-permute-start(f32[64,96]{1,0:T(8,128)S(1)} %get-tuple-element.55), channel_id=1, source_target_pairs={{4,8},{8,4},{12,16},{16,12},{20,24},{24,20},{28,32},{32,28},{36,40... | collective-permute-start | bytes 73736 | tf_op jit(solution)/shard_map/halo_sx/ppermute | solution.py:175
  69.9 5.7 %collective-permute-start.6 = (f32[64,96]{1,0:T(8,128)S(1)}, f32[64,96]{1,0:T(8,128)S(1)}, u32[]{:S(2)}, u32[]{:S(2)}) collective-permute-start(f32[64,96]{1,0:T(8,128)S(1)} %get-tuple-element.56), channel_id=1, source_target_pairs={{0,1},{1,0},{2,3},{3,2},{4,5},{5,4},{6,7},{7,6},{8,9},{9,8},{10,11... | collective-permute-start | bytes 73736 | tf_op jit(solution)/shard_map/halo_sy/ppermute | solution.py:175
  77.2 16.1 %all_to_all.77.refs_0_ = bf16[8,72,384]{2,1,0:T(8,128)(2,1)S(1)} all-to-all(bf16[8,72,384]{2,1,0:T(8,128)(2,1)S(1)} %finish.9), channel_id=1, replica_groups=mesh['freq'=8,'sx'=16,'sy'=4] {'freq'}, dimensions={0} | all-to-all | bytes 884736 | tf_op jit(solution)/shard_map/all_to_all | solution.py:299
  93.7 11.0 %all_to_all.78 = f32[4,1,64]{2,1,0:T(1,128)S(1)} all-to-all(f32[4,1,64]{2,1,0:T(1,128)S(1)} %broadcast_in_dim.113), channel_id=1, replica_groups=mesh['freq'=8,'sx'=16,'sy'=4] {'sy'}, dimensions={0} | all-to-all | bytes 2048 | tf_op jit(solution)/shard_map/all_to_all | solution.py:299
  105.3 8.9 %all-to-all-start.4 = ((f32[16,1,64]{2,1,0:T(1,128)}), f32[16,1,64]{2,1,0:T(1,128)S(1)}, u32[]{:S(2)}, u32[]{:S(2)}) async-start(f32[16,1,64]{2,1,0:T(1,128)} %broadcast_in_dim.114), calls=%async_computation.4 | async-start | bytes 16384 | tf_op jit(solution)/shard_map/all_to_all | solution.py:299
  129.3 13.7 %all_to_all.79.refs_0_ = bf16[8,64,384]{2,1,0:T(8,128)(2,1)S(1)} all-to-all(bf16[8,64,384]{2,1,0:T(8,128)(2,1)S(1)} %get-tuple-element.64), channel_id=1, replica_groups=mesh['freq'=8,'sx'=16,'sy'=4] {'freq'}, dimensions={0} | all-to-all | bytes 786432 | tf_op jit(solution)/shard_map/all_to_all | solution.py:299
  147.3 7.8 %collective-permute-start.13 = (f32[64,96]{1,0:T(8,128)S(1)}, f32[64,96]{1,0:T(8,128)S(1)}, u32[]{:S(2)}, u32[]{:S(2)}) collective-permute-start(f32[64,96]{1,0:T(8,128)S(1)} %get-tuple-element.67), channel_id=1, source_target_pairs={{4,8},{8,4},{12,16},{16,12},{20,24},{24,20},{28,32},{32,28},{36,40... | collective-permute-start | bytes 73736 | tf_op jit(solution)/shard_map/halo_sx/ppermute | solution.py:175
  155.1 4.9 %collective-permute-start.14 = (f32[64,96]{1,0:T(8,128)S(1)}, f32[64,96]{1,0:T(8,128)S(1)}, u32[]{:S(2)}, u32[]{:S(2)}) collective-permute-start(f32[64,96]{1,0:T(8,128)S(1)} %get-tuple-element.68), channel_id=1, source_target_pairs={{0,1},{1,0},{2,3},{3,2},{4,5},{5,4},{6,7},{7,6},{8,9},{9,8},{10,11... | collective-permute-start | bytes 73736 | tf_op jit(solution)/shard_map/halo_sy/ppermute | solution.py:175
  161.4 13.1 %all_to_all.80.refs_0_ = bf16[8,64,384]{2,1,0:T(8,128)(2,1)S(1)} all-to-all(bf16[8,64,384]{2,1,0:T(8,128)(2,1)S(1)} %finish.11), channel_id=1, replica_groups=mesh['freq'=8,'sx'=16,'sy'=4] {'freq'}, dimensions={0} | all-to-all | bytes 786432 | tf_op jit(solution)/shard_map/all_to_all | solution.py:299
  178.6 8.0 %collective-permute-start.17 = (f32[64,96]{1,0:T(8,128)S(1)}, f32[64,96]{1,0:T(8,128)S(1)}, u32[]{:S(2)}, u32[]{:S(2)}) collective-permute-start(f32[64,96]{1,0:T(8,128)S(1)} %get-tuple-element.72), channel_id=1, source_target_pairs={{4,8},{8,4},{12,16},{16,12},{20,24},{24,20},{28,32},{32,28},{36,40... | collective-permute-start | bytes 73736 | tf_op jit(solution)/shard_map/halo_sx/ppermute | solution.py:175
  186.6 5.3 %collective-permute-start.18 = (f32[64,96]{1,0:T(8,128)S(1)}, f32[64,96]{1,0:T(8,128)S(1)}, u32[]{:S(2)}, u32[]{:S(2)}) collective-permute-start(f32[64,96]{1,0:T(8,128)S(1)} %get-tuple-element.73), channel_id=1, source_target_pairs={{0,1},{1,0},{2,3},{3,2},{4,5},{5,4},{6,7},{7,6},{8,9},{9,8},{10,11... | collective-permute-start | bytes 73736 | tf_op jit(solution)/shard_map/halo_sy/ppermute | solution.py:175
  193.6 13.1 %all_to_all.81.refs_0_ = bf16[8,64,384]{2,1,0:T(8,128)(2,1)S(1)} all-to-all(bf16[8,64,384]{2,1,0:T(8,128)(2,1)S(1)} %get-tuple-element.76), channel_id=1, replica_groups=mesh['freq'=8,'sx'=16,'sy'=4] {'freq'}, dimensions={0} | all-to-all | bytes 786432 | tf_op jit(solution)/shard_map/all_to_all | solution.py:299
  210.9 8.0 %collective-permute-start.21 = (f32[64,96]{1,0:T(8,128)S(1)}, f32[64,96]{1,0:T(8,128)S(1)}, u32[]{:S(2)}, u32[]{:S(2)}) collective-permute-start(f32[64,96]{1,0:T(8,128)S(1)} %get-tuple-element.79), channel_id=1, source_target_pairs={{4,8},{8,4},{12,16},{16,12},{20,24},{24,20},{28,32},{32,28},{36,40... | collective-permute-start | bytes 73736 | tf_op jit(solution)/shard_map/halo_sx/ppermute | solution.py:175
  218.9 5.4 %collective-permute-start.22 = (f32[64,96]{1,0:T(8,128)S(1)}, f32[64,96]{1,0:T(8,128)S(1)}, u32[]{:S(2)}, u32[]{:S(2)}) collective-permute-start(f32[64,96]{1,0:T(8,128)S(1)} %get-tuple-element.80), channel_id=1, source_target_pairs={{0,1},{1,0},{2,3},{3,2},{4,5},{5,4},{6,7},{7,6},{8,9},{9,8},{10,11... | collective-permute-start | bytes 73736 | tf_op jit(solution)/shard_map/halo_sy/ppermute | solution.py:175
  225.9 13.1 %all_to_all.82.refs_0_ = bf16[8,64,384]{2,1,0:T(8,128)(2,1)S(1)} all-to-all(bf16[8,64,384]{2,1,0:T(8,128)(2,1)S(1)} %finish.13), channel_id=1, replica_groups=mesh['freq'=8,'sx'=16,'sy'=4] {'freq'}, dimensions={0} | all-to-all | bytes 786432 | tf_op jit(solution)/shard_map/all_to_all | solution.py:299
  243.1 7.8 %collective-permute-start.25 = (f32[64,96]{1,0:T(8,128)S(1)}, f32[64,96]{1,0:T(8,128)S(1)}, u32[]{:S(2)}, u32[]{:S(2)}) collective-permute-start(f32[64,96]{1,0:T(8,128)S(1)} %get-tuple-element.84), channel_id=1, source_target_pairs={{4,8},{8,4},{12,16},{16,12},{20,24},{24,20},{28,32},{32,28},{36,40... | collective-permute-start | bytes 73736 | tf_op jit(solution)/shard_map/halo_sx/ppermute | solution.py:175
  251.0 5.7 %collective-permute-start.26 = (f32[64,96]{1,0:T(8,128)S(1)}, f32[64,96]{1,0:T(8,128)S(1)}, u32[]{:S(2)}, u32[]{:S(2)}) collective-permute-start(f32[64,96]{1,0:T(8,128)S(1)} %get-tuple-element.85), channel_id=1, source_target_pairs={{0,1},{1,0},{2,3},{3,2},{4,5},{5,4},{6,7},{7,6},{8,9},{9,8},{10,11... | collective-permute-start | bytes 73736 | tf_op jit(solution)/shard_map/halo_sy/ppermute | solution.py:175
  259.5 3.7 %all-to-all-start.9 = ((bf16[8,80,384]{2,1,0:T(8,128)(2,1)}), bf16[8,80,384]{2,1,0:T(8,128)(2,1)S(1)}, u32[]{:S(2)}, u32[]{:S(2)}) async-start(bf16[8,80,384]{2,1,0:T(8,128)(2,1)} %finish.14), calls=%async_computation.9 | async-start | bytes 983040 | tf_op jit(solution)/shard_map/all_to_all | solution.py:299
  263.4 11.0 %all-to-all-done.9.refs_0_ = bf16[8,80,384]{2,1,0:T(8,128)(2,1)S(1)} async-done(((bf16[8,80,384]{2,1,0:T(8,128)(2,1)}), bf16[8,80,384]{2,1,0:T(8,128)(2,1)S(1)}, u32[]{:S(2)}, u32[]{:S(2)}) %all-to-all-start.9) | async-done | bytes 491552 | tf_op jit(solution)/shard_map/all_to_all | solution.py:299
  276.7 9.5 %collective-permute-start.28 = (f32[64,96]{1,0:T(8,128)S(1)}, f32[64,96]{1,0:T(8,128)S(1)}, u32[]{:S(2)}, u32[]{:S(2)}) collective-permute-start(f32[64,96]{1,0:T(8,128)S(1)} %get-tuple-element.89), channel_id=1, source_target_pairs={{0,4},{4,8},{8,12},{12,16},{16,20},{20,24},{24,28},{28,32},{32,36}... | collective-permute-start | bytes 73736 | tf_op jit(solution)/shard_map/ppermute | solution.py:175
  286.2 4.1 %collective-permute-start.29 = (f32[64,96]{1,0:T(8,128)S(1)}, f32[64,96]{1,0:T(8,128)S(1)}, u32[]{:S(2)}, u32[]{:S(2)}) collective-permute-start(f32[64,96]{1,0:T(8,128)S(1)} %get-tuple-element.90), channel_id=1, source_target_pairs={{0,1},{1,2},{2,3},{4,5},{5,6},{6,7},{8,9},{9,10},{10,11},{12,13},{... | collective-permute-start | bytes 73736 | tf_op jit(solution)/shard_map/ppermute | solution.py:175
  292.8 6.0 %all-to-all-start.10 = ((f32[32,1,40]{2,1,0:T(1,128)}), f32[32,1,40]{2,1,0:T(1,128)S(1)}, u32[]{:S(2)}, u32[]{:S(2)}) async-start(f32[32,1,40]{2,1,0:T(1,128)} %bitcast.18), calls=%async_computation.10 | async-start | bytes 32768 | tf_op jit(solution)/shard_map/all_to_all | solution.py:299
  298.9 8.5 %all-to-all-done.10 = f32[32,1,40]{2,1,0:T(1,128)S(1)} async-done(((f32[32,1,40]{2,1,0:T(1,128)}), f32[32,1,40]{2,1,0:T(1,128)S(1)}, u32[]{:S(2)}, u32[]{:S(2)}) %all-to-all-start.10) | async-done | bytes 5152 | tf_op jit(solution)/shard_map/all_to_all | solution.py:299
  308.0 4.3 %all-to-all-start.11 = ((f32[16,1,40]{2,1,0:T(1,128)}), f32[16,1,40]{2,1,0:T(1,128)S(1)}, u32[]{:S(2)}, u32[]{:S(2)}) async-start(f32[16,1,40]{2,1,0:T(1,128)} %broadcast_in_dim.119), calls=%async_computation.11 | async-start | bytes 16384 | tf_op jit(solution)/shard_map/all_to_all | solution.py:299
  312.3 7.0 %all-to-all-done.11 = f32[16,1,40]{2,1,0:T(1,128)S(1)} async-done(((f32[16,1,40]{2,1,0:T(1,128)}), f32[16,1,40]{2,1,0:T(1,128)S(1)}, u32[]{:S(2)}, u32[]{:S(2)}) %all-to-all-start.11) | async-done | bytes 2592 | tf_op jit(solution)/shard_map/all_to_all | solution.py:299
  327.4 5.8 %all-to-all-done.12 = f32[8,1,216]{2,1,0:T(1,128)S(1)} async-done(((f32[8,1,216]{2,1,0:T(1,128)}), f32[8,1,216]{2,1,0:T(1,128)S(1)}, u32[]{:S(2)}, u32[]{:S(2)}) %all-to-all-start.12) | async-done | bytes 6944 | tf_op jit(solution)/shard_map/all_to_all | solution.py:299
  (160 shorter events, 78.9 us)
Async XLA Ops:
  3.2 25.5 %all-to-all-start = ((bf16[8,8,3200]{2,1,0:T(8,128)(2,1)}), bf16[8,8,3200]{2,1,0:T(8,128)(2,1)S(1)}, u32[]{:S(2)}, u32[]{:S(2)}) async-start(bf16[8,8,3200]{2,1,0:T(8,128)(2,1)} %packet.1), calls=%async_computation | async-start | bytes 819200 | tf_op jit(solution)/shard_map/all_to_all | solution.py:299
  31.5 10.1 %collective-permute-start = (f32[64,96]{1,0:T(8,128)S(1)}, f32[64,96]{1,0:T(8,128)S(1)}, u32[]{:S(2)}, u32[]{:S(2)}) collective-permute-start(f32[64,96]{1,0:T(8,128)S(1)} %get-tuple-element.48), channel_id=1, source_target_pairs={{0,4},{4,0},{8,12},{12,8},{16,20},{20,16},{24,28},{28,24},{32,36},... | collective-permute-start | bytes 73736 | tf_op jit(solution)/shard_map/halo_sx/ppermute | solution.py:175
  34.7 6.9 %collective-permute-start.1 = (f32[64,96]{1,0:T(8,128)S(1)}, f32[64,96]{1,0:T(8,128)S(1)}, u32[]{:S(2)}, u32[]{:S(2)}) collective-permute-start(f32[64,96]{1,0:T(8,128)S(1)} %get-tuple-element.49), channel_id=1, source_target_pairs={{4,8},{8,4},{12,16},{16,12},{20,24},{24,20},{28,32},{32,28},{36,40... | collective-permute-start | bytes 73736 | tf_op jit(solution)/shard_map/halo_sx/ppermute | solution.py:175
  37.8 4.7 %collective-permute-start.2 = (f32[64,96]{1,0:T(8,128)S(1)}, f32[64,96]{1,0:T(8,128)S(1)}, u32[]{:S(2)}, u32[]{:S(2)}) collective-permute-start(f32[64,96]{1,0:T(8,128)S(1)} %get-tuple-element.50), channel_id=1, source_target_pairs={{0,1},{1,0},{2,3},{3,2},{4,5},{5,4},{6,7},{7,6},{8,9},{9,8},{10,11... | collective-permute-start | bytes 73736 | tf_op jit(solution)/shard_map/halo_sy/ppermute | solution.py:175
  43.4 17.6 %all-to-all-start.1 = ((bf16[8,64,384]{2,1,0:T(8,128)(2,1)}), bf16[8,64,384]{2,1,0:T(8,128)(2,1)S(1)}, u32[]{:S(2)}, u32[]{:S(2)}) async-start(bf16[8,64,384]{2,1,0:T(8,128)(2,1)} %get-tuple-element.52), calls=%async_computation.1 | async-start | bytes 786432 | tf_op jit(solution)/shard_map/all_to_all | solution.py:299
  63.1 13.4 %collective-permute-start.4 = (f32[64,96]{1,0:T(8,128)S(1)}, f32[64,96]{1,0:T(8,128)S(1)}, u32[]{:S(2)}, u32[]{:S(2)}) collective-permute-start(f32[64,96]{1,0:T(8,128)S(1)} %get-tuple-element.54), channel_id=1, source_target_pairs={{0,4},{4,0},{8,12},{12,8},{16,20},{20,16},{24,28},{28,24},{32,36},... | collective-permute-start | bytes 73736 | tf_op jit(solution)/shard_map/halo_sx/ppermute | solution.py:175
  65.5 11.1 %collective-permute-start.5 = (f32[64,96]{1,0:T(8,128)S(1)}, f32[64,96]{1,0:T(8,128)S(1)}, u32[]{:S(2)}, u32[]{:S(2)}) collective-permute-start(f32[64,96]{1,0:T(8,128)S(1)} %get-tuple-element.55), channel_id=1, source_target_pairs={{4,8},{8,4},{12,16},{16,12},{20,24},{24,20},{28,32},{32,28},{36,40... | collective-permute-start | bytes 73736 | tf_op jit(solution)/shard_map/halo_sx/ppermute | solution.py:175
  69.9 7.0 %collective-permute-start.6 = (f32[64,96]{1,0:T(8,128)S(1)}, f32[64,96]{1,0:T(8,128)S(1)}, u32[]{:S(2)}, u32[]{:S(2)}) collective-permute-start(f32[64,96]{1,0:T(8,128)S(1)} %get-tuple-element.56), channel_id=1, source_target_pairs={{0,1},{1,0},{2,3},{3,2},{4,5},{5,4},{6,7},{7,6},{8,9},{9,8},{10,11... | collective-permute-start | bytes 73736 | tf_op jit(solution)/shard_map/halo_sy/ppermute | solution.py:175
  105.3 20.5 %all-to-all-start.4 = ((f32[16,1,64]{2,1,0:T(1,128)}), f32[16,1,64]{2,1,0:T(1,128)S(1)}, u32[]{:S(2)}, u32[]{:S(2)}) async-start(f32[16,1,64]{2,1,0:T(1,128)} %broadcast_in_dim.114), calls=%async_computation.4 | async-start | bytes 16384 | tf_op jit(solution)/shard_map/all_to_all | solution.py:299
  117.2 9.0 %collective-permute-start.10 = (f32[64,96]{1,0:T(8,128)}, f32[64,96]{1,0:T(8,128)S(1)}, u32[]{:S(2)}, u32[]{:S(2)}) collective-permute-start(f32[64,96]{1,0:T(8,128)} %get-tuple-element.62), channel_id=1, source_target_pairs={{0,1},{1,0},{2,3},{3,2},{4,5},{5,4},{6,7},{7,6},{8,9},{9,8},{10,11... | collective-permute-start | bytes 73736 | tf_op jit(solution)/shard_map/halo_sy/ppermute | solution.py:175
  119.4 6.8 %collective-permute-start.11 = (f32[64,96]{1,0:T(8,128)}, f32[64,96]{1,0:T(8,128)S(1)}, u32[]{:S(2)}, u32[]{:S(2)}) collective-permute-start(f32[64,96]{1,0:T(8,128)} %get-tuple-element.63), channel_id=1, source_target_pairs={{1,2},{2,1},{5,6},{6,5},{9,10},{10,9},{13,14},{14,13},{17,18},{18,... | collective-permute-start | bytes 73736 | tf_op jit(solution)/shard_map/halo_sy/ppermute | solution.py:175
  120.1 6.1 %collective-permute-start.8 = (f32[64,96]{1,0:T(8,128)}, f32[64,96]{1,0:T(8,128)S(1)}, u32[]{:S(2)}, u32[]{:S(2)}) collective-permute-start(f32[64,96]{1,0:T(8,128)} %get-tuple-element.60), channel_id=1, source_target_pairs={{0,4},{4,0},{8,12},{12,8},{16,20},{20,16},{24,28},{28,24},{32,36},... | collective-permute-start | bytes 73736 | tf_op jit(solution)/shard_map/halo_sx/ppermute | solution.py:175
  122.4 5.4 %collective-permute-start.9 = (f32[64,96]{1,0:T(8,128)}, f32[64,96]{1,0:T(8,128)S(1)}, u32[]{:S(2)}, u32[]{:S(2)}) collective-permute-start(f32[64,96]{1,0:T(8,128)} %get-tuple-element.61), channel_id=1, source_target_pairs={{4,8},{8,4},{12,16},{16,12},{20,24},{24,20},{28,32},{32,28},{36,40... | collective-permute-start | bytes 73736 | tf_op jit(solution)/shard_map/halo_sx/ppermute | solution.py:175
  145.4 15.3 %collective-permute-start.12 = (f32[64,96]{1,0:T(8,128)S(1)}, f32[64,96]{1,0:T(8,128)S(1)}, u32[]{:S(2)}, u32[]{:S(2)}) collective-permute-start(f32[64,96]{1,0:T(8,128)S(1)} %get-tuple-element.66), channel_id=1, source_target_pairs={{0,4},{4,0},{8,12},{12,8},{16,20},{20,16},{24,28},{28,24},{32,36},... | collective-permute-start | bytes 73736 | tf_op jit(solution)/shard_map/halo_sx/ppermute | solution.py:175
  147.3 13.4 %collective-permute-start.13 = (f32[64,96]{1,0:T(8,128)S(1)}, f32[64,96]{1,0:T(8,128)S(1)}, u32[]{:S(2)}, u32[]{:S(2)}) collective-permute-start(f32[64,96]{1,0:T(8,128)S(1)} %get-tuple-element.67), channel_id=1, source_target_pairs={{4,8},{8,4},{12,16},{16,12},{20,24},{24,20},{28,32},{32,28},{36,40... | collective-permute-start | bytes 73736 | tf_op jit(solution)/shard_map/halo_sx/ppermute | solution.py:175
  155.1 6.2 %collective-permute-start.14 = (f32[64,96]{1,0:T(8,128)S(1)}, f32[64,96]{1,0:T(8,128)S(1)}, u32[]{:S(2)}, u32[]{:S(2)}) collective-permute-start(f32[64,96]{1,0:T(8,128)S(1)} %get-tuple-element.68), channel_id=1, source_target_pairs={{0,1},{1,0},{2,3},{3,2},{4,5},{5,4},{6,7},{7,6},{8,9},{9,8},{10,11... | collective-permute-start | bytes 73736 | tf_op jit(solution)/shard_map/halo_sy/ppermute | solution.py:175
  176.7 15.8 %collective-permute-start.16 = (f32[64,96]{1,0:T(8,128)S(1)}, f32[64,96]{1,0:T(8,128)S(1)}, u32[]{:S(2)}, u32[]{:S(2)}) collective-permute-start(f32[64,96]{1,0:T(8,128)S(1)} %get-tuple-element.71), channel_id=1, source_target_pairs={{0,4},{4,0},{8,12},{12,8},{16,20},{20,16},{24,28},{28,24},{32,36},... | collective-permute-start | bytes 73736 | tf_op jit(solution)/shard_map/halo_sx/ppermute | solution.py:175
  178.6 13.9 %collective-permute-start.17 = (f32[64,96]{1,0:T(8,128)S(1)}, f32[64,96]{1,0:T(8,128)S(1)}, u32[]{:S(2)}, u32[]{:S(2)}) collective-permute-start(f32[64,96]{1,0:T(8,128)S(1)} %get-tuple-element.72), channel_id=1, source_target_pairs={{4,8},{8,4},{12,16},{16,12},{20,24},{24,20},{28,32},{32,28},{36,40... | collective-permute-start | bytes 73736 | tf_op jit(solution)/shard_map/halo_sx/ppermute | solution.py:175
  186.6 6.8 %collective-permute-start.18 = (f32[64,96]{1,0:T(8,128)S(1)}, f32[64,96]{1,0:T(8,128)S(1)}, u32[]{:S(2)}, u32[]{:S(2)}) collective-permute-start(f32[64,96]{1,0:T(8,128)S(1)} %get-tuple-element.73), channel_id=1, source_target_pairs={{0,1},{1,0},{2,3},{3,2},{4,5},{5,4},{6,7},{7,6},{8,9},{9,8},{10,11... | collective-permute-start | bytes 73736 | tf_op jit(solution)/shard_map/halo_sy/ppermute | solution.py:175
  191.9 1.6 collective-permute-start.19
  209.0 15.9 %collective-permute-start.20 = (f32[64,96]{1,0:T(8,128)S(1)}, f32[64,96]{1,0:T(8,128)S(1)}, u32[]{:S(2)}, u32[]{:S(2)}) collective-permute-start(f32[64,96]{1,0:T(8,128)S(1)} %get-tuple-element.78), channel_id=1, source_target_pairs={{0,4},{4,0},{8,12},{12,8},{16,20},{20,16},{24,28},{28,24},{32,36},... | collective-permute-start | bytes 73736 | tf_op jit(solution)/shard_map/halo_sx/ppermute | solution.py:175
  210.9 14.0 %collective-permute-start.21 = (f32[64,96]{1,0:T(8,128)S(1)}, f32[64,96]{1,0:T(8,128)S(1)}, u32[]{:S(2)}, u32[]{:S(2)}) collective-permute-start(f32[64,96]{1,0:T(8,128)S(1)} %get-tuple-element.79), channel_id=1, source_target_pairs={{4,8},{8,4},{12,16},{16,12},{20,24},{24,20},{28,32},{32,28},{36,40... | collective-permute-start | bytes 73736 | tf_op jit(solution)/shard_map/halo_sx/ppermute | solution.py:175
  218.9 6.9 %collective-permute-start.22 = (f32[64,96]{1,0:T(8,128)S(1)}, f32[64,96]{1,0:T(8,128)S(1)}, u32[]{:S(2)}, u32[]{:S(2)}) collective-permute-start(f32[64,96]{1,0:T(8,128)S(1)} %get-tuple-element.80), channel_id=1, source_target_pairs={{0,1},{1,0},{2,3},{3,2},{4,5},{5,4},{6,7},{7,6},{8,9},{9,8},{10,11... | collective-permute-start | bytes 73736 | tf_op jit(solution)/shard_map/halo_sy/ppermute | solution.py:175
  241.2 16.2 %collective-permute-start.24 = (f32[64,96]{1,0:T(8,128)S(1)}, f32[64,96]{1,0:T(8,128)S(1)}, u32[]{:S(2)}, u32[]{:S(2)}) collective-permute-start(f32[64,96]{1,0:T(8,128)S(1)} %get-tuple-element.83), channel_id=1, source_target_pairs={{0,4},{4,0},{8,12},{12,8},{16,20},{20,16},{24,28},{28,24},{32,36},... | collective-permute-start | bytes 73736 | tf_op jit(solution)/shard_map/halo_sx/ppermute | solution.py:175
  243.1 14.3 %collective-permute-start.25 = (f32[64,96]{1,0:T(8,128)S(1)}, f32[64,96]{1,0:T(8,128)S(1)}, u32[]{:S(2)}, u32[]{:S(2)}) collective-permute-start(f32[64,96]{1,0:T(8,128)S(1)} %get-tuple-element.84), channel_id=1, source_target_pairs={{4,8},{8,4},{12,16},{16,12},{20,24},{24,20},{28,32},{32,28},{36,40... | collective-permute-start | bytes 73736 | tf_op jit(solution)/shard_map/halo_sx/ppermute | solution.py:175
  251.0 7.0 %collective-permute-start.26 = (f32[64,96]{1,0:T(8,128)S(1)}, f32[64,96]{1,0:T(8,128)S(1)}, u32[]{:S(2)}, u32[]{:S(2)}) collective-permute-start(f32[64,96]{1,0:T(8,128)S(1)} %get-tuple-element.85), channel_id=1, source_target_pairs={{0,1},{1,0},{2,3},{3,2},{4,5},{5,4},{6,7},{7,6},{8,9},{9,8},{10,11... | collective-permute-start | bytes 73736 | tf_op jit(solution)/shard_map/halo_sy/ppermute | solution.py:175
  259.5 14.8 %all-to-all-start.9 = ((bf16[8,80,384]{2,1,0:T(8,128)(2,1)}), bf16[8,80,384]{2,1,0:T(8,128)(2,1)S(1)}, u32[]{:S(2)}, u32[]{:S(2)}) async-start(bf16[8,80,384]{2,1,0:T(8,128)(2,1)} %finish.14), calls=%async_computation.9 | async-start | bytes 983040 | tf_op jit(solution)/shard_map/all_to_all | solution.py:299
  276.7 13.6 %collective-permute-start.28 = (f32[64,96]{1,0:T(8,128)S(1)}, f32[64,96]{1,0:T(8,128)S(1)}, u32[]{:S(2)}, u32[]{:S(2)}) collective-permute-start(f32[64,96]{1,0:T(8,128)S(1)} %get-tuple-element.89), channel_id=1, source_target_pairs={{0,4},{4,8},{8,12},{12,16},{16,20},{20,24},{24,28},{28,32},{32,36}... | collective-permute-start | bytes 73736 | tf_op jit(solution)/shard_map/ppermute | solution.py:175
  286.2 5.1 %collective-permute-start.29 = (f32[64,96]{1,0:T(8,128)S(1)}, f32[64,96]{1,0:T(8,128)S(1)}, u32[]{:S(2)}, u32[]{:S(2)}) collective-permute-start(f32[64,96]{1,0:T(8,128)S(1)} %get-tuple-element.90), channel_id=1, source_target_pairs={{0,1},{1,2},{2,3},{4,5},{5,6},{6,7},{8,9},{9,10},{10,11},{12,13},{... | collective-permute-start | bytes 73736 | tf_op jit(solution)/shard_map/ppermute | solution.py:175
  292.8 14.6 %all-to-all-start.10 = ((f32[32,1,40]{2,1,0:T(1,128)}), f32[32,1,40]{2,1,0:T(1,128)S(1)}, u32[]{:S(2)}, u32[]{:S(2)}) async-start(f32[32,1,40]{2,1,0:T(1,128)} %bitcast.18), calls=%async_computation.10 | async-start | bytes 32768 | tf_op jit(solution)/shard_map/all_to_all | solution.py:299
  308.0 11.2 %all-to-all-start.11 = ((f32[16,1,40]{2,1,0:T(1,128)}), f32[16,1,40]{2,1,0:T(1,128)S(1)}, u32[]{:S(2)}, u32[]{:S(2)}) async-start(f32[16,1,40]{2,1,0:T(1,128)} %broadcast_in_dim.119), calls=%async_computation.11 | async-start | bytes 16384 | tf_op jit(solution)/shard_map/all_to_all | solution.py:299
  323.4 9.8 %all-to-all-start.12 = ((f32[8,1,216]{2,1,0:T(1,128)}), f32[8,1,216]{2,1,0:T(1,128)S(1)}, u32[]{:S(2)}, u32[]{:S(2)}) async-start(f32[8,1,216]{2,1,0:T(1,128)} %all_to_all.63), calls=%async_computation.12 | async-start | bytes 16384 | tf_op jit(solution)/shard_map/all_to_all | solution.py:299
  (15 other events, 104.2 us)
